TPU v7x, 512 devices: a whole 4x8x8 slice. The times are simulated.
512 devices in a mesh: wall: 64 (over z, y), xs: 8 (over x, core).
Axes of the slice: x: 4, y: 8, z: 8, core: 2. Of those that a mesh axis runs over, the one named last changes fastest.
Arguments:
- krylov_basis: float32 [3, 4, 128, 64, 1024], P(None, None, 'wall', None, 'xs'), may hold values from -7 to 7
- base_state: float32 [4, 128, 64, 1024], P(None, 'wall', None, 'xs'), may hold values from -6 to 6
- diffusivity: float32 [4], replicated, may hold values from 150 to 1500
Outputs:
- new_vector: float32 [4, 128, 64, 1024], P(None, 'wall', None, 'xs')
- hessenberg: float32 [4], replicated
All inputs are finite; a program needn't handle non-finite values.
Results may differ from a plain program's by a relative error of at most 0.0003.
Values sent between devices are 32-bit elements; how exact they have to be, the bound alone decides.
No kernel may reach another device: no remote copies, remote signals or barrier semaphores. Data moves between devices by JAX's collectives and lax.ppermute only.
A program may use at most 64 MiB of HBM per device.

v0:
```python
import functools
import math

import jax
import jax.numpy as jnp
from jax import lax
from jax.sharding import Mesh
from jax.sharding import PartitionSpec as P

WALL_XS = ("wall_0", "wall_1", "xs_0", "xs_1")
WALL = ("wall_0", "wall_1")
XS = ("xs_0", "xs_1")


adv_step = 0.2
buoyancy = 0.5
screening = 0.004
epsilon = 1e-06


def padded_2(x, sides, width):
    edges = {}
    for axis, dim in sides:
        size, length = (lax.axis_size(axis), x.shape[dim])
        up = [(i, (i + 1) % size) for i in range(size)]
        last = lax.slice_in_dim(x, length - width, length, axis=dim)
        leading = lax.slice_in_dim(x, 0, width, axis=dim)
        edges[dim] = (
            lax.ppermute(last, axis, up),
            lax.ppermute(leading, axis, [(b, a) for a, b in up]),
        )
    done = []
    for _, dim in sides:
        low, high = edges[dim]
        around = [(width, width) if d in done else (0, 0) for d in range(x.ndim)]
        x = jnp.concatenate([jnp.pad(low, around), x, jnp.pad(high, around)], axis=dim)
        done.append(dim)
    return x


def split_up(x, dim, length):
    before, after = (x.shape[:dim], x.shape[dim + 1 :])
    return jnp.moveaxis(x.reshape(*before, length, -1, *after), dim, 0)


def sum_at_owner(x, axis, dim):
    pieces = split_up(x, dim, lax.axis_size(axis))
    arrived = lax.all_to_all(pieces, axis, split_axis=0, concat_axis=0, tiled=True)
    return arrived.sum(axis=0)


def joined_along(pieces, dim):
    pieces = jnp.moveaxis(pieces, 0, dim)
    lengths = pieces.shape
    return pieces.reshape(*lengths[:dim], lengths[dim] * lengths[dim + 1], *lengths[dim + 2 :])


def from_everyone(x, axis):
    length = lax.axis_size(axis)
    return lax.all_to_all(jnp.broadcast_to(x[None], (length, *x.shape)), axis, 0, 0, tiled=True)


def gather_directly(x, axis, dim):
    return joined_along(from_everyone(x, axis), dim)


def over_axes(x, axes):
    return functools.reduce(lax.psum, axes, x)


def fourier_table(length, cell_ids, mode_ids):
    wavenumbers = (mode_ids + 1) // 2
    phases = cell_ids[:, None] * wavenumbers[None, :] % length
    angles = phases.astype(jnp.float32) * (2.0 * math.pi / length)
    scaled = math.sqrt(2.0 / length)
    odd_mode = (mode_ids % 2 == 1)[None, :]
    values = jnp.where(odd_mode, scaled * jnp.cos(angles), scaled * jnp.sin(angles))
    values = jnp.where((mode_ids == 0)[None, :], 1.0 / math.sqrt(length), values)
    values = jnp.where(
        (mode_ids == length - 1)[None, :], jnp.cos(angles) / math.sqrt(length), values
    )
    return values


def mode_eigen(length, mode_ids):
    wavenumbers = ((mode_ids + 1) // 2).astype(jnp.float32)
    return 4.0 * jnp.sin(wavenumbers * (math.pi / length)) ** 2


def centered(values_in):
    padded = padded_2(values_in, ((WALL, 1), (XS, 3)), 1)
    wall_pos = lax.axis_index(WALL)
    wall_count = lax.axis_size(WALL)
    below_rim = padded[:, :1] * (wall_pos > 0).astype(jnp.float32)
    above_rim = padded[:, -1:] * (wall_pos < wall_count - 1).astype(jnp.float32)
    padded = jnp.concatenate([below_rim, padded[:, 1:-1], above_rim], 1)
    along_x = (padded[:, 1:-1, :, 2:] - padded[:, 1:-1, :, :-2]) * 0.5
    along_y = (padded[:, 2:, :, 1:-1] - padded[:, :-2, :, 1:-1]) * 0.5
    along_z = (jnp.roll(values_in, -1, 2) - jnp.roll(values_in, 1, 2)) * 0.5
    return (along_x, along_y, along_z)


def compose(earlier_map, later_map):
    return (earlier_map[0] * later_map[0], later_map[0] * earlier_map[1] + later_map[1])


def row_coefficients(shifts, global_row):
    root_term = jnp.sqrt(shifts * (shifts + 4.0))
    decay_rate = 2.0 / (2.0 + shifts + root_term)
    log_decay = jnp.log(decay_rate)
    numerator = 1.0 - jnp.exp((2.0 * global_row + 2.0) * log_decay)
    denominator = 1.0 - jnp.exp((2.0 * global_row + 4.0) * log_decay)
    return -decay_rate * numerator / denominator


def column_solve(right_side, shifts, row_axis):
    moved = jnp.moveaxis(right_side, row_axis, 0)
    moved_shape = moved.shape
    flat_rows = moved.reshape(moved_shape[0], -1)
    column_count = flat_rows.shape[1]
    wall_count = lax.axis_size(WALL)
    local_columns = column_count // wall_count
    shift_columns = jnp.broadcast_to(shifts, moved_shape[1:]).reshape(-1)
    shift_columns = lax.dynamic_slice_in_dim(
        shift_columns, lax.axis_index(WALL) * local_columns, local_columns, 0
    )
    columns = lax.all_to_all(flat_rows, WALL, split_axis=1, concat_axis=0, tiled=True)
    total_rows = columns.shape[0]
    global_row = jnp.arange(total_rows, dtype=jnp.int32).astype(jnp.float32)[:, None]
    coefficients = row_coefficients(shift_columns[None, :], global_row)
    _, reduced = lax.associative_scan(compose, (-coefficients, coefficients * columns), axis=0)
    _, solved = lax.associative_scan(compose, (-coefficients, reduced), reverse=True, axis=0)
    back = lax.all_to_all(solved, WALL, split_axis=0, concat_axis=1, tiled=True)
    return jnp.moveaxis(back.reshape(moved_shape), 0, row_axis)


def wall_solve(right_side, shifts, row_axis):
    return column_solve(right_side, shifts, row_axis)


def solve_pressure(flow_divergence):
    highest_mode = lax.Precision.HIGHEST
    wall_rows, spanwise_cells, local_cells = flow_divergence.shape
    stream_cells = local_cells * lax.axis_size(XS)
    span_ids = jnp.arange(spanwise_cells, dtype=jnp.int32)
    spanwise_table = fourier_table(spanwise_cells, span_ids, span_ids)
    spectral_field = jnp.einsum(
        "orp,rb->obp", flow_divergence, spanwise_table, precision=highest_mode
    )
    cells_local = lax.axis_index(XS) * local_cells + jnp.arange(local_cells, dtype=jnp.int32)
    flattened = spectral_field.reshape(-1, local_cells)
    wavenumber_table = fourier_table(
        stream_cells, cells_local, jnp.arange(local_cells * lax.axis_size(XS), dtype=jnp.int32)
    )
    spectra = sum_at_owner(
        lax.dot_general(
            wavenumber_table, flattened, (((0,), (1,)), ((), ())), precision=highest_mode
        ),
        XS,
        0,
    )
    spectra = spectra.reshape(local_cells, wall_rows, spanwise_cells)
    mode_first = lax.axis_index(XS) * local_cells
    shifts = mode_eigen(stream_cells, mode_first + jnp.arange(local_cells, dtype=jnp.int32))[
        :, None
    ]
    shifts = shifts + mode_eigen(spanwise_cells, span_ids)[None, :] + screening
    solved = wall_solve(spectra, shifts, 1)
    block_data = gather_directly(solved, XS, 0)
    count_modes = block_data.shape[0]
    wavenumber_table = fourier_table(
        stream_cells, cells_local, jnp.arange(count_modes, dtype=jnp.int32)
    )
    line_entries = lax.dot_general(
        block_data.reshape(count_modes, -1),
        wavenumber_table,
        (((0,), (1,)), ((), ())),
        precision=highest_mode,
    )
    return jnp.einsum(
        "pqa,wq->pwa",
        line_entries.reshape(wall_rows, spanwise_cells, local_cells),
        spanwise_table,
        precision=highest_mode,
    )


def time_step(current, base_state, base_grads, shifts):
    gradient_fields = centered(current)
    advect = jnp.zeros_like(current)
    for direction in range(3):
        advect = advect + base_state[direction : direction + 1] * gradient_fields[direction]
        advect = advect + current[direction : direction + 1] * base_grads[direction]
    updated = current - adv_step * advect
    updated = updated.at[1].add(buoyancy * current[3])
    velocity = updated[:3]
    vel_x, vel_y, vel_z = centered(velocity)
    flow_divergence = vel_x[0] + vel_y[1] + vel_z[2]
    pressure_field = solve_pressure(flow_divergence)
    press_x, press_y, press_z = centered(pressure_field[None])
    corrected = velocity - jnp.concatenate([press_x, press_y, press_z], 0)
    updated = jnp.concatenate([corrected, updated[3:]], 0)
    return wall_solve(-shifts[:, None] * updated, shifts, 1)


def shards(krylov_basis, base_state, diffusivity):
    highest_mode = lax.Precision.HIGHEST
    shifts = (1.0 / diffusivity)[:, None, None]
    base_grads = centered(base_state)
    vectors = krylov_basis.shape[0]
    current = krylov_basis[vectors - 1]
    current = time_step(current, base_state, base_grads, shifts)
    entries = float(current.size * lax.axis_size(WALL) * lax.axis_size(XS))
    local_products = jnp.einsum("kfyzx,fyzx->k", krylov_basis, current, precision=highest_mode)
    local_gram = jnp.einsum("kfyzx,lfyzx->kl", krylov_basis, krylov_basis, precision=highest_mode)
    totals = (
        over_axes(local_products, WALL_XS),
        over_axes(jnp.sum(current * current), WALL_XS),
        over_axes(local_gram, WALL_XS),
    )
    products = totals[0] / entries
    gram_matrix = totals[2] / entries
    mean_square = (
        totals[1] / entries
        - 2.0 * jnp.sum(products * products)
        + jnp.dot(
            products, jnp.dot(gram_matrix, products, precision=highest_mode), precision=highest_mode
        )
    )
    residual = current - jnp.einsum("k,kfyzx->fyzx", products, krylov_basis, precision=highest_mode)
    norm_value = jnp.sqrt(mean_square + epsilon)
    return (residual / norm_value, jnp.concatenate([products, norm_value[None]]))


def solution(mesh):
    torus = Mesh(mesh.devices.reshape(8, 8, 4, 2), ("wall_0", "wall_1", "xs_0", "xs_1"))
    return jax.shard_map(
        shards,
        mesh=torus,
        in_specs=(P(None, None, WALL, None, XS), P(None, WALL, None, XS), P()),
        out_specs=(P(None, WALL, None, XS), P()),
        check_vma=False,
    )
```

profile of v0, /device:TPU:1, one launch (start us, length us, event | category | flops | bytes accessed | tf_op | source)
XLA Modules:
  0.0 260.0 jit_solution(10476128225346505958)
XLA Ops:
  0.6 1.0 slice_bitcast_fusion
  1.6 0.8 fusion.213
  2.4 6.8 %collective-permute-start.2 = (f32[4,2,64,1]{3,2,1,0:T(8,128)}, f32[4,2,64,1]{3,2,1,0:T(8,128)}, u32[]{:S(2)}, u32[]{:S(2)}) collective-permute-start(f32[4,2,64,1]{3,2,1,0:T(8,128)} %get-tuple-element.69), channel_id=1, source_target_pairs={{1,0},{2,1},{3,2},{4,3},{5,4},{6,5},{7,6},{0,7},{9,8},{10,9},{11,1... | collective-permute-start | bytes 6152 | tf_op jit(solution)/shard_map/ppermute | solution.py:30
  9.2 0.7 fusion.214
  10.0 1.9 collective-permute-start
  11.9 9.3 %collective-permute-start.1 = (f32[4,1,64,128]{3,2,1,0:T(8,128)}, f32[4,1,64,128]{3,2,1,0:T(8,128)S(1)}, u32[]{:S(2)}, u32[]{:S(2)}) collective-permute-start(f32[4,1,64,128]{3,2,1,0:T(8,128)} %get-tuple-element.71), channel_id=1, source_target_pairs={{8,0},{16,8},{24,16},{32,24},{40,32},{48,40},{56,48},{64,56},{72,6... | collective-permute-start | bytes 393224 | tf_op jit(solution)/shard_map/ppermute | solution.py:30
  21.2 0.9 fusion.215
  22.1 1.4 collective-permute-start.6
  23.5 0.7 fusion.216
  24.3 1.0 copy-done.1
  25.4 0.5 fusion.167
  26.4 0.5 fusion.137
  26.9 0.6 add_select_fusion.6
  27.5 0.5 fusion.146
  29.0 0.6 iota_add_fusion.1
  29.5 1.0 pad.201
  30.6 2.1 collective-permute-start.4
  32.7 6.7 %collective-permute-start.5 = (f32[4,1,64,128]{3,2,1,0:T(8,128)S(1)}, f32[4,1,64,128]{3,2,1,0:T(8,128)S(1)}, u32[]{:S(2)}, u32[]{:S(2)}) collective-permute-start(f32[4,1,64,128]{3,2,1,0:T(8,128)S(1)} %copy-done.4), channel_id=1, source_target_pairs={{8,0},{16,8},{24,16},{32,24},{40,32},{48,40},{56,48},{64,56},{72,6... | collective-permute-start | bytes 393224 | tf_op jit(solution)/shard_map/ppermute | solution.py:30
  39.4 1.0 pad.203
  40.4 1.0 pad.204
  42.0 0.9 copy-done.2
  43.4 1.0 copy-done.3
  45.0 0.7 slice-done
  45.9 0.8 fusion.45
  46.9 2.9 %collective-permute-start.10 = (f32[3,2,64,1]{3,2,1,0:T(8,128)S(1)}, f32[3,2,64,1]{3,2,1,0:T(8,128)S(1)}, u32[]{:S(2)}, u32[]{:S(2)}) collective-permute-start(f32[3,2,64,1]{3,2,1,0:T(8,128)S(1)} %get-tuple-element.52), channel_id=1, source_target_pairs={{1,0},{2,1},{3,2},{4,3},{5,4},{6,5},{7,6},{0,7},{9,8},{10,9},{11,1... | collective-permute-start | bytes 4616 | tf_op jit(solution)/shard_map/ppermute | solution.py:30
  49.7 1.9 collective-permute-start.8
  51.7 6.7 %collective-permute-start.9 = (f32[3,1,64,128]{3,2,1,0:T(8,128)S(1)}, f32[3,1,64,128]{3,2,1,0:T(8,128)S(1)}, u32[]{:S(2)}, u32[]{:S(2)}) collective-permute-start(f32[3,1,64,128]{3,2,1,0:T(8,128)S(1)} %get-tuple-element.50), channel_id=1, source_target_pairs={{8,0},{16,8},{24,16},{32,24},{40,32},{48,40},{56,48},{64,56},{72,6... | collective-permute-start | bytes 294920 | tf_op jit(solution)/shard_map/ppermute | solution.py:30
  58.5 1.5 collective-permute-done.9
  61.9 0.5 copy-done.6
  62.4 4.3 %fusion.23 = f32[8,128,128]{2,1,0:T(8,128)} fusion(f32[128,128,1]{1,0,2:T(8,128)S(1)} %bitcast.111, s32[8,128]{1,0:T(8,128)S(1)} %copy-done.6, s32[128]{0:T(128)S(1)} %copy-done.15, pred[8,128]{1,0:T(8,128)(4,1)S(1)} %copy-done.7, pred[8,128]{1,0:T(8,128)(4,1)S(1)} %copy-done.8, pred[8,128]{1,0:T(8,128)(4,1)S(1)} %copy-done.14), kind=kOutput, calls=%fused_computation.40 | convolution fusion | flops 203948032 | bytes 597504 | tf_op jit(solution)/shard_map/dot_general | solution.py:156
  66.7 6.9 %all-to-all-start = ((f32[8,128,128]{2,1,0:T(8,128)}), f32[8,128,128]{2,1,0:T(8,128)S(1)}, u32[]{:S(2)}, u32[]{:S(2)}) async-start(f32[8,128,128]{2,1,0:T(8,128)} %fusion.23), calls=%async_computation | async-start | bytes 1048576 | tf_op jit(solution)/shard_map/all_to_all | solution.py:48
  73.9 9.1 %all-to-all-done = f32[8,128,128]{2,1,0:T(8,128)S(1)} async-done(((f32[8,128,128]{2,1,0:T(8,128)}), f32[8,128,128]{2,1,0:T(8,128)S(1)}, u32[]{:S(2)}, u32[]{:S(2)}) %all-to-all-start) | async-done | bytes 524320 | tf_op jit(solution)/shard_map/all_to_all | solution.py:48
  83.3 0.7 copy.26
  84.0 7.7 %all-to-all-start.1 = ((f32[2,64,128]{2,0,1:T(2,128)}), f32[2,64,128]{2,0,1:T(2,128)S(1)}, u32[]{:S(2)}, u32[]{:S(2)}) async-start(f32[2,64,128]{2,0,1:T(2,128)} %copy.26), calls=%async_computation.1 | async-start | bytes 131072 | tf_op jit(solution)/shard_map/all_to_all | solution.py:127
  91.9 11.0 %all-to-all-done.1 = f32[2,64,128]{2,0,1:T(2,128)S(1)} async-done(((f32[2,64,128]{2,0,1:T(2,128)}), f32[2,64,128]{2,0,1:T(2,128)S(1)}, u32[]{:S(2)}, u32[]{:S(2)}) %all-to-all-start.1) | async-done | bytes 65568 | tf_op jit(solution)/shard_map/all_to_all | solution.py:127
  105.3 14.9 %all_to_all.80 = f32[64,2,128]{2,1,0:T(2,128)S(1)} all-to-all(f32[64,2,128]{2,1,0:T(2,128)S(1)} %bitcast.108), channel_id=1, replica_groups=mesh['wall_0'=8,'wall_1'=8,'xs_0'=4,'xs_1'=2] {'wall_0','wall_1'}, dimensions={0} | all-to-all | bytes 131072 | tf_op jit(solution)/shard_map/all_to_all | solution.py:133
  120.4 0.8 broadcast_in_dim.114
  121.2 6.9 %all-to-all-start.3 = ((f32[8,128,2,64]{1,3,2,0:T(8,128)}), f32[8,128,2,64]{1,3,2,0:T(8,128)S(1)}, u32[]{:S(2)}, u32[]{:S(2)}) async-start(f32[8,128,2,64]{1,3,2,0:T(8,128)} %broadcast_in_dim.114), calls=%async_computation.3 | async-start | bytes 1048576 | tf_op jit(solution)/shard_map/all_to_all | solution.py:60
  128.2 0.6 copy-done.13
  128.9 8.7 %all-to-all-done.3 = f32[8,128,2,64]{1,3,2,0:T(8,128)S(1)} async-done(((f32[8,128,2,64]{1,3,2,0:T(8,128)}), f32[8,128,2,64]{1,3,2,0:T(8,128)S(1)}, u32[]{:S(2)}, u32[]{:S(2)}) %all-to-all-start.3) | async-done | bytes 524320 | tf_op jit(solution)/shard_map/all_to_all | solution.py:60
  138.0 2.8 %fusion.12 = f32[2,64,128]{2,1,0:T(8,128)S(1)} fusion(f32[2,64,1024]{2,1,0:T(8,128)S(1)} %bitcast.105, s32[1024]{0:T(1024)S(1)} %add_select_fusion.4, s32[128]{0:T(128)S(1)} %copy-done.15, pred[1024]{0:T(1024)(128)(4,1)S(1)} %get-tuple-element.160, pred[1024]{0:T(1024)(128)(4,1)S(1)} %get-tuple-element.161, pred[1024]{0:T(1024)(128)(4,1)S(1)} %iota_compare_fusion.1), kind=kOutput, calls=%fused_computation.30 | convolution fusion | flops 203948032 | bytes 597504 | tf_op jit(solution)/shard_map/dot_general | solution.py:174
  141.3 1.0 collective-permute-start.14
  142.3 0.8 collective-permute-start.15
  143.1 2.3 collective-permute-start.12
  145.4 6.3 %collective-permute-start.13 = (f32[1,1,64,128]{3,2,1,0:T(8,128)S(1)}, f32[1,1,64,128]{3,2,1,0:T(8,128)S(1)}, u32[]{:S(2)}, u32[]{:S(2)}) collective-permute-start(f32[1,1,64,128]{3,2,1,0:T(8,128)S(1)} %get-tuple-element.87), channel_id=1, source_target_pairs={{8,0},{16,8},{24,16},{32,24},{40,32},{48,40},{56,48},{64,56},{72,6... | collective-permute-start | bytes 98312 | tf_op jit(solution)/shard_map/ppermute | solution.py:30
  151.8 0.9 collective-permute-done.13
  153.4 0.9 copy.31
  154.3 7.3 %all-to-all-start.4 = ((f32[2,64,512]{2,0,1:T(2,128)}), f32[2,64,512]{2,0,1:T(2,128)S(1)}, u32[]{:S(2)}, u32[]{:S(2)}) async-start(f32[2,64,512]{2,0,1:T(2,128)} %copy.31), calls=%async_computation.4 | async-start | bytes 524288 | tf_op jit(solution)/shard_map/all_to_all | solution.py:127
  161.9 12.3 %all-to-all-done.4 = f32[2,64,512]{2,0,1:T(2,128)S(1)} async-done(((f32[2,64,512]{2,0,1:T(2,128)}), f32[2,64,512]{2,0,1:T(2,128)S(1)}, u32[]{:S(2)}, u32[]{:S(2)}) %all-to-all-start.4) | async-done | bytes 262176 | tf_op jit(solution)/shard_map/all_to_all | solution.py:127
  179.9 0.8 all_to_all.71
  180.8 6.3 %all-to-all-start.5 = ((f32[64,2,512]{2,1,0:T(2,128)}), f32[64,2,512]{2,1,0:T(2,128)S(1)}, u32[]{:S(2)}, u32[]{:S(2)}) async-start(f32[64,2,512]{2,1,0:T(2,128)} %all_to_all.71), calls=%async_computation.5 | async-start | bytes 524288 | tf_op jit(solution)/shard_map/all_to_all | solution.py:133
  187.1 4.8 %convolution_bitcast_fusion.1 = f32[3,3]{1,0:T(4,128)S(1)} fusion(f32[3,4,2,64,128]{4,3,2,1,0:T(8,128)S(1)} %copy-done.1), kind=kOutput, calls=%fused_computation.1 | convolution fusion | flops 7077888 | bytes 786468 | tf_op jit(solution)/shard_map/kfyzx,lfyzx->kl/dot_general | solution.py:215
  191.9 7.5 %all-to-all-done.5 = f32[64,2,512]{2,1,0:T(2,128)S(1)} async-done(((f32[64,2,512]{2,1,0:T(2,128)}), f32[64,2,512]{2,1,0:T(2,128)S(1)}, u32[]{:S(2)}, u32[]{:S(2)}) %all-to-all-start.5) | async-done | bytes 262176 | tf_op jit(solution)/shard_map/all_to_all | solution.py:133
  199.5 4.9 %convolution_bitcast_fusion.2 = f32[3]{0:T(128)S(1)} fusion(f32[3,4,2,64,128]{4,3,2,1,0:T(8,128)S(1)} %copy-done.1, f32[4,2,64,128,1]{3,2,0,1,4:T(8,128)S(1)} %bitcast.100), kind=kOutput, calls=%fused_computation.2 | convolution fusion | flops 2359296 | bytes 1048588 | tf_op jit(solution)/shard_map/kfyzx,fyzx->k/dot_general | solution.py:214
  204.3 0.7 fusion.58
  205.0 11.6 %all-reduce.65 = (f32[3]{0:T(128)S(1)}, f32[]{:T(128)}, f32[3,3]{1,0:T(4,128)S(1)}) all-reduce(f32[3]{0:T(128)S(1)} %convolution_bitcast_fusion.2, f32[]{:T(128)} %fusion.58, f32[3,3]{1,0:T(4,128)S(1)} %convolution_bitcast_fusion.1), channel_id=1, replica_groups=mesh['wall_0'=8,'wall_1'=8,'xs_0'=4,'xs_1'=2] {'wall_0'}, use_global_device_ids=true, to_apply=%region_1.2 | all-reduce | flops 13 | bytes 104 | tf_op jit(solution)/shard_map/psum | solution.py:68
  216.6 12.4 %all-reduce.64 = (f32[3]{0:T(128)S(1)}, f32[]{:T(128)}, f32[3,3]{1,0:T(4,128)S(1)}) all-reduce(f32[3]{0:T(128)S(1)} %get-tuple-element.23, f32[]{:T(128)} %get-tuple-element.24, f32[3,3]{1,0:T(4,128)S(1)} %get-tuple-element.25), channel_id=1, replica_groups=mesh['wall_0'=8,'wall_1'=8,'xs_0'=4,'xs_1'=2] {'wall_1'}, use_global_device_ids=true, to_apply=%region_2.3 | all-reduce | flops 13 | bytes 104 | tf_op jit(solution)/shard_map/psum | solution.py:68
  229.0 8.8 %all-reduce.66 = (f32[3]{0:T(128)S(1)}, f32[]{:T(128)}, f32[3,3]{1,0:T(4,128)S(1)}) all-reduce(f32[3]{0:T(128)S(1)} %get-tuple-element.20, f32[]{:T(128)} %get-tuple-element.21, f32[3,3]{1,0:T(4,128)S(1)} %get-tuple-element.22), channel_id=1, replica_groups=mesh['wall_0'=8,'wall_1'=8,'xs_0'=4,'xs_1'=2] {'xs_0'}, use_global_device_ids=true, to_apply=%region_3.4 | all-reduce | flops 13 | bytes 104 | tf_op jit(solution)/shard_map/psum | solution.py:68
  237.8 15.3 %all-reduce.67 = (f32[3]{0:T(128)S(1)}, f32[]{:T(128)}, f32[3,3]{1,0:T(4,128)S(1)}) all-reduce(f32[3]{0:T(128)S(1)} %get-tuple-element.26, f32[]{:T(128)} %get-tuple-element.27, f32[3,3]{1,0:T(4,128)S(1)} %get-tuple-element.28), channel_id=1, replica_groups=mesh['wall_0'=8,'wall_1'=8,'xs_0'=4,'xs_1'=2] {'xs_1'}, use_global_device_ids=true, to_apply=%region_4.5 | all-reduce | flops 13 | bytes 104 | tf_op jit(solution)/shard_map/psum | solution.py:68
  253.1 0.6 broadcast_multiply_fusion
  253.7 2.1 fusion.1
  255.9 0.8 fusion.5
  258.7 0.7 copy.35
  259.4 0.6 pad_maximum_fusion.65
  (438 shorter events, 14.9 us)
Async XLA Ops:
  2.4 26.2 %collective-permute-start.2 = (f32[4,2,64,1]{3,2,1,0:T(8,128)}, f32[4,2,64,1]{3,2,1,0:T(8,128)}, u32[]{:S(2)}, u32[]{:S(2)}) collective-permute-start(f32[4,2,64,1]{3,2,1,0:T(8,128)} %get-tuple-element.69), channel_id=1, source_target_pairs={{1,0},{2,1},{3,2},{4,3},{5,4},{6,5},{7,6},{0,7},{9,8},{10,9},{11,1... | collective-permute-start | bytes 6152 | tf_op jit(solution)/shard_map/ppermute | solution.py:30
  9.2 12.0 %copy-start = (f32[4,2,64,128]{3,2,1,0:T(8,128)S(1)}, f32[4,2,64,128]{3,2,1,0:T(8,128)}, u32[]{:S(2)}) copy-start(f32[4,2,64,128]{3,2,1,0:T(8,128)} %param.6) | copy-start | bytes 786436
  9.2 21.3 %collective-permute-start.3 = (f32[4,2,64,1]{3,2,1,0:T(8,128)S(1)}, f32[4,2,64,1]{3,2,1,0:T(8,128)S(1)}, u32[]{:S(2)}, u32[]{:S(2)}) collective-permute-start(f32[4,2,64,1]{3,2,1,0:T(8,128)S(1)} %get-tuple-element.68), channel_id=1, source_target_pairs={{0,1},{1,2},{2,3},{3,4},{4,5},{5,6},{6,7},{7,0},{8,9},{9,10},{10,1... | collective-permute-start | bytes 6152 | tf_op jit(solution)/shard_map/ppermute | solution.py:29
  10.0 31.5 %collective-permute-start = (f32[4,1,64,128]{3,2,1,0:T(8,128)}, f32[4,1,64,128]{3,2,1,0:T(8,128)S(1)}, u32[]{:S(2)}, u32[]{:S(2)}) collective-permute-start(f32[4,1,64,128]{3,2,1,0:T(8,128)} %get-tuple-element.70), channel_id=1, source_target_pairs={{0,8},{8,16},{16,24},{24,32},{32,40},{40,48},{48,56},{56,64},{64,7... | collective-permute-start | bytes 393224 | tf_op jit(solution)/shard_map/ppermute | solution.py:29
  11.9 29.6 %collective-permute-start.1 = (f32[4,1,64,128]{3,2,1,0:T(8,128)}, f32[4,1,64,128]{3,2,1,0:T(8,128)S(1)}, u32[]{:S(2)}, u32[]{:S(2)}) collective-permute-start(f32[4,1,64,128]{3,2,1,0:T(8,128)} %get-tuple-element.71), channel_id=1, source_target_pairs={{8,0},{16,8},{24,16},{32,24},{40,32},{48,40},{56,48},{64,56},{72,6... | collective-permute-start | bytes 393224 | tf_op jit(solution)/shard_map/ppermute | solution.py:30
  22.1 10.6 %collective-permute-start.6 = (f32[4,2,64,1]{3,2,1,0:T(8,128)}, f32[4,2,64,1]{3,2,1,0:T(8,128)}, u32[]{:S(2)}, u32[]{:S(2)}) collective-permute-start(f32[4,2,64,1]{3,2,1,0:T(8,128)} %get-tuple-element.73), channel_id=1, source_target_pairs={{1,0},{2,1},{3,2},{4,3},{5,4},{6,5},{7,6},{0,7},{9,8},{10,9},{11,1... | collective-permute-start | bytes 6152 | tf_op jit(solution)/shard_map/ppermute | solution.py:30
  24.2 1.1 copy-start.1
  28.6 11.8 %collective-permute-start.7 = (f32[4,2,64,1]{3,2,1,0:T(8,128)}, f32[4,2,64,1]{3,2,1,0:T(8,128)}, u32[]{:S(2)}, u32[]{:S(2)}) collective-permute-start(f32[4,2,64,1]{3,2,1,0:T(8,128)} %get-tuple-element.72), channel_id=1, source_target_pairs={{0,1},{1,2},{2,3},{3,4},{4,5},{5,6},{6,7},{7,0},{8,9},{9,10},{10,1... | collective-permute-start | bytes 6152 | tf_op jit(solution)/shard_map/ppermute | solution.py:29
  29.5 1.0 copy-start.5
  30.6 2.1 copy-start.4
  30.6 11.3 %collective-permute-start.4 = (f32[4,1,64,128]{3,2,1,0:T(8,128)S(1)}, f32[4,1,64,128]{3,2,1,0:T(8,128)S(1)}, u32[]{:S(2)}, u32[]{:S(2)}) collective-permute-start(f32[4,1,64,128]{3,2,1,0:T(8,128)S(1)} %copy-done.5), channel_id=1, source_target_pairs={{0,8},{8,16},{16,24},{24,32},{32,40},{40,48},{48,56},{56,64},{64,7... | collective-permute-start | bytes 393224 | tf_op jit(solution)/shard_map/ppermute | solution.py:29
  32.7 10.2 %collective-permute-start.5 = (f32[4,1,64,128]{3,2,1,0:T(8,128)S(1)}, f32[4,1,64,128]{3,2,1,0:T(8,128)S(1)}, u32[]{:S(2)}, u32[]{:S(2)}) collective-permute-start(f32[4,1,64,128]{3,2,1,0:T(8,128)S(1)} %copy-done.4), channel_id=1, source_target_pairs={{8,0},{16,8},{24,16},{32,24},{40,32},{48,40},{56,48},{64,56},{72,6... | collective-permute-start | bytes 393224 | tf_op jit(solution)/shard_map/ppermute | solution.py:30
  41.9 1.0 copy-start.2
  43.4 1.0 copy-start.3
  44.7 1.0 slice-start
  44.7 1.2 slice-start.1
  46.9 11.5 %collective-permute-start.10 = (f32[3,2,64,1]{3,2,1,0:T(8,128)S(1)}, f32[3,2,64,1]{3,2,1,0:T(8,128)S(1)}, u32[]{:S(2)}, u32[]{:S(2)}) collective-permute-start(f32[3,2,64,1]{3,2,1,0:T(8,128)S(1)} %get-tuple-element.52), channel_id=1, source_target_pairs={{1,0},{2,1},{3,2},{4,3},{5,4},{6,5},{7,6},{0,7},{9,8},{10,9},{11,1... | collective-permute-start | bytes 4616 | tf_op jit(solution)/shard_map/ppermute | solution.py:30
  49.7 8.7 %collective-permute-start.11 = (f32[3,2,64,1]{3,2,1,0:T(8,128)S(1)}, f32[3,2,64,1]{3,2,1,0:T(8,128)S(1)}, u32[]{:S(2)}, u32[]{:S(2)}) collective-permute-start(f32[3,2,64,1]{3,2,1,0:T(8,128)S(1)} %get-tuple-element.51), channel_id=1, source_target_pairs={{0,1},{1,2},{2,3},{3,4},{4,5},{5,6},{6,7},{7,0},{8,9},{9,10},{10,1... | collective-permute-start | bytes 4616 | tf_op jit(solution)/shard_map/ppermute | solution.py:29
  49.7 8.7 %collective-permute-start.8 = (f32[3,1,64,128]{3,2,1,0:T(8,128)S(1)}, f32[3,1,64,128]{3,2,1,0:T(8,128)S(1)}, u32[]{:S(2)}, u32[]{:S(2)}) collective-permute-start(f32[3,1,64,128]{3,2,1,0:T(8,128)S(1)} %get-tuple-element.49), channel_id=1, source_target_pairs={{0,8},{8,16},{16,24},{24,32},{32,40},{40,48},{48,56},{56,64},{64,7... | collective-permute-start | bytes 294920 | tf_op jit(solution)/shard_map/ppermute | solution.py:29
  51.7 8.3 %collective-permute-start.9 = (f32[3,1,64,128]{3,2,1,0:T(8,128)S(1)}, f32[3,1,64,128]{3,2,1,0:T(8,128)S(1)}, u32[]{:S(2)}, u32[]{:S(2)}) collective-permute-start(f32[3,1,64,128]{3,2,1,0:T(8,128)S(1)} %get-tuple-element.50), channel_id=1, source_target_pairs={{8,0},{16,8},{24,16},{32,24},{40,32},{48,40},{56,48},{64,56},{72,6... | collective-permute-start | bytes 294920 | tf_op jit(solution)/shard_map/ppermute | solution.py:30
  60.4 0.6 copy-start.12
  60.6 0.6 copy-start.9
  60.6 0.6 copy-start.10
  60.6 0.7 copy-start.11
  61.3 0.6 copy-start.8
  61.3 0.6 copy-start.14
  61.8 0.7 copy-start.6
  61.8 0.7 copy-start.7
  61.8 0.7 copy-start.15
  66.7 16.3 %all-to-all-start = ((f32[8,128,128]{2,1,0:T(8,128)}), f32[8,128,128]{2,1,0:T(8,128)S(1)}, u32[]{:S(2)}, u32[]{:S(2)}) async-start(f32[8,128,128]{2,1,0:T(8,128)} %fusion.23), calls=%async_computation | async-start | bytes 1048576 | tf_op jit(solution)/shard_map/all_to_all | solution.py:48
  84.0 18.8 %all-to-all-start.1 = ((f32[2,64,128]{2,0,1:T(2,128)}), f32[2,64,128]{2,0,1:T(2,128)S(1)}, u32[]{:S(2)}, u32[]{:S(2)}) async-start(f32[2,64,128]{2,0,1:T(2,128)} %copy.26), calls=%async_computation.1 | async-start | bytes 131072 | tf_op jit(solution)/shard_map/all_to_all | solution.py:127
  121.2 16.3 %all-to-all-start.3 = ((f32[8,128,2,64]{1,3,2,0:T(8,128)}), f32[8,128,2,64]{1,3,2,0:T(8,128)S(1)}, u32[]{:S(2)}, u32[]{:S(2)}) async-start(f32[8,128,2,64]{1,3,2,0:T(8,128)} %broadcast_in_dim.114), calls=%async_computation.3 | async-start | bytes 1048576 | tf_op jit(solution)/shard_map/all_to_all | solution.py:60
  128.2 0.7 copy-start.13
  141.3 10.4 %collective-permute-start.14 = (f32[1,2,64,1]{3,2,1,0:T(8,128)S(1)}, f32[1,2,64,1]{3,2,1,0:T(8,128)S(1)}, u32[]{:S(2)}, u32[]{:S(2)}) collective-permute-start(f32[1,2,64,1]{3,2,1,0:T(8,128)S(1)} %get-tuple-element.85), channel_id=1, source_target_pairs={{1,0},{2,1},{3,2},{4,3},{5,4},{6,5},{7,6},{0,7},{9,8},{10,9},{11,1... | collective-permute-start | bytes 1544 | tf_op jit(solution)/shard_map/ppermute | solution.py:30
  142.3 9.4 %collective-permute-start.15 = (f32[1,2,64,1]{3,2,1,0:T(8,128)S(1)}, f32[1,2,64,1]{3,2,1,0:T(8,128)S(1)}, u32[]{:S(2)}, u32[]{:S(2)}) collective-permute-start(f32[1,2,64,1]{3,2,1,0:T(8,128)S(1)} %get-tuple-element.84), channel_id=1, source_target_pairs={{0,1},{1,2},{2,3},{3,4},{4,5},{5,6},{6,7},{7,0},{8,9},{9,10},{10,1... | collective-permute-start | bytes 1544 | tf_op jit(solution)/shard_map/ppermute | solution.py:29
  143.1 8.7 %collective-permute-start.12 = (f32[1,1,64,128]{3,2,1,0:T(8,128)S(1)}, f32[1,1,64,128]{3,2,1,0:T(8,128)S(1)}, u32[]{:S(2)}, u32[]{:S(2)}) collective-permute-start(f32[1,1,64,128]{3,2,1,0:T(8,128)S(1)} %get-tuple-element.86), channel_id=1, source_target_pairs={{0,8},{8,16},{16,24},{24,32},{32,40},{40,48},{48,56},{56,64},{64,7... | collective-permute-start | bytes 98312 | tf_op jit(solution)/shard_map/ppermute | solution.py:29
  145.4 7.3 %collective-permute-start.13 = (f32[1,1,64,128]{3,2,1,0:T(8,128)S(1)}, f32[1,1,64,128]{3,2,1,0:T(8,128)S(1)}, u32[]{:S(2)}, u32[]{:S(2)}) collective-permute-start(f32[1,1,64,128]{3,2,1,0:T(8,128)S(1)} %get-tuple-element.87), channel_id=1, source_target_pairs={{8,0},{16,8},{24,16},{32,24},{40,32},{48,40},{56,48},{64,56},{72,6... | collective-permute-start | bytes 98312 | tf_op jit(solution)/shard_map/ppermute | solution.py:30
  154.3 19.8 %all-to-all-start.4 = ((f32[2,64,512]{2,0,1:T(2,128)}), f32[2,64,512]{2,0,1:T(2,128)S(1)}, u32[]{:S(2)}, u32[]{:S(2)}) async-start(f32[2,64,512]{2,0,1:T(2,128)} %copy.31), calls=%async_computation.4 | async-start | bytes 524288 | tf_op jit(solution)/shard_map/all_to_all | solution.py:127
  180.8 18.6 %all-to-all-start.5 = ((f32[64,2,512]{2,1,0:T(2,128)}), f32[64,2,512]{2,1,0:T(2,128)S(1)}, u32[]{:S(2)}, u32[]{:S(2)}) async-start(f32[64,2,512]{2,1,0:T(2,128)} %all_to_all.71), calls=%async_computation.5 | async-start | bytes 524288 | tf_op jit(solution)/shard_map/all_to_all | solution.py:133
where the time goes:
time: 261 us; the launch traced here: 260 us
  starting transfers between devices  85.6 us (33%)
  blocking collectives  63 us (24%)
  waiting for transfers between devices  51 us (20%)
  local copies, waits for them, and re-layouts  23.9 us (9%)
  matrix products  20.5 us (8%)
  other arithmetic  11.2 us (4%)
  between operations  4.87 us (2%)
    psum x4, blocking collectives, over_axes(): return functools.reduce(lax.psum, axes, x)  48.1 us
    ppermute x8, starting transfers between devices, padded_2(): lax.ppermute(leading, axis, [(b, a) for a, b in up])  41 us
    all_to_all x2, waiting for transfers between devices, column_solve(): lax.all_to_all(flat_rows, WALL, split_axis=1, concat_axis=0, tiled=True)  23.3 us
    all_to_all x2, starting transfers between devices, column_solve(): lax.all_to_all(flat_rows, WALL, split_axis=1, concat_axis=0, tiled=True)  15.1 us
    all_to_all x1, blocking collectives, column_solve(): back = lax.all_to_all(solved, WALL, split_axis=0, concat_axis=1, tiled=True)  14.9 us
    ppermute x8, starting transfers between devices, padded_2(): lax.ppermute(last, axis, up)  9.33 us
    all_to_all x1, waiting for transfers between devices, sum_at_owner(): lax.all_to_all(pieces, axis, split_axis=0, concat_axis=0, tiled=True)  9.11 us
    all_to_all x1, waiting for transfers between devices, from_everyone(): lax.all_to_all(jnp.broadcast_to(x[None], (length, *x.shape)), axis, 0, 0,...  8.7 us
  transfers between devices with their start and end apart: 21, of which 7 were waited for; matrix products, arithmetic and copies ran while one was open for 6% of the time, Pallas kernels for 0%

commit v1 on v0

v1 whole, which is shorter than its diff:
```python
import math

import jax
import jax.numpy as jnp
import ml_dtypes
import numpy as np
from jax import lax
from jax.experimental import pallas as pl
from jax.experimental.pallas import tpu as pltpu
from jax.sharding import Mesh
from jax.sharding import PartitionSpec as P

WALL = ("wall_0", "wall_1")
XS = ("xs_0", "xs_1")

ADV_STEP = 0.2
BUOYANCY = 0.5
SCREENING = 0.004
EPSILON = 1e-06

NX, NY, NZ = 1024, 128, 64
LINES, LANES, BLOCKS = 8, 128, 8
HALF = math.sqrt(0.5)


def split(table):
    high = table.astype(ml_dtypes.bfloat16)
    low = (table - high.astype(np.float64)).astype(ml_dtypes.bfloat16)
    return high, low


def spanwise_tables():
    cells = np.arange(NZ)
    table = np.zeros((NZ, NZ))
    eigen = np.zeros((NZ // 2, 2))
    slope = np.zeros((NZ // 2, 2))
    for pair in range(NZ // 2):
        if pair == 0:
            table[0] = 1.0 / math.sqrt(NZ)
            table[1] = np.cos(math.pi * cells) / math.sqrt(NZ)
            eigen[0] = (0.0, 4.0)
            continue
        angle = 2.0 * math.pi * (cells * pair % NZ) / NZ
        table[2 * pair] = np.cos(angle) * math.sqrt(2.0 / NZ)
        table[2 * pair + 1] = np.sin(angle) * math.sqrt(2.0 / NZ)
        eigen[pair] = 4.0 * math.sin(math.pi * pair / NZ) ** 2
        wave = math.sin(2.0 * math.pi * pair / NZ)
        slope[pair] = (wave, -wave)
    return table, eigen, slope


def stream_tables():
    cells = np.arange(LANES)
    weights = np.zeros((4, 2 * LANES, 2 * LANES))
    eigen = np.zeros((16, 2, 32))
    slope = np.zeros((16, 2, 32))
    for tile in range(8):
        group = tile // 2
        base = (0, 4)[tile] if group == 0 else group
        first = 0 if group == 0 else 64 * (tile % 2)
        for slot in range(64):
            wave = 8 * (first + slot) + base
            half, place = divmod(slot, 32)
            block = 2 * tile + half
            at = (tile % 2) * LANES + half * 64 + place
            angle = 2.0 * math.pi * (cells * wave % NX) / NX
            scale = math.sqrt(2.0 / NX)
            if wave == 0:
                alternate = np.cos(math.pi * cells)
                weights[0, :LANES, at] = 1.0 / math.sqrt(NX)
                weights[0, :LANES, at + 32] = alternate / math.sqrt(NX)
                eigen[block, :, place] = (0.0, 4.0)
                continue
            eigen[block, :, place] = 4.0 * math.sin(math.pi * wave / NX) ** 2
            rise = math.sin(2.0 * math.pi * wave / NX)
            slope[block, :, place] = (rise, -rise)
            cos, sin = scale * np.cos(angle), scale * np.sin(angle)
            if group == 0:
                rows = slice((tile % 2) * LANES, (tile % 2 + 1) * LANES)
                weights[0, rows, at] = cos
                weights[0, rows, at + 32] = sin
            else:
                weights[group, :LANES, at] = cos
                weights[group, LANES:, at] = -sin
                weights[group, :LANES, at + 32] = sin
                weights[group, LANES:, at + 32] = cos
    return weights, eigen, slope


def wall_tables():
    order = np.arange(1, NY + 1)
    sine = np.sin(math.pi * (np.outer(order, order) % (2 * NY + 2)) / (NY + 1))
    sine = sine * math.sqrt(2.0 / (NY + 1))
    shift = np.eye(NY, k=1)
    slope = 0.5 * (shift - shift.T)
    eigen = 2.0 - 2.0 * np.cos(math.pi * order / (NY + 1))
    rows = np.concatenate([np.arange(0, NY, 2), np.arange(1, NY, 2)])
    return sine[:, rows], sine @ slope @ sine, eigen


def column_tables():
    _, span_eigen, span_slope = spanwise_tables()
    _, stream_eigen, stream_slope = stream_tables()
    stream = np.zeros((16, 2, LANES), np.float32)
    for block in range(16):
        stream[block, 0] = np.tile(stream_eigen[block].reshape(-1), 2)
        stream[block, 1] = np.tile(stream_slope[block].reshape(-1), 2)
    span = np.zeros((NZ, 2, LANES), np.float32)
    for pair in range(NZ // 2):
        for odd in range(2):
            turn = slice(None, None, -1 if odd else 1)
            span[2 * pair + odd, 0] = np.repeat(span_eigen[pair][turn], 64)
            span[2 * pair + odd, 1] = np.repeat(span_slope[pair][turn], 64)
    return stream, span


def halves(x):
    high = x.astype(jnp.bfloat16)
    low = (x - high.astype(jnp.float32)).astype(jnp.bfloat16)
    return high, low


def dot(a, b):
    return jnp.dot(a, b, preferred_element_type=jnp.float32)


def times_table(x, high_table, low_table):
    high, low = halves(x)
    return dot(high, high_table) + (dot(low, high_table) + dot(high, low_table))


def table_times(high_table, low_table, x):
    high, low = halves(x)
    return dot(high_table, high) + (dot(high_table, low) + dot(low_table, high))


def lane_ids(rows):
    return lax.broadcasted_iota(jnp.int32, (rows, LANES), 1)


def edges_kernel(vec_ref, base_ref, low_x, high_x, low_y, high_y):
    lanes = lane_ids(NZ)
    low = jnp.zeros((NZ, LANES), jnp.float32)
    high = jnp.zeros((NZ, LANES), jnp.float32)
    for field in range(8):
        ref, part = (vec_ref.at[0], field) if field < 4 else (base_ref, field - 4)
        for row in range(2):
            block = ref[part, row]
            at = 2 * field + row
            low = jnp.where(lanes == at, pltpu.roll(block, at, 1), low)
            high = jnp.where(lanes == at, pltpu.roll(block, (at + 1) % LANES, 1), high)
            if row == 0:
                low_y[field] = block
            else:
                high_y[field] = block
    low_x[...] = low
    high_x[...] = high


def advect_kernel(
    vec_ref, base_ref, left_ref, right_ref, below_ref, above_ref, th_ref, tl_ref, out_ref
):
    lanes = lane_ids(NZ)
    first, last = lanes == 0, lanes == LANES - 1
    left, right = left_ref[...], right_ref[...]

    def value(field, row):
        return vec_ref[0, field, row] if field < 4 else base_ref[field - 4, row]

    def slopes(field, row):
        x = value(field, row)
        at = 2 * field + row
        up = jnp.where(last, pltpu.roll(right, (LANES - 1 - at) % LANES, 1), pltpu.roll(x, LANES - 1, 1))
        down = jnp.where(first, pltpu.roll(left, (LANES - at) % LANES, 1), pltpu.roll(x, 1, 1))
        along_x = (up - down) * 0.5
        if row == 0:
            along_y = (value(field, 1) - below_ref[field]) * 0.5
        else:
            along_y = (above_ref[field] - value(field, 0)) * 0.5
        along_z = (pltpu.roll(x, NZ - 1, 0) - pltpu.roll(x, 1, 0)) * 0.5
        return along_x, along_y, along_z

    high_table, low_table = th_ref[...], tl_ref[...]
    for row in range(2):
        for field in range(4):
            grad = slopes(field, row)
            base_grad = slopes(field + 4, row)
            advect = jnp.zeros((NZ, LANES), jnp.float32)
            for axis in range(3):
                advect += value(4 + axis, row) * grad[axis]
                advect += value(axis, row) * base_grad[axis]
            updated = value(field, row) - ADV_STEP * advect
            if field == 1:
                updated += BUOYANCY * value(3, row)
            modes = table_times(high_table, low_table, updated)
            out_ref[pl.ds(2 * field + row, NZ, stride=LINES), :] = modes


def stream_kernel(in_ref, wh_ref, wl_ref, out_ref):
    x = [in_ref[s] for s in range(BLOCKS)]
    s04, d04 = x[0] + x[4], x[0] - x[4]
    s26, d26 = x[2] + x[6], x[2] - x[6]
    s15, d15 = x[1] + x[5], x[1] - x[5]
    s37, d37 = x[3] + x[7], x[3] - x[7]
    even, odd = s04 + s26, s15 + s37
    minus, plus = HALF * (d15 - d37), HALF * (d15 + d37)
    parts = [
        (even + odd, even - odd),
        (d04 + minus, plus + d26),
        (s04 - s26, s15 - s37),
        (d04 - minus, plus - d26),
    ]
    front = lane_ids(LINES) < 64
    for group in range(4):
        joined = jnp.concatenate(parts[group], axis=1)
        modes = times_table(joined, wh_ref[group], wl_ref[group])
        for side in range(2):
            tile = 2 * group + side
            for pair in range(4):
                cols = slice(side * LANES, (side + 1) * LANES)
                cos = modes[16 * pair : 16 * pair + 8, cols]
                sin = pltpu.roll(modes[16 * pair + 8 : 16 * pair + 16, cols], 64, 1)
                out_ref[16 * pair + 2 * tile] = jnp.where(front, cos, sin)
                out_ref[16 * pair + 2 * tile + 1] = jnp.where(front, sin, cos)


def solve_kernel(
    place_ref, diff_ref, in_ref, sh_ref, sl_ref, bh_ref, bl_ref, eh_ref, el_ref,
    eigen_ref, stream_ref, span_ref, out_ref,
):
    def field_rows(field):
        return jnp.concatenate(
            [in_ref[pl.ds(2 * field + row, NZ, stride=LINES), :] for row in range(2)], axis=0
        )

    fields = jnp.concatenate([field_rows(field) for field in range(4)], axis=1)
    waves = table_times(sh_ref[...], sl_ref[...], fields)
    u, v, w, heat = (waves[:, LANES * f : LANES * (f + 1)] for f in range(4))
    stream = stream_ref[place_ref[0]]
    span = span_ref[place_ref[1]]
    column = stream[0:1] + span[0:1] + SCREENING
    wall_eigen = eigen_ref[...]
    lower = lane_ids(NY) % 64 < 32

    def slope_x(f):
        return stream[1:2] * jnp.where(lower, pltpu.roll(f, LANES - 32, 1), pltpu.roll(f, 32, 1))

    def slope_z(f):
        return span[1:2] * pltpu.roll(f, 64, 1)

    def slope_y(f):
        return table_times(eh_ref[...], el_ref[...], f)

    divergence = slope_x(u) + slope_y(v) + slope_z(w)
    pressure = -divergence / (wall_eigen + column)
    corrected = (u - slope_x(pressure), v - slope_y(pressure), w - slope_z(pressure), heat)
    scaled = []
    for field in range(4):
        shift = 1.0 / (jnp.zeros((NY, LANES), jnp.float32) + diff_ref[field])
        scaled.append(corrected[field] * (shift / (wall_eigen + shift)))
    rows = table_times(bh_ref[...], bl_ref[...], jnp.concatenate(scaled, axis=1))
    for field in range(4):
        for row in range(2):
            out_ref[pl.ds(2 * field + row, NZ, stride=LINES), :] = rows[
                NZ * row : NZ * (row + 1), LANES * field : LANES * (field + 1)
            ]


def stream_back_kernel(in_ref, wh_ref, wl_ref, out_ref):
    front = lane_ids(LINES) < 64
    parts = []
    for group in range(4):
        sides = []
        for side in range(2):
            tile = 2 * group + side
            lines = []
            for pair in range(4):
                one = in_ref[16 * pair + 2 * tile]
                two = in_ref[16 * pair + 2 * tile + 1]
                lines.append(jnp.where(front, one, two))
                lines.append(pltpu.roll(jnp.where(front, two, one), 64, 1))
            sides.append(jnp.concatenate(lines, axis=0))
        cells = times_table(jnp.concatenate(sides, axis=1), wh_ref[group], wl_ref[group])
        parts.append((cells[:, :LANES], cells[:, LANES:]))
    (c0, c4), (c1, s1), (c2, s2), (c3, s3) = parts
    sum04, dif04 = c0 + c4, c0 - c4
    sum13, dif13 = c1 + c3, HALF * (c1 - c3)
    plus13, minus13 = HALF * (s1 + s3), s1 - s3
    outer_a, outer_b = sum04 + c2, sum04 - c2
    inner_a, inner_b = dif04 + s2, dif04 - s2
    out_ref[0] = outer_a + sum13
    out_ref[4] = outer_a - sum13
    out_ref[2] = outer_b + minus13
    out_ref[6] = outer_b - minus13
    out_ref[1] = inner_a + (dif13 + plus13)
    out_ref[5] = inner_a - (dif13 + plus13)
    out_ref[3] = inner_b + (plus13 - dif13)
    out_ref[7] = inner_b - (plus13 - dif13)


PAIRS = ((0, 0), (0, 1), (0, 2), (1, 1), (1, 2), (2, 2))


def folded(x):
    total = x[:LINES]
    for part in range(1, NZ // LINES):
        total += x[LINES * part : LINES * (part + 1)]
    return total


def cells_kernel(in_ref, vec_ref, th_ref, tl_ref, cur_ref, sums_ref):
    sums = [jnp.zeros((LINES, LANES), jnp.float32) for _ in range(10)]
    high_table, low_table = th_ref[...], tl_ref[...]
    for field in range(4):
        for row in range(2):
            modes = in_ref[pl.ds(2 * field + row, NZ, stride=LINES), :]
            cells = table_times(high_table, low_table, modes)
            cur_ref[field, row] = cells
            vectors = [vec_ref[q, field, row] for q in range(3)]
            for q in range(3):
                sums[q] += folded(vectors[q] * cells)
            sums[3] += folded(cells * cells)
            for at, (q, p) in enumerate(PAIRS):
                sums[4 + at] += folded(vectors[q] * vectors[p])
    lanes = lane_ids(LINES)
    packed = jnp.zeros((LINES, LANES), jnp.float32)
    for at in range(10):
        packed = jnp.where(lanes == at, jnp.sum(sums[at]), packed)
    sums_ref[...] = packed


def residual_kernel(sums_ref, cur_ref, vec_ref, out_ref, hess_ref):
    entries = float(4 * NX * NY * NZ)
    totals = jnp.sum(sums_ref[...], axis=0, keepdims=True) * (1.0 / entries)
    lanes = lane_ids(1)

    def pick(at):
        return jnp.sum(jnp.where(lanes == at, totals, 0.0), axis=1, keepdims=True)

    values = [pick(at) for at in range(10)]
    products = values[:3]
    square = values[3]
    for q in range(3):
        square = square - 2.0 * products[q] * products[q]
    for at, (q, p) in enumerate(PAIRS):
        twice = 1.0 if q == p else 2.0
        square = square + twice * products[q] * products[p] * values[4 + at]
    norm = jnp.sqrt(square + EPSILON)
    hess = jnp.where(lanes == 3, norm, 0.0)
    for q in range(3):
        hess = jnp.where(lanes == q, products[q], hess)
    hess_ref[...] = hess
    scale = 1.0 / norm
    for field in range(4):
        for row in range(2):
            left = cur_ref[field, row]
            for q in range(3):
                left = left - products[q] * vec_ref[q, field, row]
            out_ref[field, row] = left * scale


VMEM = pl.BlockSpec(memory_space=pltpu.VMEM)
SMEM = pl.BlockSpec(memory_space=pltpu.SMEM)


def f32(*dims):
    return jax.ShapeDtypeStruct(dims, jnp.float32)


def shards(krylov_basis, base_state, diffusivity):
    span, _, _ = spanwise_tables()
    stream, _, _ = stream_tables()
    sine, wall_slope, wall_eigen = wall_tables()
    stream_columns, span_columns = column_tables()
    eigen = np.broadcast_to(wall_eigen[:, None], (NY, LANES)).astype(np.float32)

    last = pl.BlockSpec((1, 4, 2, NZ, LANES), lambda i: (2, 0, 0, 0, 0))
    base_spec = pl.BlockSpec((4, 2, NZ, LANES), lambda i: (0, 0, 0, 0))
    low_x, high_x, low_y, high_y = pl.pallas_call(
        edges_kernel,
        grid=(1,),
        in_specs=[last, base_spec],
        out_specs=[VMEM] * 4,
        out_shape=[f32(NZ, LANES), f32(NZ, LANES), f32(8, NZ, LANES), f32(8, NZ, LANES)],
        name="edges",
    )(krylov_basis, base_state)
    size, walls = lax.axis_size(XS), lax.axis_size(WALL)
    above = lax.ppermute(low_y, WALL, [(i + 1, i) for i in range(walls - 1)])
    below = lax.ppermute(high_y, WALL, [(i, i + 1) for i in range(walls - 1)])
    right = lax.ppermute(low_x, XS, [((i + 1) % size, i) for i in range(size)])
    left = lax.ppermute(high_x, XS, [(i, (i + 1) % size) for i in range(size)])

    modes = pl.pallas_call(
        advect_kernel,
        grid=(1,),
        in_specs=[last, base_spec] + [VMEM] * 6,
        out_specs=VMEM,
        out_shape=f32(NZ * LINES, LANES),
        name="advect",
    )(krylov_basis, base_state, left, right, below, above, *split(span))
    lines = lax.all_to_all(modes.reshape(BLOCKS, -1, LANES), XS, 0, 0, tiled=True)
    spectra = pl.pallas_call(
        stream_kernel,
        in_specs=[VMEM] * 3,
        out_specs=VMEM,
        out_shape=f32(walls, LINES, LANES),
        name="stream",
    )(lines, *split(stream))
    columns = lax.all_to_all(spectra, WALL, 0, 0, tiled=True)
    wall_pos, stream_pos = lax.axis_index(WALL), lax.axis_index(XS)
    block = wall_pos % 16
    pair = stream_pos * 4 + wall_pos // 16
    place = jnp.stack([block, 2 * pair + block % 2])
    solved = pl.pallas_call(
        solve_kernel,
        in_specs=[SMEM, SMEM] + [VMEM] * 10,
        out_specs=VMEM,
        out_shape=f32(NZ * LINES, LANES),
        name="solve",
    )(
        place, diffusivity, columns.reshape(-1, LANES),
        *split(sine), *split(sine.T), *split(wall_slope),
        eigen, stream_columns, span_columns,
    )
    spectra = lax.all_to_all(solved.reshape(walls, LINES, LANES), WALL, 0, 0, tiled=True)
    lines = pl.pallas_call(
        stream_back_kernel,
        in_specs=[VMEM] * 3,
        out_specs=VMEM,
        out_shape=f32(BLOCKS, NZ, LANES),
        name="stream_back",
    )(spectra, *split(stream.transpose(0, 2, 1)))
    modes = lax.all_to_all(lines, XS, 0, 0, tiled=True)
    current, sums = pl.pallas_call(
        cells_kernel,
        in_specs=[VMEM] * 4,
        out_specs=[VMEM] * 2,
        out_shape=[f32(4, 2, NZ, LANES), f32(LINES, LANES)],
        name="cells",
    )(modes.reshape(-1, LANES), krylov_basis, *split(span.T))
    sums = lax.all_to_all(sums, XS, 0, 0, tiled=True).sum(axis=0)
    sums = lax.all_to_all(jnp.broadcast_to(sums, (walls, LANES)), WALL, 0, 0, tiled=True)
    new_vector, hessenberg = pl.pallas_call(
        residual_kernel,
        in_specs=[VMEM] * 3,
        out_specs=[VMEM] * 2,
        out_shape=[f32(4, 2, NZ, LANES), f32(1, LANES)],
        name="residual",
    )(sums, current, krylov_basis)
    return new_vector, hessenberg[0, :4]


def solution(mesh):
    torus = Mesh(mesh.devices.reshape(8, 8, 4, 2), ("wall_0", "wall_1", "xs_0", "xs_1"))
    return jax.shard_map(
        shards,
        mesh=torus,
        in_specs=(P(None, None, WALL, None, XS), P(None, WALL, None, XS), P()),
        out_specs=(P(None, WALL, None, XS), P()),
        check_vma=False,
    )
```

time: 261 us -> 133 us (0.51)
  starting transfers between devices: 85.6 us -> 24.6 us
  waiting for transfers between devices: 51 us -> 13.7 us
  local copies, waits for them, and re-layouts: 23.9 us -> 2.91 us
  matrix products: 20.5 us -> 0 us
  Pallas kernels: 0 us -> 16.6 us
  other arithmetic: 11.2 us -> 0.69 us
  blocking collectives: 63 us -> 72.5 us
  between operations: 4.87 us -> 0.72 us
    all_to_all x1 -> x5, blocking collectives: 14.9 us -> 72.5 us  [the longest x1 18.7 us: shards(): lax.all_to_all(solved.reshape(walls, LINES, LANES), WALL, 0, 0, tiled=True)]
    psum x4 -> x0, blocking collectives: 48.1 us -> none  [over_axes(): return functools.reduce(lax.psum, axes, x)]
    ppermute x16 -> x4, starting transfers between devices: 50.4 us -> 9.46 us  [the longest x1 4.02 us: shards(): below = lax.ppermute(high_y, WALL, [(i, i + 1) for i in range(walls - 1)])]
    all_to_all x5 -> x1, waiting for transfers between devices: 48.6 us -> 11.8 us  [shards(): columns = lax.all_to_all(spectra, WALL, 0, 0, tiled=True)]
    dot_general x8 -> x0, matrix products: 20.5 us -> none  [the longest x1 4.86 us: shards(): jnp.einsum('kfyzx,fyzx->k', krylov_basis, current, precision=highest_mode)]
    all_to_all x5 -> x1, starting transfers between devices: 35.2 us -> 15.1 us  [shards(): columns = lax.all_to_all(spectra, WALL, 0, 0, tiled=True)]
    pallas_call x0 -> x7, Pallas kernels: none -> 16.6 us  [the longest x1 2.73 us: shards(): pl.pallas_call(advect_kernel, grid=(1,), in_specs=[last, base_spec] + [VM...]
    slice x184 -> x0, local copies, waits for them, and re-layouts: 8.75 us -> none  [the longest x7 2.58 us: padded_2(): last = lax.slice_in_dim(x, length - width, length, axis=dim)]
  transfers between devices with their start and end apart: 21 -> 5, of which waited for: 7 -> 4; matrix products, arithmetic and copies ran while one was open for 6% -> 1% of each run, Pallas kernels for 0% -> 0%
where the time goes in v1:
time: 133 us; the launch traced here: 132 us
  blocking collectives  72.5 us (55%)
  starting transfers between devices  24.6 us (18%)
  Pallas kernels  16.6 us (12%)
  waiting for transfers between devices  13.7 us (10%)
  local copies, waits for them, and re-layouts  2.91 us (2%)
    all_to_all x1, blocking collectives, shards(): lax.all_to_all(solved.reshape(walls, LINES, LANES), WALL, 0, 0, tiled=True)  18.7 us
    all_to_all x1, blocking collectives, shards(): lax.all_to_all(modes.reshape(BLOCKS, -1, LANES), XS, 0, 0, tiled=True)  15.4 us
    all_to_all x1, blocking collectives, shards(): lax.all_to_all(jnp.broadcast_to(sums, (walls, LANES)), WALL, 0, 0, tiled=...  15.4 us
    all_to_all x1, starting transfers between devices, shards(): columns = lax.all_to_all(spectra, WALL, 0, 0, tiled=True)  15.1 us
    all_to_all x1, blocking collectives, shards(): modes = lax.all_to_all(lines, XS, 0, 0, tiled=True)  14.2 us
    all_to_all x1, waiting for transfers between devices, shards(): columns = lax.all_to_all(spectra, WALL, 0, 0, tiled=True)  11.8 us
    all_to_all x1, blocking collectives, shards(): sums = lax.all_to_all(sums, XS, 0, 0, tiled=True).sum(axis=0)  8.77 us
    ppermute x1, starting transfers between devices, shards(): below = lax.ppermute(high_y, WALL, [(i, i + 1) for i in range(walls - 1)])  4.02 us
  transfers between devices with their start and end apart: 5, of which 4 were waited for; matrix products, arithmetic and copies ran while one was open for 1% of the time, Pallas kernels for 0%

profile of v1, /device:TPU:1, one launch (start us, length us, event | category | flops | bytes accessed | tf_op | source)
XLA Modules:
  0.0 131.8 jit_solution(11002475830851671955)
XLA Ops:
  0.6 2.1 %edges.1 = (f32[64,128]{1,0:T(8,128)}, f32[64,128]{1,0:T(8,128)}, f32[8,64,128]{2,1,0:T(8,128)}, f32[8,64,128]{2,1,0:T(8,128)}) custom-call(f32[3,4,2,64,128]{4,3,2,1,0:T(8,128)} %vec_ref.7, f32[4,2,64,128]{3,2,1,0:T(8,128)} %base_ref.3), custom_call_target="tpu_custom_call" | custom-call | tf_op jit(solution)/shard_map/edges/pallas_call | solution.py:379
  2.7 4.0 %collective-permute-start.2 = (f32[8,64,128]{2,1,0:T(8,128)}, f32[8,64,128]{2,1,0:T(8,128)S(1)}, u32[]{:S(2)}, u32[]{:S(2)}) collective-permute-start(f32[8,64,128]{2,1,0:T(8,128)} %get-tuple-element.12), channel_id=1, source_target_pairs={{0,8},{8,16},{16,24},{24,32},{32,40},{40,48},{48,56},{56,64},{64,7... | collective-permute-start | bytes 786440 | tf_op jit(solution)/shard_map/ppermute | solution.py:389
  6.7 1.3 collective-permute-start.3
  8.0 2.1 %collective-permute-start = (f32[64,128]{1,0:T(8,128)}, f32[64,128]{1,0:T(8,128)S(1)}, u32[]{:S(2)}, u32[]{:S(2)}) collective-permute-start(f32[64,128]{1,0:T(8,128)} %get-tuple-element.10), channel_id=1, source_target_pairs={{0,1},{1,2},{2,3},{3,4},{4,5},{5,6},{6,7},{7,0},{8,9},{9,10},{10,1... | collective-permute-start | bytes 98312 | tf_op jit(solution)/shard_map/ppermute | solution.py:391
  10.1 2.1 %collective-permute-start.1 = (f32[64,128]{1,0:T(8,128)}, f32[64,128]{1,0:T(8,128)S(1)}, u32[]{:S(2)}, u32[]{:S(2)}) collective-permute-start(f32[64,128]{1,0:T(8,128)} %get-tuple-element.11), channel_id=1, source_target_pairs={{1,0},{2,1},{3,2},{4,3},{5,4},{6,5},{7,6},{0,7},{9,8},{10,9},{11,1... | collective-permute-start | bytes 98312 | tf_op jit(solution)/shard_map/ppermute | solution.py:390
  12.2 0.9 collective-permute-done.left_ref
  13.1 0.0 copy-start.3
  13.1 0.6 collective-permute-done.1.right_ref
  13.6 0.0 copy-start.4
  13.6 0.0 collective-permute-done.2.below_ref
  13.6 0.0 copy-start.1
  13.6 0.4 collective-permute-done.3.above_ref
  14.1 0.0 copy-done.3
  14.1 0.2 copy-done.4
  14.2 0.1 copy-done.1
  14.4 0.0 copy-start.2
  14.4 0.7 copy-done.2
  15.1 2.7 %advect.1 = f32[512,128]{1,0:T(8,128)} custom-call(f32[3,4,2,64,128]{4,3,2,1,0:T(8,128)} %vec_ref.7, f32[4,2,64,128]{3,2,1,0:T(8,128)} %base_ref.3, f32[64,128]{1,0:T(8,128)} %copy-done.3, f32[64,128]{1,0:T(8,128)} %copy-done.4, f32[8,64,128]{2,1,0:T(8,128)} %copy-done.1, f32[8,64,128]{2,1,0:T(8,128)} %copy-done.2, bf16[64,64]{1,0:T(8,128)(2,1)} %constant.90.clone.th_ref, ...), custom_call_target="tpu_custom_call" | custom-call | tf_op jit(solution)/shard_map/advect/pallas_call | solution.py:393
  17.8 15.4 %all_to_all.37.in_ref = f32[8,64,128]{2,1,0:T(8,128)} all-to-all(f32[8,64,128]{2,1,0:T(8,128)} %bitcast.15), channel_id=1, replica_groups=mesh['wall_0'=8,'wall_1'=8,'xs_0'=4,'xs_1'=2] {'xs_0','xs_1'}, dimensions={0} | all-to-all | bytes 524288 | tf_op jit(solution)/shard_map/all_to_all | solution.py:401
  33.2 2.4 %stream.1 = f32[64,8,128]{2,1,0:T(8,128)} custom-call(f32[8,64,128]{2,1,0:T(8,128)} %all_to_all.37.in_ref, bf16[4,256,256]{2,1,0:T(8,128)(2,1)} %constant.92.clone.wh_ref, bf16[4,256,256]{2,1,0:T(8,128)(2,1)} %constant.93.clone.wl_ref), custom_call_target="tpu_custom_call" | custom-call | tf_op jit(solution)/shard_map/stream/pallas_call | solution.py:402
  35.7 15.1 %all-to-all-start.1 = ((f32[64,8,128]{2,1,0:T(8,128)}), f32[64,8,128]{2,1,0:T(8,128)S(1)}, u32[]{:S(2)}, u32[]{:S(2)}) async-start(f32[64,8,128]{2,1,0:T(8,128)} %stream.1), calls=%async_computation.1 | async-start | bytes 524288 | tf_op jit(solution)/shard_map/all_to_all | solution.py:409
  50.8 0.7 pad_add_fusion.place_ref
  51.5 11.8 %all-to-all-done.1 = f32[64,8,128]{2,1,0:T(8,128)S(1)} async-done(((f32[64,8,128]{2,1,0:T(8,128)}), f32[64,8,128]{2,1,0:T(8,128)S(1)}, u32[]{:S(2)}, u32[]{:S(2)}) %all-to-all-start.1) | async-done | bytes 262176 | tf_op jit(solution)/shard_map/all_to_all | solution.py:409
  63.4 0.0 copy-start
  63.4 0.7 copy-done
  64.1 2.6 %solve.1 = f32[512,128]{1,0:T(8,128)} custom-call(s32[2]{0:T(128)} %pad_add_fusion.place_ref, f32[4]{0:T(128)} %diff_ref.1, f32[512,128]{1,0:T(8,128)} %bitcast.12, bf16[128,128]{1,0:T(8,128)(2,1)} %constant.94.clone.sh_ref, bf16[128,128]{1,0:T(8,128)(2,1)} %constant.95.clone.sl_ref, bf16[128,128]{1,0:T(8,128)(2,1)} %constant.96.clone.bh_ref, ...), custom_call_target="tpu_custom_call" | custom-call | tf_op jit(solution)/shard_map/solve/pallas_call | solution.py:414
  66.7 18.7 %all_to_all.38.in_ref = f32[64,8,128]{2,1,0:T(8,128)} all-to-all(f32[64,8,128]{2,1,0:T(8,128)} %bitcast.13), channel_id=1, replica_groups=mesh['wall_0'=8,'wall_1'=8,'xs_0'=4,'xs_1'=2] {'wall_0','wall_1'}, dimensions={0} | all-to-all | bytes 524288 | tf_op jit(solution)/shard_map/all_to_all | solution.py:425
  85.3 2.4 %stream_back.1 = f32[8,64,128]{2,1,0:T(8,128)} custom-call(f32[64,8,128]{2,1,0:T(8,128)} %all_to_all.38.in_ref, bf16[4,256,256]{2,1,0:T(8,128)(2,1)} %constant.103.clone.wh_ref, bf16[4,256,256]{2,1,0:T(8,128)(2,1)} %constant.104.clone.wl_ref), custom_call_target="tpu_custom_call" | custom-call | tf_op jit(solution)/shard_map/stream_back/pallas_call | solution.py:426
  87.8 14.2 %all_to_all.39 = f32[8,64,128]{2,1,0:T(8,128)} all-to-all(f32[8,64,128]{2,1,0:T(8,128)} %stream_back.1), channel_id=1, replica_groups=mesh['wall_0'=8,'wall_1'=8,'xs_0'=4,'xs_1'=2] {'xs_0','xs_1'}, dimensions={0} | all-to-all | bytes 524288 | tf_op jit(solution)/shard_map/all_to_all | solution.py:433
  102.0 2.2 %cells.1 = (f32[4,2,64,128]{3,2,1,0:T(8,128)}, f32[8,128]{1,0:T(8,128)}) custom-call(f32[512,128]{1,0:T(8,128)} %bitcast.14, f32[3,4,2,64,128]{4,3,2,1,0:T(8,128)} %vec_ref.7, bf16[64,64]{1,0:T(8,128)(2,1)} %constant.105.clone.th_ref, bf16[64,64]{1,0:T(8,128)(2,1)} %constant.106.clone.tl_ref), custom_call_target="tpu_custom_call" | custom-call | tf_op jit(solution)/shard_map/cells/pallas_call | solution.py:434
  104.2 8.8 %all_to_all.40 = f32[8,1,128]{2,1,0:T(1,128)S(1)} all-to-all(f32[8,1,128]{2,1,0:T(1,128)} %bitcast.17), channel_id=1, replica_groups=mesh['wall_0'=8,'wall_1'=8,'xs_0'=4,'xs_1'=2] {'xs_0','xs_1'}, dimensions={0} | all-to-all | bytes 8192 | tf_op jit(solution)/shard_map/all_to_all | solution.py:441
  113.1 15.4 %all_to_all.41 = f32[64,1,128]{2,1,0:T(1,128)} all-to-all(f32[64,1,128]{2,1,0:T(1,128)S(1)} %broadcast_in_dim.3), channel_id=1, replica_groups=mesh['wall_0'=8,'wall_1'=8,'xs_0'=4,'xs_1'=2] {'wall_0','wall_1'}, dimensions={0} | all-to-all | bytes 65536 | tf_op jit(solution)/shard_map/all_to_all | solution.py:442
  128.5 2.1 %residual.1 = (f32[4,2,64,128]{3,2,1,0:T(8,128)}, f32[1,128]{1,0:T(1,128)}) custom-call(f32[64,128]{1,0:T(8,128)} %bitcast.16, f32[4,2,64,128]{3,2,1,0:T(8,128)} %get-tuple-element.15.cur_ref, f32[3,4,2,64,128]{4,3,2,1,0:T(8,128)} %vec_ref.7), custom_call_target="tpu_custom_call" | custom-call | tf_op jit(solution)/shard_map/residual/pallas_call | solution.py:443
  130.6 0.0 copy-start.5
  130.6 0.7 copy-done.5
  131.3 0.5 slice_bitcast_fusion
  (2 shorter events, 0.0 us)
Async XLA Ops:
  2.7 10.9 %collective-permute-start.2 = (f32[8,64,128]{2,1,0:T(8,128)}, f32[8,64,128]{2,1,0:T(8,128)S(1)}, u32[]{:S(2)}, u32[]{:S(2)}) collective-permute-start(f32[8,64,128]{2,1,0:T(8,128)} %get-tuple-element.12), channel_id=1, source_target_pairs={{0,8},{8,16},{16,24},{24,32},{32,40},{40,48},{48,56},{56,64},{64,7... | collective-permute-start | bytes 786440 | tf_op jit(solution)/shard_map/ppermute | solution.py:389
  6.7 7.3 %collective-permute-start.3 = (f32[8,64,128]{2,1,0:T(8,128)}, f32[8,64,128]{2,1,0:T(8,128)S(1)}, u32[]{:S(2)}, u32[]{:S(2)}) collective-permute-start(f32[8,64,128]{2,1,0:T(8,128)} %get-tuple-element.13), channel_id=1, source_target_pairs={{8,0},{16,8},{24,16},{32,24},{40,32},{48,40},{56,48},{64,56},{72,6... | collective-permute-start | bytes 786440 | tf_op jit(solution)/shard_map/ppermute | solution.py:388
  8.0 5.0 %collective-permute-start = (f32[64,128]{1,0:T(8,128)}, f32[64,128]{1,0:T(8,128)S(1)}, u32[]{:S(2)}, u32[]{:S(2)}) collective-permute-start(f32[64,128]{1,0:T(8,128)} %get-tuple-element.10), channel_id=1, source_target_pairs={{0,1},{1,2},{2,3},{3,4},{4,5},{5,6},{6,7},{7,0},{8,9},{9,10},{10,1... | collective-permute-start | bytes 98312 | tf_op jit(solution)/shard_map/ppermute | solution.py:391
  10.1 3.6 %collective-permute-start.1 = (f32[64,128]{1,0:T(8,128)}, f32[64,128]{1,0:T(8,128)S(1)}, u32[]{:S(2)}, u32[]{:S(2)}) collective-permute-start(f32[64,128]{1,0:T(8,128)} %get-tuple-element.11), channel_id=1, source_target_pairs={{1,0},{2,1},{3,2},{4,3},{5,4},{6,5},{7,6},{0,7},{9,8},{10,9},{11,1... | collective-permute-start | bytes 98312 | tf_op jit(solution)/shard_map/ppermute | solution.py:390
  13.1 1.0 copy-start.3
  13.6 0.6 copy-start.4
  13.6 0.7 copy-start.1
  14.4 0.7 copy-start.2
  35.7 27.7 %all-to-all-start.1 = ((f32[64,8,128]{2,1,0:T(8,128)}), f32[64,8,128]{2,1,0:T(8,128)S(1)}, u32[]{:S(2)}, u32[]{:S(2)}) async-start(f32[64,8,128]{2,1,0:T(8,128)} %stream.1), calls=%async_computation.1 | async-start | bytes 524288 | tf_op jit(solution)/shard_map/all_to_all | solution.py:409
  63.4 0.7 copy-start
  130.6 0.7 copy-start.5

commit v2 on v1

--- a/solution.py
+++ b/solution.py
@@ -95,7 +95,7 @@
     slope = 0.5 * (shift - shift.T)
     eigen = 2.0 - 2.0 * np.cos(math.pi * order / (NY + 1))
     rows = np.concatenate([np.arange(0, NY, 2), np.arange(1, NY, 2)])
-    return sine[:, rows], sine @ slope @ sine, eigen
+    return sine[:, rows], (sine @ slope)[:, rows], sine @ slope @ sine, eigen
 
 
 def column_tables():
@@ -138,34 +138,60 @@
     return lax.broadcasted_iota(jnp.int32, (rows, LANES), 1)
 
 
-def edges_kernel(vec_ref, base_ref, low_x, high_x, low_y, high_y):
+def copy_kernel(vec_ref, base_ref, low_ref, high_ref, sems):
+    copies = []
+    for row, ref in enumerate((low_ref, high_ref)):
+        copies.append(
+            pltpu.make_async_copy(vec_ref.at[2, :, row], ref.at[pl.ds(0, 4)], sems.at[2 * row])
+        )
+        copies.append(
+            pltpu.make_async_copy(base_ref.at[:, row], ref.at[pl.ds(4, 4)], sems.at[2 * row + 1])
+        )
+    for copy in copies:
+        copy.start()
+    for copy in copies:
+        copy.wait()
+
+
+def edges_kernel(
+    diff_ref, low_y, high_y, eigen_ref, stream_ref, span_ref,
+    low_x, high_x, gain_ref, inverse_ref, slope_ref,
+):
     lanes = lane_ids(NZ)
     low = jnp.zeros((NZ, LANES), jnp.float32)
     high = jnp.zeros((NZ, LANES), jnp.float32)
     for field in range(8):
-        ref, part = (vec_ref.at[0], field) if field < 4 else (base_ref, field - 4)
-        for row in range(2):
-            block = ref[part, row]
+        for row, ref in enumerate((low_y, high_y)):
+            block = ref[field]
             at = 2 * field + row
             low = jnp.where(lanes == at, pltpu.roll(block, at, 1), low)
             high = jnp.where(lanes == at, pltpu.roll(block, (at + 1) % LANES, 1), high)
-            if row == 0:
-                low_y[field] = block
-            else:
-                high_y[field] = block
     low_x[...] = low
     high_x[...] = high
 
+    wall = lax.axis_index("wall_0") * 8 + lax.axis_index("wall_1")
+    line = lax.axis_index("xs_0") * 2 + lax.axis_index("xs_1")
+    tile, slot = lax.div(wall, 8), lax.rem(wall, 8)
+    stream = stream_ref[2 * tile + lax.rem(slot, 2)]
+    span = span_ref[8 * line + slot]
+    wall_eigen = eigen_ref[...]
+    inverse_ref[...] = -1.0 / (wall_eigen + (stream[0:1] + span[0:1] + SCREENING))
+    slope_ref[0:1, :] = stream[1:2]
+    slope_ref[1:2, :] = span[1:2]
+    for field in range(4):
+        shift = 1.0 / (jnp.zeros((NY, LANES), jnp.float32) + diff_ref[field])
+        gain_ref[field] = shift / (wall_eigen + shift)
+
 
 def advect_kernel(
-    vec_ref, base_ref, left_ref, right_ref, below_ref, above_ref, th_ref, tl_ref, out_ref
+    low_ref, high_ref, left_ref, right_ref, below_ref, above_ref, th_ref, tl_ref, out_ref, heat_ref
 ):
     lanes = lane_ids(NZ)
     first, last = lanes == 0, lanes == LANES - 1
     left, right = left_ref[...], right_ref[...]
 
     def value(field, row):
-        return vec_ref[0, field, row] if field < 4 else base_ref[field - 4, row]
+        return (low_ref, high_ref)[row][field]
 
     def slopes(field, row):
         x = value(field, row)
@@ -192,11 +218,40 @@
             updated = value(field, row) - ADV_STEP * advect
             if field == 1:
                 updated += BUOYANCY * value(3, row)
+            if field == 3:
+                heat_ref[row] = updated
+                continue
             modes = table_times(high_table, low_table, updated)
-            out_ref[pl.ds(2 * field + row, NZ, stride=LINES), :] = modes
-
-
-def stream_kernel(in_ref, wh_ref, wl_ref, out_ref):
+            part = 2 * field + row
+            for s in range(BLOCKS):
+                out_ref[s, LINES * part : LINES * (part + 1)] = modes[LINES * s : LINES * (s + 1)]
+
+
+def deal(x):
+    rows = x.shape[0]
+    even = lax.broadcasted_iota(jnp.int32, (rows, LANES), 0) % 2 == 0
+    front = lane_ids(rows) < 64
+    turned = pltpu.roll(x, 64, 1)
+    return jnp.where(
+        even,
+        jnp.where(front, x, pltpu.roll(turned, rows - 1, 0)),
+        jnp.where(front, turned, pltpu.roll(x, 1, 0)),
+    )
+
+
+def collect(x):
+    rows = x.shape[0]
+    even = lax.broadcasted_iota(jnp.int32, (rows, LANES), 0) % 2 == 0
+    front = lane_ids(rows) < 64
+    turned = pltpu.roll(x, 64, 1)
+    return jnp.where(
+        even,
+        jnp.where(front, x, pltpu.roll(x, rows - 1, 0)),
+        jnp.where(front, pltpu.roll(turned, 1, 0), turned),
+    )
+
+
+def stream_kernel(in_ref, heat_ref, wh_ref, wl_ref, out_ref):
     x = [in_ref[s] for s in range(BLOCKS)]
     s04, d04 = x[0] + x[4], x[0] - x[4]
     s26, d26 = x[2] + x[6], x[2] - x[6]
@@ -210,54 +265,46 @@
         (s04 - s26, s15 - s37),
         (d04 - minus, plus - d26),
     ]
-    front = lane_ids(LINES) < 64
     for group in range(4):
         joined = jnp.concatenate(parts[group], axis=1)
         modes = times_table(joined, wh_ref[group], wl_ref[group])
         for side in range(2):
             tile = 2 * group + side
-            for pair in range(4):
-                cols = slice(side * LANES, (side + 1) * LANES)
-                cos = modes[16 * pair : 16 * pair + 8, cols]
-                sin = pltpu.roll(modes[16 * pair + 8 : 16 * pair + 16, cols], 64, 1)
-                out_ref[16 * pair + 2 * tile] = jnp.where(front, cos, sin)
-                out_ref[16 * pair + 2 * tile + 1] = jnp.where(front, sin, cos)
+            dealt = deal(modes[:, side * LANES : (side + 1) * LANES])
+            for part in range(6):
+                out_ref[pl.ds(NZ * tile + part, LINES, stride=LINES), :] = dealt[
+                    LINES * part : LINES * (part + 1)
+                ]
+    for row in range(2):
+        out_ref[pl.ds(6 + row, NZ, stride=LINES), :] = heat_ref[row]
 
 
 def solve_kernel(
-    place_ref, diff_ref, in_ref, sh_ref, sl_ref, bh_ref, bl_ref, eh_ref, el_ref,
-    eigen_ref, stream_ref, span_ref, out_ref,
+    in_ref, sh_ref, sl_ref, dh_ref, dl_ref, bh_ref, bl_ref, eh_ref, el_ref,
+    gain_ref, inverse_ref, slope_ref, out_ref,
 ):
     def field_rows(field):
         return jnp.concatenate(
             [in_ref[pl.ds(2 * field + row, NZ, stride=LINES), :] for row in range(2)], axis=0
         )
 
-    fields = jnp.concatenate([field_rows(field) for field in range(4)], axis=1)
-    waves = table_times(sh_ref[...], sl_ref[...], fields)
+    fields = [field_rows(field) for field in range(4)]
+    waves = table_times(sh_ref[...], sl_ref[...], jnp.concatenate(fields, axis=1))
     u, v, w, heat = (waves[:, LANES * f : LANES * (f + 1)] for f in range(4))
-    stream = stream_ref[place_ref[0]]
-    span = span_ref[place_ref[1]]
-    column = stream[0:1] + span[0:1] + SCREENING
-    wall_eigen = eigen_ref[...]
+    rise = table_times(dh_ref[...], dl_ref[...], fields[1])
+    stream, span = slope_ref[0:1, :], slope_ref[1:2, :]
     lower = lane_ids(NY) % 64 < 32
 
     def slope_x(f):
-        return stream[1:2] * jnp.where(lower, pltpu.roll(f, LANES - 32, 1), pltpu.roll(f, 32, 1))
+        return stream * jnp.where(lower, pltpu.roll(f, LANES - 32, 1), pltpu.roll(f, 32, 1))
 
     def slope_z(f):
-        return span[1:2] * pltpu.roll(f, 64, 1)
-
-    def slope_y(f):
-        return table_times(eh_ref[...], el_ref[...], f)
-
-    divergence = slope_x(u) + slope_y(v) + slope_z(w)
-    pressure = -divergence / (wall_eigen + column)
-    corrected = (u - slope_x(pressure), v - slope_y(pressure), w - slope_z(pressure), heat)
-    scaled = []
-    for field in range(4):
-        shift = 1.0 / (jnp.zeros((NY, LANES), jnp.float32) + diff_ref[field])
-        scaled.append(corrected[field] * (shift / (wall_eigen + shift)))
+        return span * pltpu.roll(f, 64, 1)
+
+    pressure = inverse_ref[...] * (slope_x(u) + rise + slope_z(w))
+    lift = table_times(eh_ref[...], el_ref[...], pressure)
+    corrected = (u - slope_x(pressure), v - lift, w - slope_z(pressure), heat)
+    scaled = [corrected[field] * gain_ref[field] for field in range(4)]
     rows = table_times(bh_ref[...], bl_ref[...], jnp.concatenate(scaled, axis=1))
     for field in range(4):
         for row in range(2):
@@ -266,22 +313,18 @@
             ]
 
 
-def stream_back_kernel(in_ref, wh_ref, wl_ref, out_ref):
-    front = lane_ids(LINES) < 64
+def stream_back_kernel(in_ref, wh_ref, wl_ref, out_ref, heat_ref):
     parts = []
     for group in range(4):
         sides = []
         for side in range(2):
             tile = 2 * group + side
-            lines = []
-            for pair in range(4):
-                one = in_ref[16 * pair + 2 * tile]
-                two = in_ref[16 * pair + 2 * tile + 1]
-                lines.append(jnp.where(front, one, two))
-                lines.append(pltpu.roll(jnp.where(front, two, one), 64, 1))
-            sides.append(jnp.concatenate(lines, axis=0))
+            dealt = [in_ref[pl.ds(NZ * tile + part, LINES, stride=LINES), :] for part in range(6)]
+            sides.append(collect(jnp.concatenate(dealt, axis=0)))
         cells = times_table(jnp.concatenate(sides, axis=1), wh_ref[group], wl_ref[group])
         parts.append((cells[:, :LANES], cells[:, LANES:]))
+    for row in range(2):
+        heat_ref[row] = in_ref[pl.ds(6 + row, NZ, stride=LINES), :]
     (c0, c4), (c1, s1), (c2, s2), (c3, s3) = parts
     sum04, dif04 = c0 + c4, c0 - c4
     sum13, dif13 = c1 + c3, HALF * (c1 - c3)
@@ -308,13 +351,17 @@
     return total
 
 
-def cells_kernel(in_ref, vec_ref, th_ref, tl_ref, cur_ref, sums_ref):
+def cells_kernel(in_ref, heat_ref, vec_ref, th_ref, tl_ref, cur_ref, sums_ref):
     sums = [jnp.zeros((LINES, LANES), jnp.float32) for _ in range(10)]
     high_table, low_table = th_ref[...], tl_ref[...]
     for field in range(4):
         for row in range(2):
-            modes = in_ref[pl.ds(2 * field + row, NZ, stride=LINES), :]
-            cells = table_times(high_table, low_table, modes)
+            part = 2 * field + row
+            if field == 3:
+                cells = heat_ref[row]
+            else:
+                lines = [in_ref[s, LINES * part : LINES * (part + 1)] for s in range(BLOCKS)]
+                cells = table_times(high_table, low_table, jnp.concatenate(lines, axis=0))
             cur_ref[field, row] = cells
             vectors = [vec_ref[q, field, row] for q in range(3)]
             for q in range(3):
@@ -322,8 +369,8 @@
             sums[3] += folded(cells * cells)
             for at, (q, p) in enumerate(PAIRS):
                 sums[4 + at] += folded(vectors[q] * vectors[p])
-    lanes = lane_ids(LINES)
-    packed = jnp.zeros((LINES, LANES), jnp.float32)
+    lanes = lane_ids(16)
+    packed = jnp.zeros((16, LANES), jnp.float32)
     for at in range(10):
         packed = jnp.where(lanes == at, jnp.sum(sums[at]), packed)
     sums_ref[...] = packed
@@ -346,10 +393,9 @@
         twice = 1.0 if q == p else 2.0
         square = square + twice * products[q] * products[p] * values[4 + at]
     norm = jnp.sqrt(square + EPSILON)
-    hess = jnp.where(lanes == 3, norm, 0.0)
     for q in range(3):
-        hess = jnp.where(lanes == q, products[q], hess)
-    hess_ref[...] = hess
+        hess_ref[q] = jnp.sum(products[q])
+    hess_ref[3] = jnp.sum(norm)
     scale = 1.0 / norm
     for field in range(4):
         for row in range(2):
@@ -360,6 +406,8 @@
 
 
 VMEM = pl.BlockSpec(memory_space=pltpu.VMEM)
+SMALL = pltpu.CompilerParams(vmem_limit_bytes=8 * 1024 * 1024)
+LARGE = pltpu.CompilerParams(vmem_limit_bytes=54500 * 1024)
 SMEM = pl.BlockSpec(memory_space=pltpu.SMEM)
 
 
@@ -370,84 +418,95 @@
 def shards(krylov_basis, base_state, diffusivity):
     span, _, _ = spanwise_tables()
     stream, _, _ = stream_tables()
-    sine, wall_slope, wall_eigen = wall_tables()
+    sine, sine_slope, wall_slope, wall_eigen = wall_tables()
     stream_columns, span_columns = column_tables()
     eigen = np.broadcast_to(wall_eigen[:, None], (NY, LANES)).astype(np.float32)
 
-    last = pl.BlockSpec((1, 4, 2, NZ, LANES), lambda i: (2, 0, 0, 0, 0))
-    base_spec = pl.BlockSpec((4, 2, NZ, LANES), lambda i: (0, 0, 0, 0))
-    low_x, high_x, low_y, high_y = pl.pallas_call(
-        edges_kernel,
-        grid=(1,),
-        in_specs=[last, base_spec],
-        out_specs=[VMEM] * 4,
-        out_shape=[f32(NZ, LANES), f32(NZ, LANES), f32(8, NZ, LANES), f32(8, NZ, LANES)],
-        name="edges",
+    rows = f32(8, NZ, LANES)
+    low_y, high_y = pl.pallas_call(
+        copy_kernel,
+        in_specs=[pl.BlockSpec(memory_space=pltpu.HBM)] * 2,
+        out_specs=[VMEM] * 2,
+        out_shape=[rows, rows],
+        scratch_shapes=[pltpu.SemaphoreType.DMA((4,))],
+        compiler_params=LARGE,
+        name="copy",
     )(krylov_basis, base_state)
     size, walls = lax.axis_size(XS), lax.axis_size(WALL)
     above = lax.ppermute(low_y, WALL, [(i + 1, i) for i in range(walls - 1)])
     below = lax.ppermute(high_y, WALL, [(i, i + 1) for i in range(walls - 1)])
+    low_x, high_x, gain, inverse, slope = pl.pallas_call(
+        edges_kernel,
+        in_specs=[SMEM] + [VMEM] * 5,
+        out_specs=[VMEM] * 5,
+        out_shape=[
+            f32(NZ, LANES), f32(NZ, LANES), f32(4, NY, LANES), f32(NY, LANES), f32(2, LANES)
+        ],
+        compiler_params=SMALL,
+        name="edges",
+    )(diffusivity, low_y, high_y, eigen, stream_columns, span_columns)
     right = lax.ppermute(low_x, XS, [((i + 1) % size, i) for i in range(size)])
     left = lax.ppermute(high_x, XS, [(i, (i + 1) % size) for i in range(size)])
 
-    modes = pl.pallas_call(
+    modes, heat = pl.pallas_call(
         advect_kernel,
-        grid=(1,),
-        in_specs=[last, base_spec] + [VMEM] * 6,
-        out_specs=VMEM,
-        out_shape=f32(NZ * LINES, LANES),
+        in_specs=[VMEM] * 8,
+        out_specs=[VMEM] * 2,
+        out_shape=[f32(BLOCKS, 6 * LINES, LANES), f32(2, NZ, LANES)],
+        compiler_params=SMALL,
         name="advect",
-    )(krylov_basis, base_state, left, right, below, above, *split(span))
-    lines = lax.all_to_all(modes.reshape(BLOCKS, -1, LANES), XS, 0, 0, tiled=True)
+    )(low_y, high_y, left, right, below, above, *split(span))
+    lines = lax.all_to_all(modes, XS, 0, 0, tiled=True)
     spectra = pl.pallas_call(
         stream_kernel,
-        in_specs=[VMEM] * 3,
+        in_specs=[VMEM] * 4,
         out_specs=VMEM,
-        out_shape=f32(walls, LINES, LANES),
+        out_shape=f32(walls * LINES, LANES),
+        compiler_params=SMALL,
         name="stream",
-    )(lines, *split(stream))
-    columns = lax.all_to_all(spectra, WALL, 0, 0, tiled=True)
-    wall_pos, stream_pos = lax.axis_index(WALL), lax.axis_index(XS)
-    block = wall_pos % 16
-    pair = stream_pos * 4 + wall_pos // 16
-    place = jnp.stack([block, 2 * pair + block % 2])
+    )(lines, heat, *split(stream))
+    columns = lax.all_to_all(spectra.reshape(walls, LINES, LANES), WALL, 0, 0, tiled=True)
     solved = pl.pallas_call(
         solve_kernel,
-        in_specs=[SMEM, SMEM] + [VMEM] * 10,
+        in_specs=[VMEM] * 12,
         out_specs=VMEM,
-        out_shape=f32(NZ * LINES, LANES),
+        out_shape=f32(walls * LINES, LANES),
+        compiler_params=SMALL,
         name="solve",
     )(
-        place, diffusivity, columns.reshape(-1, LANES),
-        *split(sine), *split(sine.T), *split(wall_slope),
-        eigen, stream_columns, span_columns,
+        columns.reshape(-1, LANES), *split(sine), *split(sine_slope), *split(sine.T),
+        *split(wall_slope), gain, inverse, slope,
     )
     spectra = lax.all_to_all(solved.reshape(walls, LINES, LANES), WALL, 0, 0, tiled=True)
-    lines = pl.pallas_call(
+    lines, heat = pl.pallas_call(
         stream_back_kernel,
         in_specs=[VMEM] * 3,
-        out_specs=VMEM,
-        out_shape=f32(BLOCKS, NZ, LANES),
+        out_specs=[VMEM] * 2,
+        out_shape=[f32(BLOCKS, 6 * LINES, LANES), f32(2, NZ, LANES)],
+        compiler_params=SMALL,
         name="stream_back",
-    )(spectra, *split(stream.transpose(0, 2, 1)))
+    )(spectra.reshape(-1, LANES), *split(stream.transpose(0, 2, 1)))
     modes = lax.all_to_all(lines, XS, 0, 0, tiled=True)
     current, sums = pl.pallas_call(
         cells_kernel,
-        in_specs=[VMEM] * 4,
+        in_specs=[VMEM] * 5,
         out_specs=[VMEM] * 2,
-        out_shape=[f32(4, 2, NZ, LANES), f32(LINES, LANES)],
+        out_shape=[f32(4, 2, NZ, LANES), f32(16, LANES)],
+        compiler_params=SMALL,
         name="cells",
-    )(modes.reshape(-1, LANES), krylov_basis, *split(span.T))
-    sums = lax.all_to_all(sums, XS, 0, 0, tiled=True).sum(axis=0)
-    sums = lax.all_to_all(jnp.broadcast_to(sums, (walls, LANES)), WALL, 0, 0, tiled=True)
+    )(modes, heat, krylov_basis, *split(span.T))
+    sums = lax.all_to_all(sums, ("wall_0", "xs_1"), 0, 0, tiled=True).sum(axis=0)
+    sums = jnp.broadcast_to(sums, (32, LANES))
+    sums = lax.all_to_all(sums, ("wall_1", "xs_0"), 0, 0, tiled=True)
     new_vector, hessenberg = pl.pallas_call(
         residual_kernel,
         in_specs=[VMEM] * 3,
-        out_specs=[VMEM] * 2,
-        out_shape=[f32(4, 2, NZ, LANES), f32(1, LANES)],
+        out_specs=[VMEM, SMEM],
+        out_shape=[f32(4, 2, NZ, LANES), f32(4)],
+        compiler_params=SMALL,
         name="residual",
     )(sums, current, krylov_basis)
-    return new_vector, hessenberg[0, :4]
+    return new_vector, hessenberg
 
 
 def solution(mesh):

time: 133 us -> 112 us (0.84)
  blocking collectives: 72.5 us -> 91.2 us
  waiting for transfers between devices: 13.7 us -> 0.86 us
  starting transfers between devices: 24.6 us -> 12.7 us
  Pallas kernels: 16.6 us -> 5.72 us
  local copies, waits for them, and re-layouts: 2.91 us -> 0.15 us
    all_to_all x3 -> x4, blocking collectives: 39.7 us -> 61.6 us  [the longest x1 25.5 us: shards(): lax.all_to_all(spectra.reshape(walls, LINES, LANES), WALL, 0, 0, tiled=True)]
    all_to_all x1 -> x0, starting transfers between devices: 15.1 us -> none  [shards(): columns = lax.all_to_all(spectra, WALL, 0, 0, tiled=True)]
    all_to_all x1 -> x0, waiting for transfers between devices: 11.8 us -> none  [shards(): columns = lax.all_to_all(spectra, WALL, 0, 0, tiled=True)]
    pallas_call x7 -> x8, Pallas kernels: 16.6 us -> 5.72 us  [the longest x1 1.17 us: shards(): pl.pallas_call(copy_kernel, in_specs=[pl.BlockSpec(memory_space=pltpu.HBM...]
    all_to_all x1, blocking collectives: 14.2 us -> 11.5 us  [shards(): modes = lax.all_to_all(lines, XS, 0, 0, tiled=True)]
    unnamed x12 -> x42, local copies, waits for them, and re-layouts: 2.38 us -> 0.13 us
    ppermute x1, starting transfers between devices: 2.08 us -> 4.29 us  [shards(): right = lax.ppermute(low_x, XS, [((i + 1) % size, i) for i in range(size)])]
  transfers between devices with their start and end apart: 5 -> 4, of which waited for: 4 -> 2; matrix products, arithmetic and copies ran while one was open for 1% -> 0% of each run, Pallas kernels for 0% -> 1%
where the time goes in v2:
time: 112 us
  blocking collectives  91.2 us (81%)
  starting transfers between devices  12.7 us (11%)
  Pallas kernels  5.72 us (5%)
    all_to_all x1, blocking collectives, shards(): lax.all_to_all(spectra.reshape(walls, LINES, LANES), WALL, 0, 0, tiled=True)  25.5 us
    all_to_all x1, blocking collectives, shards(): lax.all_to_all(solved.reshape(walls, LINES, LANES), WALL, 0, 0, tiled=True)  18.1 us
    all_to_all x1, blocking collectives, shards(): lines = lax.all_to_all(modes, XS, 0, 0, tiled=True)  13.5 us
    all_to_all x1, blocking collectives, shards(): sums = lax.all_to_all(sums, ('wall_1', 'xs_0'), 0, 0, tiled=True)  11.8 us
    all_to_all x1, blocking collectives, shards(): modes = lax.all_to_all(lines, XS, 0, 0, tiled=True)  11.5 us
    all_to_all x1, blocking collectives, shards(): lax.all_to_all(sums, ('wall_0', 'xs_1'), 0, 0, tiled=True).sum(axis=0)  10.7 us
    ppermute x1, starting transfers between devices, shards(): below = lax.ppermute(high_y, WALL, [(i, i + 1) for i in range(walls - 1)])  4.66 us
    ppermute x1, starting transfers between devices, shards(): right = lax.ppermute(low_x, XS, [((i + 1) % size, i) for i in range(size)])  4.29 us
  transfers between devices with their start and end apart: 4, of which 2 were waited for; matrix products, arithmetic and copies ran while one was open for 0% of the time, Pallas kernels for 1%

profile of v2, /device:TPU:1, one launch (start us, length us, event | category | flops | bytes accessed | tf_op | source)
XLA Modules:
  0.0 111.6 jit_solution(10228973123733444642)
XLA Ops:
  0.6 0.0 copy-start.5
  0.6 0.0 copy-start.6
  0.7 0.0 copy-start.19
  0.7 1.2 %copy.26 = (f32[8,64,128]{2,1,0:T(8,128)S(1)}, f32[8,64,128]{2,1,0:T(8,128)S(1)}) custom-call(f32[3,4,2,64,128]{4,3,2,1,0:T(8,128)} %vec_ref.5, f32[4,2,64,128]{3,2,1,0:T(8,128)} %base_ref.1), custom_call_target="tpu_custom_call" | custom-call | tf_op jit(solution)/shard_map/copy/pallas_call | solution.py:426
  1.8 0.0 copy-start.20
  1.9 1.3 %collective-permute-start.3 = (f32[8,64,128]{2,1,0:T(8,128)S(1)}, f32[8,64,128]{2,1,0:T(8,128)S(1)}, u32[]{:S(2)}, u32[]{:S(2)}) collective-permute-start(f32[8,64,128]{2,1,0:T(8,128)S(1)} %get-tuple-element.15.low_y.low_ref), channel_id=1, source_target_pairs={{8,0},{16,8},{24,16},{32,24},{40,32},{48,40},{56,48},{64,56},{72,6... | collective-permute-start | bytes 786440 | tf_op jit(solution)/shard_map/ppermute | solution.py:436
  3.2 0.0 copy-start.17
  3.2 0.0 copy-start.18
  3.2 4.7 %collective-permute-start.2 = (f32[8,64,128]{2,1,0:T(8,128)S(1)}, f32[8,64,128]{2,1,0:T(8,128)S(1)}, u32[]{:S(2)}, u32[]{:S(2)}) collective-permute-start(f32[8,64,128]{2,1,0:T(8,128)S(1)} %get-tuple-element.16.high_y.high_ref), channel_id=1, source_target_pairs={{0,8},{8,16},{16,24},{24,32},{32,40},{40,48},{48,56},{56,64},{64,7... | collective-permute-start | bytes 786440 | tf_op jit(solution)/shard_map/ppermute | solution.py:437
  7.9 0.0 copy-done.5
  7.9 0.0 copy-done.6
  7.9 0.0 copy-done.19
  7.9 0.0 copy-done.20
  7.9 0.9 edges.1
  8.8 2.5 %collective-permute-start = (f32[64,128]{1,0:T(8,128)S(1)}, f32[64,128]{1,0:T(8,128)S(1)}, u32[]{:S(2)}, u32[]{:S(2)}) collective-permute-start(f32[64,128]{1,0:T(8,128)S(1)} %get-tuple-element.17), channel_id=1, source_target_pairs={{0,1},{1,2},{2,3},{3,4},{4,5},{5,6},{6,7},{7,0},{8,9},{9,10},{10,1... | collective-permute-start | bytes 98312 | tf_op jit(solution)/shard_map/ppermute | solution.py:449
  11.3 0.0 copy-start.1
  11.3 0.0 copy-start.2
  11.3 4.3 %collective-permute-start.1 = (f32[64,128]{1,0:T(8,128)S(1)}, f32[64,128]{1,0:T(8,128)S(1)}, u32[]{:S(2)}, u32[]{:S(2)}) collective-permute-start(f32[64,128]{1,0:T(8,128)S(1)} %get-tuple-element.18), channel_id=1, source_target_pairs={{1,0},{2,1},{3,2},{4,3},{5,4},{6,5},{7,6},{0,7},{9,8},{10,9},{11,1... | collective-permute-start | bytes 98312 | tf_op jit(solution)/shard_map/ppermute | solution.py:448
  15.6 0.7 collective-permute-done.left_ref
  16.2 0.2 collective-permute-done.1.right_ref
  16.4 0.0 collective-permute-done.3.above_ref
  16.4 0.0 collective-permute-done.2.below_ref
  16.4 0.0 copy-done.17
  16.4 0.0 copy-done.18
  16.5 0.7 advect.1
  17.2 13.5 %all_to_all.37.in_ref = f32[8,48,128]{2,1,0:T(8,128)S(1)} all-to-all(f32[8,48,128]{2,1,0:T(8,128)S(1)} %get-tuple-element.19), channel_id=1, replica_groups=mesh['wall_0'=8,'wall_1'=8,'xs_0'=4,'xs_1'=2] {'xs_0','xs_1'}, dimensions={0} | all-to-all | bytes 393216 | tf_op jit(solution)/shard_map/all_to_all | solution.py:459
  30.7 0.0 copy-done.1
  30.7 0.0 copy-done.2
  30.7 0.5 stream.1
  31.2 0.0 copy-start.7
  31.2 0.0 copy-start.8
  31.2 0.0 copy-start.9
  31.2 0.0 copy-start.10
  31.2 0.0 copy-start.11
  31.3 0.0 copy-start.12
  31.3 0.0 copy-start.13
  31.3 0.0 copy-start.14
  31.3 25.5 %all_to_all.38 = f32[64,8,128]{2,1,0:T(8,128)S(1)} all-to-all(f32[64,8,128]{2,1,0:T(8,128)S(1)} %bitcast.11), channel_id=1, replica_groups=mesh['wall_0'=8,'wall_1'=8,'xs_0'=4,'xs_1'=2] {'wall_0','wall_1'}, dimensions={0} | all-to-all | bytes 524288 | tf_op jit(solution)/shard_map/all_to_all | solution.py:468
  56.8 0.0 copy-done.7
  56.8 0.0 copy-done.8
  56.8 0.0 copy-done.9
  56.8 0.0 copy-done.10
  56.8 0.0 copy-done.11
  56.8 0.0 copy-done.12
  56.8 0.0 copy-done.13
  56.9 0.0 copy-done.14
  56.9 0.0 copy-start.4
  56.9 0.8 solve.1
  57.7 0.0 copy-start.3
  57.7 18.1 %all_to_all.39 = f32[64,8,128]{2,1,0:T(8,128)S(1)} all-to-all(f32[64,8,128]{2,1,0:T(8,128)S(1)} %bitcast.9), channel_id=1, replica_groups=mesh['wall_0'=8,'wall_1'=8,'xs_0'=4,'xs_1'=2] {'wall_0','wall_1'}, dimensions={0} | all-to-all | bytes 524288 | tf_op jit(solution)/shard_map/all_to_all | solution.py:480
  75.8 0.0 copy-done.4
  75.8 0.0 copy-done.3
  75.8 0.0 copy-start
  75.8 0.4 stream_back.1
  76.2 0.0 copy-start.15
  76.2 0.0 copy-start.16
  76.3 11.5 %all_to_all.40.in_ref = f32[8,48,128]{2,1,0:T(8,128)S(1)} all-to-all(f32[8,48,128]{2,1,0:T(8,128)S(1)} %get-tuple-element.24), channel_id=1, replica_groups=mesh['wall_0'=8,'wall_1'=8,'xs_0'=4,'xs_1'=2] {'xs_0','xs_1'}, dimensions={0} | all-to-all | bytes 393216 | tf_op jit(solution)/shard_map/all_to_all | solution.py:489
  87.8 0.0 copy-done
  87.8 0.0 copy-done.15
  87.8 0.0 copy-done.16
  87.8 0.4 cells.1
  88.2 10.7 %all_to_all.41 = f32[16,1,128]{2,1,0:T(1,128)S(1)} all-to-all(f32[16,1,128]{2,1,0:T(1,128)S(1)} %bitcast.13), channel_id=1, replica_groups=mesh['wall_0'=8,'wall_1'=8,'xs_0'=4,'xs_1'=2] {'wall_0','xs_1'}, dimensions={0} | all-to-all | bytes 16384 | tf_op jit(solution)/shard_map/all_to_all | solution.py:498
  99.0 11.8 %all_to_all.42 = f32[32,1,128]{2,1,0:T(1,128)S(1)} all-to-all(f32[32,1,128]{2,1,0:T(1,128)S(1)} %broadcast_in_dim.3), channel_id=1, replica_groups=mesh['wall_0'=8,'wall_1'=8,'xs_0'=4,'xs_1'=2] {'wall_1','xs_0'}, dimensions={0} | all-to-all | bytes 32768 | tf_op jit(solution)/shard_map/all_to_all | solution.py:500
  110.8 0.9 residual.1
  (2 shorter events, 0.0 us)
Async XLA Ops:
  0.6 7.2 %copy-start.5 = (f32[64,2,128]{2,1,0:T(2,128)S(1)}, f32[64,2,128]{2,1,0:T(2,128)}, u32[]{:S(2)}) copy-start(f32[64,2,128]{2,1,0:T(2,128)} %constant.42.clone.span_ref) | copy-start | bytes 196612
  0.6 7.2 %copy-start.6 = (f32[128,128]{1,0:T(8,128)S(1)}, f32[128,128]{1,0:T(8,128)}, u32[]{:S(2)}) copy-start(f32[128,128]{1,0:T(8,128)} %constant.40.clone.eigen_ref) | copy-start | bytes 196612
  0.7 7.2 %copy-start.19 = (f32[16,2,128]{2,1,0:T(2,128)S(1)}, f32[16,2,128]{2,1,0:T(2,128)}, u32[]{:S(2)}) copy-start(f32[16,2,128]{2,1,0:T(2,128)} %constant.41.clone.stream_ref) | copy-start | bytes 49156
  1.8 6.0 %copy-start.20 = (f32[4]{0:T(128)S(1)}, f32[4]{0:T(128)}, u32[]{:S(2)}) copy-start(f32[4]{0:T(128)} %diff_ref.1) | copy-start | bytes 52
  1.9 14.6 %collective-permute-start.3 = (f32[8,64,128]{2,1,0:T(8,128)S(1)}, f32[8,64,128]{2,1,0:T(8,128)S(1)}, u32[]{:S(2)}, u32[]{:S(2)}) collective-permute-start(f32[8,64,128]{2,1,0:T(8,128)S(1)} %get-tuple-element.15.low_y.low_ref), channel_id=1, source_target_pairs={{8,0},{16,8},{24,16},{32,24},{40,32},{48,40},{56,48},{64,56},{72,6... | collective-permute-start | bytes 786440 | tf_op jit(solution)/shard_map/ppermute | solution.py:436
  3.2 13.3 %copy-start.17 = (bf16[64,64]{1,0:T(8,128)(2,1)S(1)}, bf16[64,64]{1,0:T(8,128)(2,1)}, u32[]{:S(2)}) copy-start(bf16[64,64]{1,0:T(8,128)(2,1)} %constant.44.clone.tl_ref) | copy-start | bytes 24580
  3.2 13.3 %copy-start.18 = (bf16[64,64]{1,0:T(8,128)(2,1)S(1)}, bf16[64,64]{1,0:T(8,128)(2,1)}, u32[]{:S(2)}) copy-start(bf16[64,64]{1,0:T(8,128)(2,1)} %constant.43.clone.th_ref) | copy-start | bytes 24580
  3.2 13.3 %collective-permute-start.2 = (f32[8,64,128]{2,1,0:T(8,128)S(1)}, f32[8,64,128]{2,1,0:T(8,128)S(1)}, u32[]{:S(2)}, u32[]{:S(2)}) collective-permute-start(f32[8,64,128]{2,1,0:T(8,128)S(1)} %get-tuple-element.16.high_y.high_ref), channel_id=1, source_target_pairs={{0,8},{8,16},{16,24},{24,32},{32,40},{40,48},{48,56},{56,64},{64,7... | collective-permute-start | bytes 786440 | tf_op jit(solution)/shard_map/ppermute | solution.py:437
  8.8 7.5 %collective-permute-start = (f32[64,128]{1,0:T(8,128)S(1)}, f32[64,128]{1,0:T(8,128)S(1)}, u32[]{:S(2)}, u32[]{:S(2)}) collective-permute-start(f32[64,128]{1,0:T(8,128)S(1)} %get-tuple-element.17), channel_id=1, source_target_pairs={{0,1},{1,2},{2,3},{3,4},{4,5},{5,6},{6,7},{7,0},{8,9},{9,10},{10,1... | collective-permute-start | bytes 98312 | tf_op jit(solution)/shard_map/ppermute | solution.py:449
  11.3 19.5 %copy-start.1 = (bf16[4,256,256]{2,1,0:T(8,128)(2,1)S(1)}, bf16[4,256,256]{2,1,0:T(8,128)(2,1)}, u32[]{:S(2)}) copy-start(bf16[4,256,256]{2,1,0:T(8,128)(2,1)} %constant.46.clone.wl_ref) | copy-start | bytes 1572868
  11.3 19.5 %copy-start.2 = (bf16[4,256,256]{2,1,0:T(8,128)(2,1)S(1)}, bf16[4,256,256]{2,1,0:T(8,128)(2,1)}, u32[]{:S(2)}) copy-start(bf16[4,256,256]{2,1,0:T(8,128)(2,1)} %constant.45.clone.wh_ref) | copy-start | bytes 1572868
  11.3 5.2 %collective-permute-start.1 = (f32[64,128]{1,0:T(8,128)S(1)}, f32[64,128]{1,0:T(8,128)S(1)}, u32[]{:S(2)}, u32[]{:S(2)}) collective-permute-start(f32[64,128]{1,0:T(8,128)S(1)} %get-tuple-element.18), channel_id=1, source_target_pairs={{1,0},{2,1},{3,2},{4,3},{5,4},{6,5},{7,6},{0,7},{9,8},{10,9},{11,1... | collective-permute-start | bytes 98312 | tf_op jit(solution)/shard_map/ppermute | solution.py:448
  31.2 25.6 %copy-start.7 = (bf16[128,128]{1,0:T(8,128)(2,1)S(1)}, bf16[128,128]{1,0:T(8,128)(2,1)}, u32[]{:S(2)}) copy-start(bf16[128,128]{1,0:T(8,128)(2,1)} %constant.54.clone.el_ref) | copy-start | bytes 98308
  31.2 25.6 %copy-start.8 = (bf16[128,128]{1,0:T(8,128)(2,1)S(1)}, bf16[128,128]{1,0:T(8,128)(2,1)}, u32[]{:S(2)}) copy-start(bf16[128,128]{1,0:T(8,128)(2,1)} %constant.53.clone.eh_ref) | copy-start | bytes 98308
  31.2 25.6 %copy-start.9 = (bf16[128,128]{1,0:T(8,128)(2,1)S(1)}, bf16[128,128]{1,0:T(8,128)(2,1)}, u32[]{:S(2)}) copy-start(bf16[128,128]{1,0:T(8,128)(2,1)} %constant.52.clone.bl_ref) | copy-start | bytes 98308
  31.2 25.6 %copy-start.10 = (bf16[128,128]{1,0:T(8,128)(2,1)S(1)}, bf16[128,128]{1,0:T(8,128)(2,1)}, u32[]{:S(2)}) copy-start(bf16[128,128]{1,0:T(8,128)(2,1)} %constant.51.clone.bh_ref) | copy-start | bytes 98308
  31.2 25.6 %copy-start.11 = (bf16[128,128]{1,0:T(8,128)(2,1)S(1)}, bf16[128,128]{1,0:T(8,128)(2,1)}, u32[]{:S(2)}) copy-start(bf16[128,128]{1,0:T(8,128)(2,1)} %constant.50.clone.dl_ref) | copy-start | bytes 98308
  31.3 25.6 %copy-start.12 = (bf16[128,128]{1,0:T(8,128)(2,1)S(1)}, bf16[128,128]{1,0:T(8,128)(2,1)}, u32[]{:S(2)}) copy-start(bf16[128,128]{1,0:T(8,128)(2,1)} %constant.49.clone.dh_ref) | copy-start | bytes 98308
  31.3 25.6 %copy-start.13 = (bf16[128,128]{1,0:T(8,128)(2,1)S(1)}, bf16[128,128]{1,0:T(8,128)(2,1)}, u32[]{:S(2)}) copy-start(bf16[128,128]{1,0:T(8,128)(2,1)} %constant.48.clone.sl_ref) | copy-start | bytes 98308
  31.3 25.6 %copy-start.14 = (bf16[128,128]{1,0:T(8,128)(2,1)S(1)}, bf16[128,128]{1,0:T(8,128)(2,1)}, u32[]{:S(2)}) copy-start(bf16[128,128]{1,0:T(8,128)(2,1)} %constant.47.clone.sh_ref) | copy-start | bytes 98308
  56.9 18.9 %copy-start.4 = (bf16[4,256,256]{2,1,0:T(8,128)(2,1)S(1)}, bf16[4,256,256]{2,1,0:T(8,128)(2,1)}, u32[]{:S(2)}) copy-start(bf16[4,256,256]{2,1,0:T(8,128)(2,1)} %constant.55.clone.wh_ref) | copy-start | bytes 1572868
  57.7 18.2 %copy-start.3 = (bf16[4,256,256]{2,1,0:T(8,128)(2,1)S(1)}, bf16[4,256,256]{2,1,0:T(8,128)(2,1)}, u32[]{:S(2)}) copy-start(bf16[4,256,256]{2,1,0:T(8,128)(2,1)} %constant.56.clone.wl_ref) | copy-start | bytes 1572868
  75.8 12.0 %copy-start = (f32[3,4,2,64,128]{4,3,2,1,0:T(8,128)S(1)}, f32[3,4,2,64,128]{4,3,2,1,0:T(8,128)}, u32[]{:S(2)}) copy-start(f32[3,4,2,64,128]{4,3,2,1,0:T(8,128)} %vec_ref.5) | copy-start | bytes 2359300
  76.2 11.5 %copy-start.15 = (bf16[64,64]{1,0:T(8,128)(2,1)S(1)}, bf16[64,64]{1,0:T(8,128)(2,1)}, u32[]{:S(2)}) copy-start(bf16[64,64]{1,0:T(8,128)(2,1)} %constant.58.clone.tl_ref) | copy-start | bytes 24580
  76.2 11.5 %copy-start.16 = (bf16[64,64]{1,0:T(8,128)(2,1)S(1)}, bf16[64,64]{1,0:T(8,128)(2,1)}, u32[]{:S(2)}) copy-start(bf16[64,64]{1,0:T(8,128)(2,1)} %constant.57.clone.th_ref) | copy-start | bytes 24580

commit v3 on v2

--- a/solution.py
+++ b/solution.py
@@ -138,15 +138,18 @@
     return lax.broadcasted_iota(jnp.int32, (rows, LANES), 1)
 
 
-def copy_kernel(vec_ref, base_ref, low_ref, high_ref, sems):
+def copy_kernel(vec_ref, base_ref, first_ref, second_ref, sems):
+    core = lax.axis_index("xs_1")
     copies = []
-    for row, ref in enumerate((low_ref, high_ref)):
-        copies.append(
-            pltpu.make_async_copy(vec_ref.at[2, :, row], ref.at[pl.ds(0, 4)], sems.at[2 * row])
-        )
-        copies.append(
-            pltpu.make_async_copy(base_ref.at[:, row], ref.at[pl.ds(4, 4)], sems.at[2 * row + 1])
-        )
+    for slot, ref in enumerate((first_ref, second_ref)):
+        row = core if slot == 0 else 1 - core
+        for field in range(4):
+            copies.append((vec_ref.at[2, field, row], ref.at[field]))
+            copies.append((base_ref.at[field, row], ref.at[4 + field]))
+    copies = [
+        pltpu.make_async_copy(source, target, sems.at[at])
+        for at, (source, target) in enumerate(copies)
+    ]
     for copy in copies:
         copy.start()
     for copy in copies:
@@ -154,16 +157,16 @@
 
 
 def edges_kernel(
-    diff_ref, low_y, high_y, eigen_ref, stream_ref, span_ref,
+    diff_ref, first_ref, second_ref, eigen_ref, stream_ref, span_ref,
     low_x, high_x, gain_ref, inverse_ref, slope_ref,
 ):
     lanes = lane_ids(NZ)
     low = jnp.zeros((NZ, LANES), jnp.float32)
     high = jnp.zeros((NZ, LANES), jnp.float32)
     for field in range(8):
-        for row, ref in enumerate((low_y, high_y)):
+        for slot, ref in enumerate((first_ref, second_ref)):
             block = ref[field]
-            at = 2 * field + row
+            at = 2 * field + slot
             low = jnp.where(lanes == at, pltpu.roll(block, at, 1), low)
             high = jnp.where(lanes == at, pltpu.roll(block, (at + 1) % LANES, 1), high)
     low_x[...] = low
@@ -184,47 +187,63 @@
 
 
 def advect_kernel(
-    low_ref, high_ref, left_ref, right_ref, below_ref, above_ref, th_ref, tl_ref, out_ref, heat_ref
+    first_ref, second_ref, left_ref, right_ref, inner_ref, outer_ref, th_ref, tl_ref,
+    out_ref, heat_ref,
 ):
     lanes = lane_ids(NZ)
     first, last = lanes == 0, lanes == LANES - 1
     left, right = left_ref[...], right_ref[...]
-
-    def value(field, row):
-        return (low_ref, high_ref)[row][field]
-
-    def slopes(field, row):
-        x = value(field, row)
-        at = 2 * field + row
+    core = lax.axis_index("xs_1")
+    half = jnp.where(core == 0, 0.5, -0.5)
+
+    def value(field, slot):
+        return (first_ref, second_ref)[slot][field]
+
+    def slopes(field, slot):
+        x = value(field, slot)
+        at = 2 * field + 1 - slot
         up = jnp.where(last, pltpu.roll(right, (LANES - 1 - at) % LANES, 1), pltpu.roll(x, LANES - 1, 1))
         down = jnp.where(first, pltpu.roll(left, (LANES - at) % LANES, 1), pltpu.roll(x, 1, 1))
         along_x = (up - down) * 0.5
-        if row == 0:
-            along_y = (value(field, 1) - below_ref[field]) * 0.5
+        if slot == 0:
+            along_y = (value(field, 1) - outer_ref[field]) * half
         else:
-            along_y = (above_ref[field] - value(field, 0)) * 0.5
+            along_y = (inner_ref[field] - value(field, 0)) * half
         along_z = (pltpu.roll(x, NZ - 1, 0) - pltpu.roll(x, 1, 0)) * 0.5
         return along_x, along_y, along_z
 
     high_table, low_table = th_ref[...], tl_ref[...]
-    for row in range(2):
-        for field in range(4):
-            grad = slopes(field, row)
-            base_grad = slopes(field + 4, row)
+    for field in range(4):
+        updated = []
+        for slot in range(2):
+            grad = slopes(field, slot)
+            base_grad = slopes(field + 4, slot)
             advect = jnp.zeros((NZ, LANES), jnp.float32)
             for axis in range(3):
-                advect += value(4 + axis, row) * grad[axis]
-                advect += value(axis, row) * base_grad[axis]
-            updated = value(field, row) - ADV_STEP * advect
+                advect += value(4 + axis, slot) * grad[axis]
+                advect += value(axis, slot) * base_grad[axis]
+            result = value(field, slot) - ADV_STEP * advect
             if field == 1:
-                updated += BUOYANCY * value(3, row)
-            if field == 3:
-                heat_ref[row] = updated
-                continue
-            modes = table_times(high_table, low_table, updated)
+                result += BUOYANCY * value(3, slot)
+            updated.append(result)
+        if field == 3:
+            heat_ref[core] = updated[0]
+            heat_ref[1 - core] = updated[1]
+            continue
+        rows = jnp.concatenate(
+            [
+                jnp.where(core == 0, updated[0], updated[1]),
+                jnp.where(core == 0, updated[1], updated[0]),
+            ],
+            axis=1,
+        )
+        modes = table_times(high_table, low_table, rows)
+        for row in range(2):
             part = 2 * field + row
             for s in range(BLOCKS):
-                out_ref[s, LINES * part : LINES * (part + 1)] = modes[LINES * s : LINES * (s + 1)]
+                out_ref[s, LINES * part : LINES * (part + 1)] = modes[
+                    LINES * s : LINES * (s + 1), LANES * row : LANES * (row + 1)
+                ]
 
 
 def deal(x):
@@ -423,18 +442,20 @@
     eigen = np.broadcast_to(wall_eigen[:, None], (NY, LANES)).astype(np.float32)
 
     rows = f32(8, NZ, LANES)
-    low_y, high_y = pl.pallas_call(
+    first, second = pl.pallas_call(
         copy_kernel,
         in_specs=[pl.BlockSpec(memory_space=pltpu.HBM)] * 2,
         out_specs=[VMEM] * 2,
         out_shape=[rows, rows],
-        scratch_shapes=[pltpu.SemaphoreType.DMA((4,))],
+        scratch_shapes=[pltpu.SemaphoreType.DMA((16,))],
         compiler_params=LARGE,
         name="copy",
     )(krylov_basis, base_state)
     size, walls = lax.axis_size(XS), lax.axis_size(WALL)
-    above = lax.ppermute(low_y, WALL, [(i + 1, i) for i in range(walls - 1)])
-    below = lax.ppermute(high_y, WALL, [(i, i + 1) for i in range(walls - 1)])
+    down = [[(size * (i + 1) + s, size * i + s) for i in range(walls - 1)] for s in range(size)]
+    up = [[(b, a) for a, b in pairs] for pairs in down]
+    inner = lax.ppermute(first, WALL + XS, sum([(down, up)[s % 2][s] for s in range(size)], []))
+    outer = lax.ppermute(second, WALL + XS, sum([(up, down)[s % 2][s] for s in range(size)], []))
     low_x, high_x, gain, inverse, slope = pl.pallas_call(
         edges_kernel,
         in_specs=[SMEM] + [VMEM] * 5,
@@ -444,7 +465,7 @@
         ],
         compiler_params=SMALL,
         name="edges",
-    )(diffusivity, low_y, high_y, eigen, stream_columns, span_columns)
+    )(diffusivity, first, second, eigen, stream_columns, span_columns)
     right = lax.ppermute(low_x, XS, [((i + 1) % size, i) for i in range(size)])
     left = lax.ppermute(high_x, XS, [(i, (i + 1) % size) for i in range(size)])
 
@@ -455,7 +476,7 @@
         out_shape=[f32(BLOCKS, 6 * LINES, LANES), f32(2, NZ, LANES)],
         compiler_params=SMALL,
         name="advect",
-    )(low_y, high_y, left, right, below, above, *split(span))
+    )(first, second, left, right, inner, outer, *split(span))
     lines = lax.all_to_all(modes, XS, 0, 0, tiled=True)
     spectra = pl.pallas_call(
         stream_kernel,

time: 112 us -> 111 us (level)
  blocking collectives: 91.2 us -> 89.8 us
    all_to_all x1, blocking collectives: 25.5 us -> 24.1 us  [shards(): lax.all_to_all(spectra.reshape(walls, LINES, LANES), WALL, 0, 0, tiled=True)]
where the time goes in v3:
time: 111 us; the launch traced here: 110 us
  blocking collectives  89.8 us (81%)
  starting transfers between devices  12.7 us (11%)
  Pallas kernels  5.73 us (5%)
    all_to_all x1, blocking collectives, shards(): lax.all_to_all(spectra.reshape(walls, LINES, LANES), WALL, 0, 0, tiled=True)  24.1 us
    all_to_all x1, blocking collectives, shards(): lax.all_to_all(solved.reshape(walls, LINES, LANES), WALL, 0, 0, tiled=True)  18.1 us
    all_to_all x1, blocking collectives, shards(): lines = lax.all_to_all(modes, XS, 0, 0, tiled=True)  13.5 us
    all_to_all x1, blocking collectives, shards(): sums = lax.all_to_all(sums, ('wall_1', 'xs_0'), 0, 0, tiled=True)  11.8 us
    all_to_all x1, blocking collectives, shards(): modes = lax.all_to_all(lines, XS, 0, 0, tiled=True)  11.5 us
    all_to_all x1, blocking collectives, shards(): lax.all_to_all(sums, ('wall_0', 'xs_1'), 0, 0, tiled=True).sum(axis=0)  10.7 us
    ppermute x1, starting transfers between devices, shards(): right = lax.ppermute(low_x, XS, [((i + 1) % size, i) for i in range(size)])  4.29 us
    ppermute x1, starting transfers between devices, shards(): lax.ppermute(first, WALL + XS, sum([(down, up)[s % 2][s] for s in range(s...  4.03 us
  transfers between devices with their start and end apart: 4, of which 2 were waited for; matrix products, arithmetic and copies ran while one was open for 0% of the time, Pallas kernels for 1%

profile of v3, /device:TPU:1, one launch (start us, length us, event | category | flops | bytes accessed | tf_op | source)
XLA Modules:
  0.0 110.2 jit_solution(10140463362319193390)
XLA Ops:
  0.6 0.0 copy-start.5
  0.6 0.0 copy-start.6
  0.7 0.0 copy-start.19
  0.7 1.2 %copy.26 = (f32[8,64,128]{2,1,0:T(8,128)S(1)}, f32[8,64,128]{2,1,0:T(8,128)S(1)}) custom-call(f32[3,4,2,64,128]{4,3,2,1,0:T(8,128)} %vec_ref.5, f32[4,2,64,128]{3,2,1,0:T(8,128)} %base_ref.1), custom_call_target="tpu_custom_call" | custom-call | tf_op jit(solution)/shard_map/copy/pallas_call | solution.py:445
  1.9 0.0 copy-start.20
  1.9 4.0 %collective-permute-start.2 = (f32[8,64,128]{2,1,0:T(8,128)S(1)}, f32[8,64,128]{2,1,0:T(8,128)S(1)}, u32[]{:S(2)}, u32[]{:S(2)}) collective-permute-start(f32[8,64,128]{2,1,0:T(8,128)S(1)} %get-tuple-element.15.first_ref), channel_id=1, source_target_pairs={{8,0},{16,8},{24,16},{32,24},{40,32},{48,40},{56,48},{64,56},{72,6... | collective-permute-start | bytes 786440 | tf_op jit(solution)/shard_map/ppermute | solution.py:457
  5.9 0.0 copy-start.17
  5.9 0.0 copy-start.18
  5.9 1.3 %collective-permute-start.3 = (f32[8,64,128]{2,1,0:T(8,128)S(1)}, f32[8,64,128]{2,1,0:T(8,128)S(1)}, u32[]{:S(2)}, u32[]{:S(2)}) collective-permute-start(f32[8,64,128]{2,1,0:T(8,128)S(1)} %get-tuple-element.16.second_ref), channel_id=1, source_target_pairs={{0,8},{8,16},{16,24},{24,32},{32,40},{40,48},{48,56},{56,64},{64,7... | collective-permute-start | bytes 786440 | tf_op jit(solution)/shard_map/ppermute | solution.py:458
  7.2 0.0 copy-done.5
  7.2 0.0 copy-done.6
  7.2 0.0 copy-done.19
  7.3 0.0 copy-done.20
  7.3 0.9 edges.1
  8.2 3.1 %collective-permute-start = (f32[64,128]{1,0:T(8,128)S(1)}, f32[64,128]{1,0:T(8,128)S(1)}, u32[]{:S(2)}, u32[]{:S(2)}) collective-permute-start(f32[64,128]{1,0:T(8,128)S(1)} %get-tuple-element.17), channel_id=1, source_target_pairs={{0,1},{1,2},{2,3},{3,4},{4,5},{5,6},{6,7},{7,0},{8,9},{9,10},{10,1... | collective-permute-start | bytes 98312 | tf_op jit(solution)/shard_map/ppermute | solution.py:470
  11.3 0.0 copy-start.1
  11.3 0.0 copy-start.2
  11.3 4.3 %collective-permute-start.1 = (f32[64,128]{1,0:T(8,128)S(1)}, f32[64,128]{1,0:T(8,128)S(1)}, u32[]{:S(2)}, u32[]{:S(2)}) collective-permute-start(f32[64,128]{1,0:T(8,128)S(1)} %get-tuple-element.18), channel_id=1, source_target_pairs={{1,0},{2,1},{3,2},{4,3},{5,4},{6,5},{7,6},{0,7},{9,8},{10,9},{11,1... | collective-permute-start | bytes 98312 | tf_op jit(solution)/shard_map/ppermute | solution.py:469
  15.6 0.7 collective-permute-done.left_ref
  16.2 0.2 collective-permute-done.1.right_ref
  16.4 0.0 collective-permute-done.2.inner_ref
  16.4 0.0 collective-permute-done.3.outer_ref
  16.4 0.0 copy-done.17
  16.4 0.0 copy-done.18
  16.5 0.7 advect.1
  17.2 13.5 %all_to_all.37.in_ref = f32[8,48,128]{2,1,0:T(8,128)S(1)} all-to-all(f32[8,48,128]{2,1,0:T(8,128)S(1)} %get-tuple-element.19), channel_id=1, replica_groups=mesh['wall_0'=8,'wall_1'=8,'xs_0'=4,'xs_1'=2] {'xs_0','xs_1'}, dimensions={0} | all-to-all | bytes 393216 | tf_op jit(solution)/shard_map/all_to_all | solution.py:480
  30.7 0.0 copy-done.1
  30.7 0.0 copy-done.2
  30.7 0.5 stream.1
  31.2 0.0 copy-start.7
  31.2 0.0 copy-start.8
  31.2 0.0 copy-start.9
  31.2 0.0 copy-start.10
  31.2 0.0 copy-start.11
  31.3 0.0 copy-start.12
  31.3 0.0 copy-start.13
  31.3 0.0 copy-start.14
  31.3 24.1 %all_to_all.38 = f32[64,8,128]{2,1,0:T(8,128)S(1)} all-to-all(f32[64,8,128]{2,1,0:T(8,128)S(1)} %bitcast.11), channel_id=1, replica_groups=mesh['wall_0'=8,'wall_1'=8,'xs_0'=4,'xs_1'=2] {'wall_0','wall_1'}, dimensions={0} | all-to-all | bytes 524288 | tf_op jit(solution)/shard_map/all_to_all | solution.py:489
  55.4 0.0 copy-done.7
  55.4 0.0 copy-done.8
  55.4 0.0 copy-done.9
  55.4 0.0 copy-done.10
  55.4 0.0 copy-done.11
  55.4 0.0 copy-done.12
  55.5 0.0 copy-done.13
  55.5 0.0 copy-done.14
  55.5 0.0 copy-start.4
  55.5 0.8 solve.1
  56.3 0.0 copy-start.3
  56.3 18.1 %all_to_all.39 = f32[64,8,128]{2,1,0:T(8,128)S(1)} all-to-all(f32[64,8,128]{2,1,0:T(8,128)S(1)} %bitcast.9), channel_id=1, replica_groups=mesh['wall_0'=8,'wall_1'=8,'xs_0'=4,'xs_1'=2] {'wall_0','wall_1'}, dimensions={0} | all-to-all | bytes 524288 | tf_op jit(solution)/shard_map/all_to_all | solution.py:501
  74.4 0.0 copy-done.4
  74.4 0.0 copy-done.3
  74.4 0.0 copy-start
  74.4 0.4 stream_back.1
  74.8 0.0 copy-start.15
  74.9 0.0 copy-start.16
  74.9 11.5 %all_to_all.40.in_ref = f32[8,48,128]{2,1,0:T(8,128)S(1)} all-to-all(f32[8,48,128]{2,1,0:T(8,128)S(1)} %get-tuple-element.24), channel_id=1, replica_groups=mesh['wall_0'=8,'wall_1'=8,'xs_0'=4,'xs_1'=2] {'xs_0','xs_1'}, dimensions={0} | all-to-all | bytes 393216 | tf_op jit(solution)/shard_map/all_to_all | solution.py:510
  86.4 0.0 copy-done
  86.4 0.0 copy-done.15
  86.4 0.0 copy-done.16
  86.4 0.4 cells.1
  86.8 10.7 %all_to_all.41 = f32[16,1,128]{2,1,0:T(1,128)S(1)} all-to-all(f32[16,1,128]{2,1,0:T(1,128)S(1)} %bitcast.13), channel_id=1, replica_groups=mesh['wall_0'=8,'wall_1'=8,'xs_0'=4,'xs_1'=2] {'wall_0','xs_1'}, dimensions={0} | all-to-all | bytes 16384 | tf_op jit(solution)/shard_map/all_to_all | solution.py:519
  97.6 11.8 %all_to_all.42 = f32[32,1,128]{2,1,0:T(1,128)S(1)} all-to-all(f32[32,1,128]{2,1,0:T(1,128)S(1)} %broadcast_in_dim.3), channel_id=1, replica_groups=mesh['wall_0'=8,'wall_1'=8,'xs_0'=4,'xs_1'=2] {'wall_1','xs_0'}, dimensions={0} | all-to-all | bytes 32768 | tf_op jit(solution)/shard_map/all_to_all | solution.py:521
  109.4 0.9 residual.1
  (2 shorter events, 0.0 us)
Async XLA Ops:
  0.6 6.6 %copy-start.5 = (f32[64,2,128]{2,1,0:T(2,128)S(1)}, f32[64,2,128]{2,1,0:T(2,128)}, u32[]{:S(2)}) copy-start(f32[64,2,128]{2,1,0:T(2,128)} %constant.42.clone.span_ref) | copy-start | bytes 196612
  0.6 6.6 %copy-start.6 = (f32[128,128]{1,0:T(8,128)S(1)}, f32[128,128]{1,0:T(8,128)}, u32[]{:S(2)}) copy-start(f32[128,128]{1,0:T(8,128)} %constant.40.clone.eigen_ref) | copy-start | bytes 196612
  0.7 6.6 %copy-start.19 = (f32[16,2,128]{2,1,0:T(2,128)S(1)}, f32[16,2,128]{2,1,0:T(2,128)}, u32[]{:S(2)}) copy-start(f32[16,2,128]{2,1,0:T(2,128)} %constant.41.clone.stream_ref) | copy-start | bytes 49156
  1.9 5.4 %copy-start.20 = (f32[4]{0:T(128)S(1)}, f32[4]{0:T(128)}, u32[]{:S(2)}) copy-start(f32[4]{0:T(128)} %diff_ref.1) | copy-start | bytes 52
  1.9 14.6 %collective-permute-start.2 = (f32[8,64,128]{2,1,0:T(8,128)S(1)}, f32[8,64,128]{2,1,0:T(8,128)S(1)}, u32[]{:S(2)}, u32[]{:S(2)}) collective-permute-start(f32[8,64,128]{2,1,0:T(8,128)S(1)} %get-tuple-element.15.first_ref), channel_id=1, source_target_pairs={{8,0},{16,8},{24,16},{32,24},{40,32},{48,40},{56,48},{64,56},{72,6... | collective-permute-start | bytes 786440 | tf_op jit(solution)/shard_map/ppermute | solution.py:457
  5.9 10.5 %copy-start.17 = (bf16[64,64]{1,0:T(8,128)(2,1)S(1)}, bf16[64,64]{1,0:T(8,128)(2,1)}, u32[]{:S(2)}) copy-start(bf16[64,64]{1,0:T(8,128)(2,1)} %constant.44.clone.tl_ref) | copy-start | bytes 24580
  5.9 10.5 %copy-start.18 = (bf16[64,64]{1,0:T(8,128)(2,1)S(1)}, bf16[64,64]{1,0:T(8,128)(2,1)}, u32[]{:S(2)}) copy-start(bf16[64,64]{1,0:T(8,128)(2,1)} %constant.43.clone.th_ref) | copy-start | bytes 24580
  5.9 10.5 %collective-permute-start.3 = (f32[8,64,128]{2,1,0:T(8,128)S(1)}, f32[8,64,128]{2,1,0:T(8,128)S(1)}, u32[]{:S(2)}, u32[]{:S(2)}) collective-permute-start(f32[8,64,128]{2,1,0:T(8,128)S(1)} %get-tuple-element.16.second_ref), channel_id=1, source_target_pairs={{0,8},{8,16},{16,24},{24,32},{32,40},{40,48},{48,56},{56,64},{64,7... | collective-permute-start | bytes 786440 | tf_op jit(solution)/shard_map/ppermute | solution.py:458
  8.2 8.1 %collective-permute-start = (f32[64,128]{1,0:T(8,128)S(1)}, f32[64,128]{1,0:T(8,128)S(1)}, u32[]{:S(2)}, u32[]{:S(2)}) collective-permute-start(f32[64,128]{1,0:T(8,128)S(1)} %get-tuple-element.17), channel_id=1, source_target_pairs={{0,1},{1,2},{2,3},{3,4},{4,5},{5,6},{6,7},{7,0},{8,9},{9,10},{10,1... | collective-permute-start | bytes 98312 | tf_op jit(solution)/shard_map/ppermute | solution.py:470
  11.3 19.5 %copy-start.1 = (bf16[4,256,256]{2,1,0:T(8,128)(2,1)S(1)}, bf16[4,256,256]{2,1,0:T(8,128)(2,1)}, u32[]{:S(2)}) copy-start(bf16[4,256,256]{2,1,0:T(8,128)(2,1)} %constant.46.clone.wl_ref) | copy-start | bytes 1572868
  11.3 19.5 %copy-start.2 = (bf16[4,256,256]{2,1,0:T(8,128)(2,1)S(1)}, bf16[4,256,256]{2,1,0:T(8,128)(2,1)}, u32[]{:S(2)}) copy-start(bf16[4,256,256]{2,1,0:T(8,128)(2,1)} %constant.45.clone.wh_ref) | copy-start | bytes 1572868
  11.3 5.2 %collective-permute-start.1 = (f32[64,128]{1,0:T(8,128)S(1)}, f32[64,128]{1,0:T(8,128)S(1)}, u32[]{:S(2)}, u32[]{:S(2)}) collective-permute-start(f32[64,128]{1,0:T(8,128)S(1)} %get-tuple-element.18), channel_id=1, source_target_pairs={{1,0},{2,1},{3,2},{4,3},{5,4},{6,5},{7,6},{0,7},{9,8},{10,9},{11,1... | collective-permute-start | bytes 98312 | tf_op jit(solution)/shard_map/ppermute | solution.py:469
  31.2 24.2 %copy-start.7 = (bf16[128,128]{1,0:T(8,128)(2,1)S(1)}, bf16[128,128]{1,0:T(8,128)(2,1)}, u32[]{:S(2)}) copy-start(bf16[128,128]{1,0:T(8,128)(2,1)} %constant.54.clone.el_ref) | copy-start | bytes 98308
  31.2 24.2 %copy-start.8 = (bf16[128,128]{1,0:T(8,128)(2,1)S(1)}, bf16[128,128]{1,0:T(8,128)(2,1)}, u32[]{:S(2)}) copy-start(bf16[128,128]{1,0:T(8,128)(2,1)} %constant.53.clone.eh_ref) | copy-start | bytes 98308
  31.2 24.2 %copy-start.9 = (bf16[128,128]{1,0:T(8,128)(2,1)S(1)}, bf16[128,128]{1,0:T(8,128)(2,1)}, u32[]{:S(2)}) copy-start(bf16[128,128]{1,0:T(8,128)(2,1)} %constant.52.clone.bl_ref) | copy-start | bytes 98308
  31.2 24.2 %copy-start.10 = (bf16[128,128]{1,0:T(8,128)(2,1)S(1)}, bf16[128,128]{1,0:T(8,128)(2,1)}, u32[]{:S(2)}) copy-start(bf16[128,128]{1,0:T(8,128)(2,1)} %constant.51.clone.bh_ref) | copy-start | bytes 98308
  31.2 24.2 %copy-start.11 = (bf16[128,128]{1,0:T(8,128)(2,1)S(1)}, bf16[128,128]{1,0:T(8,128)(2,1)}, u32[]{:S(2)}) copy-start(bf16[128,128]{1,0:T(8,128)(2,1)} %constant.50.clone.dl_ref) | copy-start | bytes 98308
  31.3 24.2 %copy-start.12 = (bf16[128,128]{1,0:T(8,128)(2,1)S(1)}, bf16[128,128]{1,0:T(8,128)(2,1)}, u32[]{:S(2)}) copy-start(bf16[128,128]{1,0:T(8,128)(2,1)} %constant.49.clone.dh_ref) | copy-start | bytes 98308
  31.3 24.2 %copy-start.13 = (bf16[128,128]{1,0:T(8,128)(2,1)S(1)}, bf16[128,128]{1,0:T(8,128)(2,1)}, u32[]{:S(2)}) copy-start(bf16[128,128]{1,0:T(8,128)(2,1)} %constant.48.clone.sl_ref) | copy-start | bytes 98308
  31.3 24.2 %copy-start.14 = (bf16[128,128]{1,0:T(8,128)(2,1)S(1)}, bf16[128,128]{1,0:T(8,128)(2,1)}, u32[]{:S(2)}) copy-start(bf16[128,128]{1,0:T(8,128)(2,1)} %constant.47.clone.sh_ref) | copy-start | bytes 98308
  55.5 18.9 %copy-start.4 = (bf16[4,256,256]{2,1,0:T(8,128)(2,1)S(1)}, bf16[4,256,256]{2,1,0:T(8,128)(2,1)}, u32[]{:S(2)}) copy-start(bf16[4,256,256]{2,1,0:T(8,128)(2,1)} %constant.55.clone.wh_ref) | copy-start | bytes 1572868
  56.3 18.2 %copy-start.3 = (bf16[4,256,256]{2,1,0:T(8,128)(2,1)S(1)}, bf16[4,256,256]{2,1,0:T(8,128)(2,1)}, u32[]{:S(2)}) copy-start(bf16[4,256,256]{2,1,0:T(8,128)(2,1)} %constant.56.clone.wl_ref) | copy-start | bytes 1572868
  74.4 11.9 %copy-start = (f32[3,4,2,64,128]{4,3,2,1,0:T(8,128)S(1)}, f32[3,4,2,64,128]{4,3,2,1,0:T(8,128)}, u32[]{:S(2)}) copy-start(f32[3,4,2,64,128]{4,3,2,1,0:T(8,128)} %vec_ref.5) | copy-start | bytes 2359300
  74.8 11.5 %copy-start.15 = (bf16[64,64]{1,0:T(8,128)(2,1)S(1)}, bf16[64,64]{1,0:T(8,128)(2,1)}, u32[]{:S(2)}) copy-start(bf16[64,64]{1,0:T(8,128)(2,1)} %constant.58.clone.tl_ref) | copy-start | bytes 24580
  74.9 11.5 %copy-start.16 = (bf16[64,64]{1,0:T(8,128)(2,1)S(1)}, bf16[64,64]{1,0:T(8,128)(2,1)}, u32[]{:S(2)}) copy-start(bf16[64,64]{1,0:T(8,128)(2,1)} %constant.57.clone.th_ref) | copy-start | bytes 24580

commit v4 on v3

v4 whole, which is shorter than its diff:
```python
import math

import jax
import jax.numpy as jnp
import ml_dtypes
import numpy as np
from jax import lax
from jax.experimental import pallas as pl
from jax.experimental.pallas import tpu as pltpu
from jax.sharding import Mesh
from jax.sharding import PartitionSpec as P

WALL = ("wall_0", "wall_1")
XS = ("xs_0", "xs_1")

ADV_STEP = 0.2
BUOYANCY = 0.5
SCREENING = 0.004
EPSILON = 1e-06

NX, NY, NZ = 1024, 128, 64
LINES, LANES, BLOCKS = 8, 128, 8
ROWS = 16
HALF = math.sqrt(0.5)


def split(table):
    high = table.astype(ml_dtypes.bfloat16)
    low = (table - high.astype(np.float64)).astype(ml_dtypes.bfloat16)
    return high, low


def spanwise_tables():
    cells = np.arange(NZ)
    table = np.zeros((NZ, NZ))
    eigen = np.zeros((NZ // 2, 2))
    slope = np.zeros((NZ // 2, 2))
    for pair in range(NZ // 2):
        if pair == 0:
            table[0] = 1.0 / math.sqrt(NZ)
            table[1] = np.cos(math.pi * cells) / math.sqrt(NZ)
            eigen[0] = (0.0, 4.0)
            continue
        angle = 2.0 * math.pi * (cells * pair % NZ) / NZ
        table[2 * pair] = np.cos(angle) * math.sqrt(2.0 / NZ)
        table[2 * pair + 1] = np.sin(angle) * math.sqrt(2.0 / NZ)
        eigen[pair] = 4.0 * math.sin(math.pi * pair / NZ) ** 2
        wave = math.sin(2.0 * math.pi * pair / NZ)
        slope[pair] = (wave, -wave)
    return table, eigen, slope


def stream_tables():
    cells = np.arange(LANES)
    weights = np.zeros((4, 2 * LANES, 2 * LANES))
    eigen = np.zeros((8, 2, 64))
    slope = np.zeros((8, 2, 64))
    for tile in range(8):
        group = tile // 2
        base = (0, 4)[tile] if group == 0 else group
        first = 0 if group == 0 else 64 * (tile % 2)
        for slot in range(64):
            wave = 8 * (first + slot) + base
            at = (tile % 2) * LANES + slot
            angle = 2.0 * math.pi * (cells * wave % NX) / NX
            scale = math.sqrt(2.0 / NX)
            if wave == 0:
                alternate = np.cos(math.pi * cells)
                weights[0, :LANES, at] = 1.0 / math.sqrt(NX)
                weights[0, :LANES, at + 64] = alternate / math.sqrt(NX)
                eigen[tile, :, slot] = (0.0, 4.0)
                continue
            eigen[tile, :, slot] = 4.0 * math.sin(math.pi * wave / NX) ** 2
            rise = math.sin(2.0 * math.pi * wave / NX)
            slope[tile, :, slot] = (rise, -rise)
            cos, sin = scale * np.cos(angle), scale * np.sin(angle)
            if group == 0:
                rows = slice((tile % 2) * LANES, (tile % 2 + 1) * LANES)
                weights[0, rows, at] = cos
                weights[0, rows, at + 64] = sin
            else:
                weights[group, :LANES, at] = cos
                weights[group, LANES:, at] = -sin
                weights[group, :LANES, at + 64] = sin
                weights[group, LANES:, at + 64] = cos
    columns = np.stack([eigen.reshape(8, LANES), slope.reshape(8, LANES)])
    return weights, columns.astype(np.float32)


def block_tables():
    order = np.arange(1, ROWS + 1)
    sine = np.sin(math.pi * np.outer(order, order) / (ROWS + 1))
    sine = sine * math.sqrt(2.0 / (ROWS + 1))
    shift = np.eye(ROWS, k=1)
    slope = 0.5 * (shift - shift.T)
    eigen = 2.0 - 2.0 * np.cos(math.pi * order / (ROWS + 1))
    rows = np.concatenate([np.arange(0, ROWS, 2), np.arange(1, ROWS, 2)])
    marks = np.stack([eigen, sine[:, 0], sine[:, ROWS - 1]])
    marks = np.broadcast_to(marks[:, :, None], (3, ROWS, LANES)).astype(np.float32)
    lift = sine @ slope @ sine
    tables = np.stack([sine[:, rows], (sine @ slope)[:, rows], lift, sine[:, rows].T, lift.T])
    return np.stack(split(tables)), marks


def halves(x):
    high = x.astype(jnp.bfloat16)
    low = (x - high.astype(jnp.float32)).astype(jnp.bfloat16)
    return high, low


def dot(a, b):
    return jnp.dot(a, b, preferred_element_type=jnp.float32)


def times_table(x, high_table, low_table):
    high, low = halves(x)
    return dot(high, high_table) + (dot(low, high_table) + dot(high, low_table))


SINE, SINE_SLOPE, LIFT, SINE_BACK, LIFT_BACK = range(5)


def wall_times(ref, which, x):
    return table_times(ref[0, which], ref[1, which], x)


def table_times(high_table, low_table, x):
    high, low = halves(x)
    return dot(high_table, high) + (dot(high_table, low) + dot(low_table, high))


def lane_ids(rows):
    return lax.broadcasted_iota(jnp.int32, (rows, LANES), 1)


def copy_kernel(vec_ref, base_ref, first_ref, second_ref, sems):
    core = lax.axis_index("xs_1")
    copies = []
    for slot, ref in enumerate((first_ref, second_ref)):
        row = core if slot == 0 else 1 - core
        for field in range(4):
            copies.append((vec_ref.at[2, field, row], ref.at[field]))
            copies.append((base_ref.at[field, row], ref.at[4 + field]))
    copies = [
        pltpu.make_async_copy(source, target, sems.at[at])
        for at, (source, target) in enumerate(copies)
    ]
    for copy in copies:
        copy.start()
    for copy in copies:
        copy.wait()


def edges_kernel(
    diff_ref, first_ref, second_ref, marks_ref, stream_ref, span_ref, wall_ref,
    low_x, high_x, inverse_ref, gain_ref, share_ref, coef_ref, slope_ref, joint_ref,
):
    lanes = lane_ids(NZ)
    low = jnp.zeros((NZ, LANES), jnp.float32)
    high = jnp.zeros((NZ, LANES), jnp.float32)
    for field in range(8):
        for slot, ref in enumerate((first_ref, second_ref)):
            block = ref[field]
            at = 2 * field + slot
            low = jnp.where(lanes == at, pltpu.roll(block, at, 1), low)
            high = jnp.where(lanes == at, pltpu.roll(block, (at + 1) % LANES, 1), high)
    low_x[...] = low
    high_x[...] = high

    slot = lax.axis_index("wall_1") * 8 + lax.axis_index("xs_0") * 2 + lax.axis_index("xs_1")
    span = span_ref[slot]
    column = stream_ref[0] + (span[0:1] + SCREENING)
    slope_ref[...] = jnp.broadcast_to(span[1:2], (LINES, LANES))
    eigen, head, tail = marks_ref[0], marks_ref[1], marks_ref[2]
    shifts = [1.0 / (jnp.zeros((LINES, LANES), jnp.float32) + diff_ref[f]) for f in range(4)]
    gains = []
    for field in range(4):
        shift = jnp.concatenate([shifts[field]] * 2, axis=0)
        share = 1.0 / (eigen + shift)
        gains.append(shift * share)
        share_ref[field] = share
        gain_ref[field] = gains[field]
    head_lift = wall_times(wall_ref, LIFT_BACK, head * gains[1])
    tail_lift = wall_times(wall_ref, LIFT_BACK, tail * gains[1])
    weights = [
        gains[0] * head * head, gains[0] * head * tail,
        gains[2] * head * head, gains[2] * head * tail,
        head_lift * head, head_lift * tail, tail_lift * head, tail_lift * tail,
        head * head, head * tail,
    ]
    for tile in range(BLOCKS):
        inverse = 1.0 / (eigen + column[tile : tile + 1])
        inverse_ref[:, LANES * tile : LANES * (tile + 1)] = inverse
        for at, weight in enumerate(weights):
            coef_ref[at, tile : tile + 1] = jnp.sum(weight * inverse, axis=0, keepdims=True)
    coef_ref[10] = 0.5 * shifts[1]

    shift = jnp.concatenate([column] + shifts, axis=0)
    root = jnp.sqrt(shift * (shift + 4.0))
    decay = 2.0 / (2.0 + shift + root)
    two = decay * decay
    four = two * two
    eight = four * four
    sixteen = eight * eight
    powers = [jnp.ones_like(decay)]
    for _ in range(8):
        powers.append(powers[-1] * (sixteen * sixteen))
    joint_ref[0] = decay
    joint_ref[1] = eight * four * two * decay
    joint_ref[2] = sixteen
    joint_ref[3] = 1.0 / (root * (1.0 - powers[8] * two))
    for b in range(1, 8):
        joint_ref[4 * b] = 1.0 - powers[b]
        joint_ref[4 * b + 1] = 1.0 - powers[b] * two
        joint_ref[4 * b + 2] = 1.0 - powers[8 - b] * two
        joint_ref[4 * b + 3] = 1.0 - powers[8 - b]


def advect_kernel(
    first_ref, second_ref, left_ref, right_ref, inner_ref, outer_ref, table_ref,
    out_ref,
):
    lanes = lane_ids(NZ)
    first, last = lanes == 0, lanes == LANES - 1
    left, right = left_ref[...], right_ref[...]
    core = lax.axis_index("xs_1")
    half = jnp.where(core == 0, 0.5, -0.5)

    def value(field, slot):
        return (first_ref, second_ref)[slot][field]

    def slopes(field, slot):
        x = value(field, slot)
        at = 2 * field + 1 - slot
        up = jnp.where(last, pltpu.roll(right, (LANES - 1 - at) % LANES, 1), pltpu.roll(x, LANES - 1, 1))
        down = jnp.where(first, pltpu.roll(left, (LANES - at) % LANES, 1), pltpu.roll(x, 1, 1))
        along_x = (up - down) * 0.5
        if slot == 0:
            along_y = (value(field, 1) - outer_ref[field]) * half
        else:
            along_y = (inner_ref[field] - value(field, 0)) * half
        along_z = (pltpu.roll(x, NZ - 1, 0) - pltpu.roll(x, 1, 0)) * 0.5
        return along_x, along_y, along_z

    for field in range(4):
        updated = []
        for slot in range(2):
            grad = slopes(field, slot)
            base_grad = slopes(field + 4, slot)
            advect = jnp.zeros((NZ, LANES), jnp.float32)
            for axis in range(3):
                advect += value(4 + axis, slot) * grad[axis]
                advect += value(axis, slot) * base_grad[axis]
            result = value(field, slot) - ADV_STEP * advect
            if field == 1:
                result += BUOYANCY * value(3, slot)
            updated.append(result)
        rows = (
            jnp.where(core == 0, updated[0], updated[1]),
            jnp.where(core == 0, updated[1], updated[0]),
        )
        if field < 3:
            kind = field // 2
            modes = table_times(table_ref[0, kind], table_ref[1, kind], jnp.concatenate(rows, axis=1))
            rows = (modes[:, :LANES], modes[:, LANES:])
        for row in range(2):
            out_ref[pl.ds(2 * field + row, NZ, stride=LINES), :] = rows[row]


def lanes_of(x, tile):
    return x[:, LANES * tile : LANES * (tile + 1)]


def side_by_side(parts):
    return jnp.concatenate(parts, axis=1)


def stream_kernel(
    in_ref, table_ref, wall_ref, marks_ref, stream_ref, inverse_ref, gain_ref, coef_ref, slope_ref,
    waves_ref, pressure_ref, out_ref,
):
    def lines(part, s):
        return in_ref[pl.ds(LINES * s + part, LINES, stride=NZ), :]

    x = [jnp.concatenate([lines(part, s) for part in range(6)], axis=0) for s in range(BLOCKS)]
    s04, d04 = x[0] + x[4], x[0] - x[4]
    s26, d26 = x[2] + x[6], x[2] - x[6]
    s15, d15 = x[1] + x[5], x[1] - x[5]
    s37, d37 = x[3] + x[7], x[3] - x[7]
    even, odd = s04 + s26, s15 + s37
    minus, plus = HALF * (d15 - d37), HALF * (d15 + d37)
    parts = [
        (even + odd, even - odd),
        (d04 + minus, plus + d26),
        (s04 - s26, s15 - s37),
        (d04 - minus, plus - d26),
    ]
    modes = side_by_side(
        [times_table(side_by_side(parts[g]), table_ref[0, g], table_ref[1, g]) for g in range(4)]
    )
    heat = side_by_side(
        [jnp.concatenate([lines(6, s), lines(7, s)], axis=0) for s in range(BLOCKS)]
    )
    fields = [modes[ROWS * f : ROWS * (f + 1)] for f in range(3)] + [heat]
    waves = wall_times(wall_ref, SINE, side_by_side(fields))
    waves_ref[...] = waves
    rise = wall_times(wall_ref, SINE_SLOPE, fields[1])
    head, tail = marks_ref[1], marks_ref[2]
    span = slope_ref[0:1, :]

    def wave(field, tile):
        return lanes_of(waves, BLOCKS * field + tile)

    pressure = []
    for tile in range(BLOCKS):
        slope = stream_ref[1, tile : tile + 1]
        source = slope * pltpu.roll(wave(0, tile), 64, 1) + lanes_of(rise, tile)
        source += span * wave(2, tile)
        pressure.append(-lanes_of(inverse_ref, tile) * source)
    joined = side_by_side(pressure)
    pressure_ref[...] = joined
    lift = wall_times(wall_ref, LIFT, joined)

    def ends(f):
        return (
            jnp.sum(f * tail, axis=0, keepdims=True), jnp.sum(f * head, axis=0, keepdims=True)
        )

    for tile in range(BLOCKS):
        p = pressure[tile]
        last, first = ends(p)
        half = coef_ref[10, tile : tile + 1]
        rows = lanes_of(fields[1], tile)
        values = [(last + 0.5 * rows[ROWS - 1 :], first - 0.5 * rows[:1])]
        slope = stream_ref[1, tile : tile + 1]
        corrected = (
            wave(0, tile) - slope * pltpu.roll(p, 64, 1),
            wave(1, tile) - lanes_of(lift, tile),
            wave(2, tile) + span * p,
            wave(3, tile),
        )
        for field in range(4):
            high, low = ends(gain_ref[field] * corrected[field])
            if field == 1:
                high, low = high + half * last, low - half * first
            values.append((high, low))
        for at, (high, low) in enumerate(values):
            out_ref[0, LINES * at + tile : LINES * at + tile + 1] = high
            out_ref[0, 40 + LINES * at + tile : 40 + LINES * at + tile + 1] = low
    for b in range(1, 8):
        out_ref[b] = out_ref[0]


def joints(joint_ref, rows, highs, lows):
    def coef(at):
        return joint_ref[at, rows]

    decay, fifteen, sixteen, scale = (coef(at) for at in range(4))
    ahead, behind = [None] * 9, [None] * 9
    ahead[1] = jnp.zeros_like(decay)
    for b in range(2, 8):
        ahead[b] = sixteen * (ahead[b - 1] + coef(4 * b - 4) * lows[b - 1])
        ahead[b] += fifteen * (coef(4 * b - 3) * highs[b - 2])
    behind[7] = jnp.zeros_like(decay)
    for b in range(6, 0, -1):
        behind[b] = sixteen * (behind[b + 1] + coef(4 * b + 7) * highs[b])
        behind[b] += fifteen * (coef(4 * b + 6) * lows[b + 1])
    alpha, beta = [jnp.zeros_like(decay)], []
    for b in range(1, 8):
        left_u, right_u, left_w, right_w = (coef(4 * b + at) for at in range(4))
        before = ahead[b] + left_u * lows[b]
        after = behind[b] + right_w * highs[b - 1]
        alpha.append(highs[b - 1] + scale * (left_w * before + left_u * decay * after))
        late = right_w * highs[b - 1] + behind[b]
        beta.append(lows[b] + scale * (decay * right_w * before + right_u * late))
    beta.append(jnp.zeros_like(decay))
    return alpha, beta


def stream_back_kernel(
    in_ref, waves_ref, pressure_ref, table_ref, wall_ref, marks_ref, stream_ref, inverse_ref, gain_ref, share_ref, coef_ref, slope_ref, joint_ref,
    out_ref, alpha_ref, beta_ref,
):
    head, tail = marks_ref[1], marks_ref[2]
    span = slope_ref[0:1, :]
    alpha, beta = joints(
        joint_ref, pl.ds(0, 8), [in_ref[b, :8] for b in range(8)], [in_ref[b, 40:48] for b in range(8)]
    )
    coef = [coef_ref[at] for at in range(11)]
    slope = stream_ref[1]
    highs, lows = [], []
    for b in range(8):
        one, two = alpha[b], beta[b]
        one_x, two_x = slope * pltpu.roll(one, 64, 1), slope * pltpu.roll(two, 64, 1)
        one_z, two_z = span * one, span * two
        high = [
            -(one_x * coef[1] + two_x * coef[0]),
            coef[10] * (one * coef[9] + two * coef[8]) - (one * coef[6] + two * coef[7]),
            one_z * coef[3] + two_z * coef[2],
            jnp.zeros_like(one),
        ]
        low = [
            -(one_x * coef[0] + two_x * coef[1]),
            -coef[10] * (one * coef[8] + two * coef[9]) - (one * coef[4] + two * coef[5]),
            one_z * coef[2] + two_z * coef[3],
            jnp.zeros_like(one),
        ]
        highs.append(in_ref[b, 8:40] + jnp.concatenate(high, axis=0))
        lows.append(in_ref[b, 48:80] + jnp.concatenate(low, axis=0))
    alphas, betas = joints(joint_ref, pl.ds(8, 32), highs, lows)
    for b in range(8):
        alpha_ref[b, :8] = alpha[b]
        beta_ref[b, :8] = beta[b]
        alpha_ref[b, 8:] = alphas[b]
        beta_ref[b, 8:] = betas[b]
    own = lax.axis_index("wall_0")

    def outside(field, tile):
        at = LINES * field + tile
        return alpha_ref[own, at : at + 1] * head + beta_ref[own, at : at + 1] * tail

    def wave(field, tile):
        return lanes_of(waves_ref, BLOCKS * field + tile)

    pressure = [
        lanes_of(pressure_ref, tile) + lanes_of(inverse_ref, tile) * outside(0, tile)
        for tile in range(BLOCKS)
    ]
    lift = wall_times(wall_ref, LIFT, side_by_side(pressure))
    solved = [[], [], [], []]
    for tile in range(BLOCKS):
        p = pressure[tile]
        corrected = (
            wave(0, tile) - stream_ref[1, tile : tile + 1] * pltpu.roll(p, 64, 1),
            wave(1, tile) - lanes_of(lift, tile),
            wave(2, tile) + span * p,
            wave(3, tile),
        )
        for field in range(4):
            value = gain_ref[field] * corrected[field]
            solved[field].append(value + share_ref[field] * outside(field + 1, tile))
    rows = wall_times(wall_ref, SINE_BACK, side_by_side(sum(solved, [])))
    fields = [rows[:, NX * f : NX * (f + 1)] for f in range(4)]
    modes = jnp.concatenate(fields[:3], axis=0)
    parts = []
    for group in range(4):
        cells = times_table(
            modes[:, 2 * LANES * group : 2 * LANES * (group + 1)],
            table_ref[0, group], table_ref[1, group],
        )
        parts.append((cells[:, :LANES], cells[:, LANES:]))
    (c0, c4), (c1, s1), (c2, s2), (c3, s3) = parts
    sum04, dif04 = c0 + c4, c0 - c4
    sum13, dif13 = c1 + c3, HALF * (c1 - c3)
    plus13, minus13 = HALF * (s1 + s3), s1 - s3
    outer_a, outer_b = sum04 + c2, sum04 - c2
    inner_a, inner_b = dif04 + s2, dif04 - s2
    cells = [
        outer_a + sum13,
        inner_a + (dif13 + plus13),
        outer_b + minus13,
        inner_b + (plus13 - dif13),
        outer_a - sum13,
        inner_a - (dif13 + plus13),
        outer_b - minus13,
        inner_b - (plus13 - dif13),
    ]
    for s in range(BLOCKS):
        for part in range(8):
            if part < 6:
                value = cells[s][LINES * part : LINES * (part + 1)]
            else:
                value = lanes_of(fields[3], s)[LINES * (part - 6) : LINES * (part - 5)]
            out_ref[pl.ds(LINES * s + part, LINES, stride=NZ), :] = value


PAIRS = ((0, 0), (0, 1), (0, 2), (1, 1), (1, 2), (2, 2))


def folded(x):
    total = x[:LINES]
    for part in range(1, NZ // LINES):
        total += x[LINES * part : LINES * (part + 1)]
    return total


def cells_kernel(in_ref, vec_ref, table_ref, cur_ref, sums_ref):
    sums = [jnp.zeros((LINES, LANES), jnp.float32) for _ in range(10)]
    for field in range(4):
        for row in range(2):
            part = 2 * field + row
            cells = in_ref[pl.ds(part, NZ, stride=LINES), :]
            if field < 3:
                cells = table_times(table_ref[0, field // 2], table_ref[1, field // 2], cells)
            cur_ref[field, row] = cells
            vectors = [vec_ref[q, field, row] for q in range(3)]
            for q in range(3):
                sums[q] += folded(vectors[q] * cells)
            sums[3] += folded(cells * cells)
            for at, (q, p) in enumerate(PAIRS):
                sums[4 + at] += folded(vectors[q] * vectors[p])
    lanes = lane_ids(16)
    packed = jnp.zeros((16, LANES), jnp.float32)
    for at in range(10):
        packed = jnp.where(lanes == at, jnp.sum(sums[at]), packed)
    sums_ref[...] = packed


def residual_kernel(sums_ref, cur_ref, vec_ref, out_ref, hess_ref):
    entries = float(4 * NX * NY * NZ)
    totals = jnp.sum(sums_ref[...], axis=0, keepdims=True) * (1.0 / entries)
    lanes = lane_ids(1)

    def pick(at):
        return jnp.sum(jnp.where(lanes == at, totals, 0.0), axis=1, keepdims=True)

    values = [pick(at) for at in range(10)]
    products = values[:3]
    square = values[3]
    for q in range(3):
        square = square - 2.0 * products[q] * products[q]
    for at, (q, p) in enumerate(PAIRS):
        twice = 1.0 if q == p else 2.0
        square = square + twice * products[q] * products[p] * values[4 + at]
    norm = jnp.sqrt(square + EPSILON)
    for q in range(3):
        hess_ref[q] = jnp.sum(products[q])
    hess_ref[3] = jnp.sum(norm)
    scale = 1.0 / norm
    for field in range(4):
        for row in range(2):
            left = cur_ref[field, row]
            for q in range(3):
                left = left - products[q] * vec_ref[q, field, row]
            out_ref[field, row] = left * scale


VMEM = pl.BlockSpec(memory_space=pltpu.VMEM)
SMALL = pltpu.CompilerParams(vmem_limit_bytes=8 * 1024 * 1024)
LARGE = pltpu.CompilerParams(vmem_limit_bytes=54500 * 1024)
SMEM = pl.BlockSpec(memory_space=pltpu.SMEM)


def f32(*dims):
    return jax.ShapeDtypeStruct(dims, jnp.float32)


def shards(krylov_basis, base_state, diffusivity):
    span, span_eigen, span_slope = spanwise_tables()
    span = np.stack([span, span[np.arange(NZ) ^ 1]])
    span_columns = np.stack([span_eigen.reshape(-1), span_slope.reshape(-1)], axis=1)
    span_columns = np.broadcast_to(span_columns[:, :, None], (NZ, 2, LANES)).astype(np.float32)
    stream, stream_columns = stream_tables()
    wall, marks = block_tables()
    span, stream = np.stack(split(span)), np.stack(split(stream))

    rows = f32(8, NZ, LANES)
    first, second = pl.pallas_call(
        copy_kernel,
        in_specs=[pl.BlockSpec(memory_space=pltpu.HBM)] * 2,
        out_specs=[VMEM] * 2,
        out_shape=[rows, rows],
        scratch_shapes=[pltpu.SemaphoreType.DMA((16,))],
        compiler_params=LARGE,
        name="copy",
    )(krylov_basis, base_state)
    size, walls = lax.axis_size(XS), lax.axis_size(WALL)
    down = [[(size * (i + 1) + s, size * i + s) for i in range(walls - 1)] for s in range(size)]
    up = [[(b, a) for a, b in pairs] for pairs in down]
    inner = lax.ppermute(first, WALL + XS, sum([(down, up)[s % 2][s] for s in range(size)], []))
    outer = lax.ppermute(second, WALL + XS, sum([(up, down)[s % 2][s] for s in range(size)], []))
    low_x, high_x, inverse, gain, share, coef, slope, joint = pl.pallas_call(
        edges_kernel,
        in_specs=[SMEM] + [VMEM] * 6,
        out_specs=[VMEM] * 8,
        out_shape=[
            f32(NZ, LANES), f32(NZ, LANES), f32(ROWS, NX), f32(4, ROWS, LANES),
            f32(4, ROWS, LANES), f32(11, LINES, LANES), f32(LINES, LANES), f32(32, 40, LANES),
        ],
        compiler_params=SMALL,
        name="edges",
    )(
        diffusivity, first, second, marks, stream_columns, span_columns, wall
    )
    right = lax.ppermute(low_x, XS, [((i + 1) % size, i) for i in range(size)])
    left = lax.ppermute(high_x, XS, [(i, (i + 1) % size) for i in range(size)])

    plane = ("wall_1",) + XS
    modes = pl.pallas_call(
        advect_kernel,
        in_specs=[VMEM] * 7,
        out_specs=VMEM,
        out_shape=f32(NZ * LINES, LANES),
        compiler_params=SMALL,
        name="advect",
    )(first, second, left, right, inner, outer, span)
    lines = lax.all_to_all(modes.reshape(NZ, LINES, LANES), plane, 0, 0, tiled=True)
    waves, pressure, ends = pl.pallas_call(
        stream_kernel,
        in_specs=[VMEM] * 9,
        out_specs=[VMEM] * 3,
        out_shape=[f32(ROWS, 4 * NX), f32(ROWS, NX), f32(8, 80, LANES)],
        compiler_params=SMALL,
        name="stream",
    )(
        lines.reshape(-1, LANES), stream, wall, marks, stream_columns, inverse, gain, coef, slope
    )
    ends = lax.all_to_all(ends, "wall_0", 0, 0, tiled=True)
    lines = pl.pallas_call(
        stream_back_kernel,
        in_specs=[VMEM] * 13,
        out_specs=VMEM,
        out_shape=f32(NZ * LINES, LANES),
        scratch_shapes=[pltpu.VMEM((8, 40, LANES), jnp.float32)] * 2,
        compiler_params=SMALL,
        name="stream_back",
    )(
        ends, waves, pressure, stream.transpose(0, 1, 3, 2), wall, marks, stream_columns,
        inverse, gain, share, coef, slope, joint,
    )
    modes = lax.all_to_all(lines.reshape(NZ, LINES, LANES), plane, 0, 0, tiled=True)
    current, sums = pl.pallas_call(
        cells_kernel,
        in_specs=[VMEM] * 3,
        out_specs=[VMEM] * 2,
        out_shape=[f32(4, 2, NZ, LANES), f32(16, LANES)],
        compiler_params=SMALL,
        name="cells",
    )(modes.reshape(-1, LANES), krylov_basis, span.transpose(0, 1, 3, 2))
    sums = lax.all_to_all(sums, ("wall_0", "xs_1"), 0, 0, tiled=True).sum(axis=0)
    sums = jnp.broadcast_to(sums, (32, LANES))
    sums = lax.all_to_all(sums, ("wall_1", "xs_0"), 0, 0, tiled=True)
    new_vector, hessenberg = pl.pallas_call(
        residual_kernel,
        in_specs=[VMEM] * 3,
        out_specs=[VMEM, SMEM],
        out_shape=[f32(4, 2, NZ, LANES), f32(4)],
        compiler_params=SMALL,
        name="residual",
    )(sums, current, krylov_basis)
    return new_vector, hessenberg


def solution(mesh):
    torus = Mesh(mesh.devices.reshape(8, 8, 4, 2), ("wall_0", "wall_1", "xs_0", "xs_1"))
    return jax.shard_map(
        shards,
        mesh=torus,
        in_specs=(P(None, None, WALL, None, XS), P(None, WALL, None, XS), P()),
        out_specs=(P(None, WALL, None, XS), P()),
        check_vma=False,
    )
```

time: 111 us -> 106 us (0.955)
  blocking collectives: 89.8 us -> 85.1 us
    all_to_all x4 -> x3, blocking collectives: 67.3 us -> 62.9 us  [the longest x1 22.6 us: shards(): ends = lax.all_to_all(ends, 'wall_0', 0, 0, tiled=True)]
    pallas_call x6 -> x5, Pallas kernels: 3.68 us -> 4.09 us  [the longest x1 1.06 us: shards(): pl.pallas_call(stream_back_kernel, in_specs=[VMEM] * 13, out_specs=VMEM,...]
where the time goes in v4:
time: 106 us
  blocking collectives  85.1 us (80%)
  starting transfers between devices  12.9 us (12%)
  Pallas kernels  6.14 us (6%)
    all_to_all x1, blocking collectives, shards(): ends = lax.all_to_all(ends, 'wall_0', 0, 0, tiled=True)  22.6 us
    all_to_all x1, blocking collectives, shards(): lax.all_to_all(modes.reshape(NZ, LINES, LANES), plane, 0, 0, tiled=True)  21.7 us
    all_to_all x1, blocking collectives, shards(): lax.all_to_all(lines.reshape(NZ, LINES, LANES), plane, 0, 0, tiled=True)  18.6 us
    all_to_all x1, blocking collectives, shards(): sums = lax.all_to_all(sums, ('wall_1', 'xs_0'), 0, 0, tiled=True)  12.5 us
    all_to_all x1, blocking collectives, shards(): lax.all_to_all(sums, ('wall_0', 'xs_1'), 0, 0, tiled=True).sum(axis=0)  9.74 us
    ppermute x1, starting transfers between devices, shards(): right = lax.ppermute(low_x, XS, [((i + 1) % size, i) for i in range(size)])  4.27 us
    ppermute x1, starting transfers between devices, shards(): lax.ppermute(first, WALL + XS, sum([(down, up)[s % 2][s] for s in range(s...  4.03 us
    ppermute x1, starting transfers between devices, shards(): left = lax.ppermute(high_x, XS, [(i, (i + 1) % size) for i in range(size)])  3.13 us
  transfers between devices with their start and end apart: 4, of which 2 were waited for; matrix products, arithmetic and copies ran while one was open for 0% of the time, Pallas kernels for 1%

profile of v4, /device:TPU:1, one launch (start us, length us, event | category | flops | bytes accessed | tf_op | source)
XLA Modules:
  0.0 105.9 jit_solution(3937971626134141915)
XLA Ops:
  0.6 0.0 copy-start.3
  0.6 0.0 copy-start.4
  0.7 0.0 copy-start.8
  0.7 0.0 copy-start.5
  0.7 1.2 %copy.15 = (f32[8,64,128]{2,1,0:T(8,128)S(1)}, f32[8,64,128]{2,1,0:T(8,128)S(1)}) custom-call(f32[3,4,2,64,128]{4,3,2,1,0:T(8,128)} %vec_ref.5, f32[4,2,64,128]{3,2,1,0:T(8,128)} %base_ref.1), custom_call_target="tpu_custom_call" | custom-call | tf_op jit(solution)/shard_map/copy/pallas_call | solution.py:558
  1.9 0.0 copy-start.9
  1.9 4.0 %collective-permute-start.2 = (f32[8,64,128]{2,1,0:T(8,128)S(1)}, f32[8,64,128]{2,1,0:T(8,128)S(1)}, u32[]{:S(2)}, u32[]{:S(2)}) collective-permute-start(f32[8,64,128]{2,1,0:T(8,128)S(1)} %get-tuple-element.17.first_ref), channel_id=1, source_target_pairs={{8,0},{16,8},{24,16},{32,24},{40,32},{48,40},{56,48},{64,56},{72,6... | collective-permute-start | bytes 786440 | tf_op jit(solution)/shard_map/ppermute | solution.py:570
  5.9 0.0 copy-start.7
  5.9 1.4 %collective-permute-start.3 = (f32[8,64,128]{2,1,0:T(8,128)S(1)}, f32[8,64,128]{2,1,0:T(8,128)S(1)}, u32[]{:S(2)}, u32[]{:S(2)}) collective-permute-start(f32[8,64,128]{2,1,0:T(8,128)S(1)} %get-tuple-element.18.second_ref), channel_id=1, source_target_pairs={{0,8},{8,16},{16,24},{24,32},{32,40},{40,48},{48,56},{56,64},{64,7... | collective-permute-start | bytes 786440 | tf_op jit(solution)/shard_map/ppermute | solution.py:571
  7.4 0.0 copy-done.3
  7.4 0.0 copy-done.4
  7.4 0.0 copy-done.8
  7.4 0.0 copy-done.5
  7.4 0.0 copy-done.9
  7.4 0.9 edges.1
  8.3 0.0 copy-start.1
  8.4 3.1 %collective-permute-start = (f32[64,128]{1,0:T(8,128)S(1)}, f32[64,128]{1,0:T(8,128)S(1)}, u32[]{:S(2)}, u32[]{:S(2)}) collective-permute-start(f32[64,128]{1,0:T(8,128)S(1)} %get-tuple-element.19), channel_id=1, source_target_pairs={{0,1},{1,2},{2,3},{3,4},{4,5},{5,6},{6,7},{7,0},{8,9},{9,10},{10,1... | collective-permute-start | bytes 98312 | tf_op jit(solution)/shard_map/ppermute | solution.py:586
  11.5 4.3 %collective-permute-start.1 = (f32[64,128]{1,0:T(8,128)S(1)}, f32[64,128]{1,0:T(8,128)S(1)}, u32[]{:S(2)}, u32[]{:S(2)}) collective-permute-start(f32[64,128]{1,0:T(8,128)S(1)} %get-tuple-element.20), channel_id=1, source_target_pairs={{1,0},{2,1},{3,2},{4,3},{5,4},{6,5},{7,6},{0,7},{9,8},{10,9},{11,1... | collective-permute-start | bytes 98312 | tf_op jit(solution)/shard_map/ppermute | solution.py:585
  15.8 0.7 collective-permute-done.left_ref
  16.4 0.2 collective-permute-done.1.right_ref
  16.6 0.0 collective-permute-done.2.inner_ref
  16.6 0.0 collective-permute-done.3.outer_ref
  16.6 0.0 copy-done.7
  16.6 0.7 advect.1
  17.4 21.7 %all_to_all.32 = f32[64,8,128]{2,1,0:T(8,128)S(1)} all-to-all(f32[64,8,128]{2,1,0:T(8,128)S(1)} %bitcast.9), channel_id=1, replica_groups=mesh['wall_0'=8,'wall_1'=8,'xs_0'=4,'xs_1'=2] {'wall_1','xs_0','xs_1'}, dimensions={0} | all-to-all | bytes 524288 | tf_op jit(solution)/shard_map/all_to_all | solution.py:597
  39.1 0.0 copy-done.1
  39.1 0.0 copy-start.2
  39.1 0.9 stream.1
  40.0 22.6 %all_to_all.33.in_ref = f32[8,80,128]{2,1,0:T(8,128)S(1)} all-to-all(f32[8,80,128]{2,1,0:T(8,128)S(1)} %get-tuple-element.25), channel_id=1, replica_groups=mesh['wall_0'=8,'wall_1'=8,'xs_0'=4,'xs_1'=2] {'wall_0'}, dimensions={0} | all-to-all | bytes 655360 | tf_op jit(solution)/shard_map/all_to_all | solution.py:608
  62.6 0.0 copy-done.2
  62.6 0.0 copy-start
  62.6 1.1 %stream_back.1 = f32[512,128]{1,0:T(8,128)S(1)} custom-call(f32[8,80,128]{2,1,0:T(8,128)S(1)} %all_to_all.33.in_ref, f32[16,4096]{1,0:T(8,128)S(1)} %get-tuple-element.26.waves_ref, f32[16,1024]{1,0:T(8,128)S(1)} %get-tuple-element.27.pressure_ref, bf16[2,4,256,256]{3,2,1,0:T(8,128)(2,1)S(1)} %copy-done.2, bf16[2,5,16,16]{3,2,1,0:T(8,128)(2,1)S(1)} %copy-done.3, ...), custom_call_target="tpu_custom_call" | custom-call | tf_op jit(solution)/shard_map/stream_back/pallas_call | solution.py:609
  63.7 0.0 copy-start.6
  63.7 18.6 %all_to_all.34 = f32[64,8,128]{2,1,0:T(8,128)S(1)} all-to-all(f32[64,8,128]{2,1,0:T(8,128)S(1)} %bitcast.11), channel_id=1, replica_groups=mesh['wall_0'=8,'wall_1'=8,'xs_0'=4,'xs_1'=2] {'wall_1','xs_0','xs_1'}, dimensions={0} | all-to-all | bytes 524288 | tf_op jit(solution)/shard_map/all_to_all | solution.py:621
  82.3 0.0 copy-done
  82.3 0.0 copy-done.6
  82.3 0.4 cells.1
  82.7 9.7 %all_to_all.35 = f32[16,1,128]{2,1,0:T(1,128)S(1)} all-to-all(f32[16,1,128]{2,1,0:T(1,128)S(1)} %bitcast.13), channel_id=1, replica_groups=mesh['wall_0'=8,'wall_1'=8,'xs_0'=4,'xs_1'=2] {'wall_0','xs_1'}, dimensions={0} | all-to-all | bytes 16384 | tf_op jit(solution)/shard_map/all_to_all | solution.py:630
  92.5 12.5 %all_to_all.36 = f32[32,1,128]{2,1,0:T(1,128)S(1)} all-to-all(f32[32,1,128]{2,1,0:T(1,128)S(1)} %broadcast_in_dim.3), channel_id=1, replica_groups=mesh['wall_0'=8,'wall_1'=8,'xs_0'=4,'xs_1'=2] {'wall_1','xs_0'}, dimensions={0} | all-to-all | bytes 32768 | tf_op jit(solution)/shard_map/all_to_all | solution.py:632
  105.0 0.9 residual.1
  (2 shorter events, 0.0 us)
Async XLA Ops:
  0.6 6.7 %copy-start.3 = (bf16[2,5,16,16]{3,2,1,0:T(8,128)(2,1)S(1)}, bf16[2,5,16,16]{3,2,1,0:T(8,128)(2,1)}, u32[]{:S(2)}) copy-start(bf16[2,5,16,16]{3,2,1,0:T(8,128)(2,1)} %constant.21.clone.wall_ref) | copy-start | bytes 15364
  0.6 6.7 %copy-start.4 = (f32[3,16,128]{2,1,0:T(8,128)S(1)}, f32[3,16,128]{2,1,0:T(8,128)}, u32[]{:S(2)}) copy-start(f32[3,16,128]{2,1,0:T(8,128)} %constant.18.clone.marks_ref) | copy-start | bytes 73732
  0.7 6.7 %copy-start.8 = (f32[64,2,128]{2,1,0:T(2,128)S(1)}, f32[64,2,128]{2,1,0:T(2,128)}, u32[]{:S(2)}) copy-start(f32[64,2,128]{2,1,0:T(2,128)} %constant.20.clone.span_ref) | copy-start | bytes 196612
  0.7 6.7 %copy-start.5 = (f32[2,8,128]{2,1,0:T(8,128)S(1)}, f32[2,8,128]{2,1,0:T(8,128)}, u32[]{:S(2)}) copy-start(f32[2,8,128]{2,1,0:T(8,128)} %constant.19.clone.stream_ref) | copy-start | bytes 24580
  1.9 5.5 %copy-start.9 = (f32[4]{0:T(128)S(1)}, f32[4]{0:T(128)}, u32[]{:S(2)}) copy-start(f32[4]{0:T(128)} %diff_ref.1) | copy-start | bytes 52
  1.9 14.8 %collective-permute-start.2 = (f32[8,64,128]{2,1,0:T(8,128)S(1)}, f32[8,64,128]{2,1,0:T(8,128)S(1)}, u32[]{:S(2)}, u32[]{:S(2)}) collective-permute-start(f32[8,64,128]{2,1,0:T(8,128)S(1)} %get-tuple-element.17.first_ref), channel_id=1, source_target_pairs={{8,0},{16,8},{24,16},{32,24},{40,32},{48,40},{56,48},{64,56},{72,6... | collective-permute-start | bytes 786440 | tf_op jit(solution)/shard_map/ppermute | solution.py:570
  5.9 10.7 %copy-start.7 = (bf16[2,2,64,64]{3,2,1,0:T(8,128)(2,1)S(1)}, bf16[2,2,64,64]{3,2,1,0:T(8,128)(2,1)}, u32[]{:S(2)}) copy-start(bf16[2,2,64,64]{3,2,1,0:T(8,128)(2,1)} %constant.22.clone.table_ref) | copy-start | bytes 98308
  5.9 10.7 %collective-permute-start.3 = (f32[8,64,128]{2,1,0:T(8,128)S(1)}, f32[8,64,128]{2,1,0:T(8,128)S(1)}, u32[]{:S(2)}, u32[]{:S(2)}) collective-permute-start(f32[8,64,128]{2,1,0:T(8,128)S(1)} %get-tuple-element.18.second_ref), channel_id=1, source_target_pairs={{0,8},{8,16},{16,24},{24,32},{32,40},{40,48},{48,56},{56,64},{64,7... | collective-permute-start | bytes 786440 | tf_op jit(solution)/shard_map/ppermute | solution.py:571
  8.3 30.8 %copy-start.1 = (bf16[2,4,256,256]{3,2,1,0:T(8,128)(2,1)S(1)}, bf16[2,4,256,256]{3,2,1,0:T(8,128)(2,1)}, u32[]{:S(2)}) copy-start(bf16[2,4,256,256]{3,2,1,0:T(8,128)(2,1)} %constant.23.clone.table_ref) | copy-start | bytes 3145732
  8.4 8.1 %collective-permute-start = (f32[64,128]{1,0:T(8,128)S(1)}, f32[64,128]{1,0:T(8,128)S(1)}, u32[]{:S(2)}, u32[]{:S(2)}) collective-permute-start(f32[64,128]{1,0:T(8,128)S(1)} %get-tuple-element.19), channel_id=1, source_target_pairs={{0,1},{1,2},{2,3},{3,4},{4,5},{5,6},{6,7},{7,0},{8,9},{9,10},{10,1... | collective-permute-start | bytes 98312 | tf_op jit(solution)/shard_map/ppermute | solution.py:586
  11.5 5.1 %collective-permute-start.1 = (f32[64,128]{1,0:T(8,128)S(1)}, f32[64,128]{1,0:T(8,128)S(1)}, u32[]{:S(2)}, u32[]{:S(2)}) collective-permute-start(f32[64,128]{1,0:T(8,128)S(1)} %get-tuple-element.20), channel_id=1, source_target_pairs={{1,0},{2,1},{3,2},{4,3},{5,4},{6,5},{7,6},{0,7},{9,8},{10,9},{11,1... | collective-permute-start | bytes 98312 | tf_op jit(solution)/shard_map/ppermute | solution.py:585
  39.1 23.5 %copy-start.2 = (bf16[2,4,256,256]{3,2,1,0:T(8,128)(2,1)S(1)}, bf16[2,4,256,256]{3,2,1,0:T(8,128)(2,1)}, u32[]{:S(2)}) copy-start(bf16[2,4,256,256]{3,2,1,0:T(8,128)(2,1)} %constant.24.clone.table_ref) | copy-start | bytes 3145732
  62.6 19.7 %copy-start = (f32[3,4,2,64,128]{4,3,2,1,0:T(8,128)S(1)}, f32[3,4,2,64,128]{4,3,2,1,0:T(8,128)}, u32[]{:S(2)}) copy-start(f32[3,4,2,64,128]{4,3,2,1,0:T(8,128)} %vec_ref.5) | copy-start | bytes 2359300
  63.7 18.6 %copy-start.6 = (bf16[2,2,64,64]{3,2,1,0:T(8,128)(2,1)S(1)}, bf16[2,2,64,64]{3,2,1,0:T(8,128)(2,1)}, u32[]{:S(2)}) copy-start(bf16[2,2,64,64]{3,2,1,0:T(8,128)(2,1)} %constant.25.clone.table_ref) | copy-start | bytes 98308

commit v5 on v4

--- a/solution.py
+++ b/solution.py
@@ -195,7 +195,7 @@
             coef_ref[at, tile : tile + 1] = jnp.sum(weight * inverse, axis=0, keepdims=True)
     coef_ref[10] = 0.5 * shifts[1]
 
-    shift = jnp.concatenate([column] + shifts, axis=0)
+    shift = jnp.concatenate([column] + [part[:2] for part in shifts], axis=0)
     root = jnp.sqrt(shift * (shift + 4.0))
     decay = 2.0 / (2.0 + shift + root)
     two = decay * decay
@@ -205,15 +205,27 @@
     powers = [jnp.ones_like(decay)]
     for _ in range(8):
         powers.append(powers[-1] * (sixteen * sixteen))
-    joint_ref[0] = decay
-    joint_ref[1] = eight * four * two * decay
-    joint_ref[2] = sixteen
-    joint_ref[3] = 1.0 / (root * (1.0 - powers[8] * two))
+    scale = 1.0 / (root * (1.0 - powers[8] * two))
+    none = jnp.zeros_like(decay)
+    left_u, right_u = [none] * 9, [none] * 9
+    left_w, right_w = [none] * 9, [none] * 9
     for b in range(1, 8):
-        joint_ref[4 * b] = 1.0 - powers[b]
-        joint_ref[4 * b + 1] = 1.0 - powers[b] * two
-        joint_ref[4 * b + 2] = 1.0 - powers[8 - b] * two
-        joint_ref[4 * b + 3] = 1.0 - powers[8 - b]
+        left_u[b], right_u[b] = 1.0 - powers[b], 1.0 - powers[b] * two
+        left_w[b], right_w[b] = 1.0 - powers[8 - b] * two, 1.0 - powers[8 - b]
+    for b in range(8):
+        above = b + 1 if b < 7 else 8
+        if b > 0:
+            over_u, over_w = 1.0 / right_u[b], 1.0 / left_w[b]
+            if b < 7:
+                joint_ref[b + 1, 0] = sixteen * left_w[b + 1] * over_w
+            if b > 1:
+                joint_ref[b - 1, 1] = sixteen * right_u[b - 1] * over_u
+            joint_ref[b, 2] = decay * left_u[b] * over_u
+            joint_ref[b, 3] = decay * right_w[b] * over_w
+        joint_ref[b, 4] = 1.0 + scale * decay * left_u[above] * right_w[above]
+        joint_ref[b, 5] = scale * sixteen * left_u[b] * left_w[above]
+        joint_ref[b, 6] = 1.0 + scale * decay * left_u[b] * right_w[b]
+        joint_ref[b, 7] = scale * sixteen * right_u[b] * right_w[above]
 
 
 def advect_kernel(
@@ -276,8 +288,8 @@
 
 
 def stream_kernel(
-    in_ref, table_ref, wall_ref, marks_ref, stream_ref, inverse_ref, gain_ref, coef_ref, slope_ref,
-    waves_ref, pressure_ref, out_ref,
+    in_ref, table_ref, wall_ref, marks_ref, stream_ref, inverse_ref, gain_ref, coef_ref, slope_ref, joint_ref,
+    waves_ref, pressure_ref, out_ref, local_ref, ends_ref,
 ):
     def lines(part, s):
         return in_ref[pl.ds(LINES * s + part, LINES, stride=NZ), :]
@@ -345,50 +357,53 @@
                 high, low = high + half * last, low - half * first
             values.append((high, low))
         for at, (high, low) in enumerate(values):
-            out_ref[0, LINES * at + tile : LINES * at + tile + 1] = high
-            out_ref[0, 40 + LINES * at + tile : 40 + LINES * at + tile + 1] = low
-    for b in range(1, 8):
-        out_ref[b] = out_ref[0]
-
-
-def joints(joint_ref, rows, highs, lows):
-    def coef(at):
-        return joint_ref[at, rows]
-
-    decay, fifteen, sixteen, scale = (coef(at) for at in range(4))
-    ahead, behind = [None] * 9, [None] * 9
-    ahead[1] = jnp.zeros_like(decay)
+            ends_ref[0, LINES * at + tile : LINES * at + tile + 1] = high
+            ends_ref[1, LINES * at + tile : LINES * at + tile + 1] = low
+    own = lax.axis_index("wall_0")
+    high, low = ends_ref[0], ends_ref[1]
+    coefs = [joint_ref[own, at] for at in range(4, 8)]
+    for system in range(5):
+        part = slice(LINES * system, LINES * (system + 1))
+        rows = slice(0, LINES) if system == 0 else slice(2 * system + 6, 2 * system + 7)
+        up, down = high[part], low[part]
+        upward = coefs[0][rows] * up + coefs[1][rows] * down
+        downward = coefs[2][rows] * down + coefs[3][rows] * up
+        if system > 0:
+            local_ref[0, system - 1] = upward
+            local_ref[1, system - 1] = downward
+        for b in range(8):
+            if system == 0:
+                out_ref[b, 0] = upward
+                out_ref[b, 1] = downward
+            else:
+                out_ref[b, system + 1] = jnp.where(own < b, upward, downward)
+
+
+def joints(joint_ref, rows, upward, downward):
+    rise, fall = [None, upward[0]], [None] * 7 + [downward[7]]
     for b in range(2, 8):
-        ahead[b] = sixteen * (ahead[b - 1] + coef(4 * b - 4) * lows[b - 1])
-        ahead[b] += fifteen * (coef(4 * b - 3) * highs[b - 2])
-    behind[7] = jnp.zeros_like(decay)
+        rise.append(upward[b - 1] + joint_ref[b, 0, rows] * rise[b - 1])
     for b in range(6, 0, -1):
-        behind[b] = sixteen * (behind[b + 1] + coef(4 * b + 7) * highs[b])
-        behind[b] += fifteen * (coef(4 * b + 6) * lows[b + 1])
-    alpha, beta = [jnp.zeros_like(decay)], []
-    for b in range(1, 8):
-        left_u, right_u, left_w, right_w = (coef(4 * b + at) for at in range(4))
-        before = ahead[b] + left_u * lows[b]
-        after = behind[b] + right_w * highs[b - 1]
-        alpha.append(highs[b - 1] + scale * (left_w * before + left_u * decay * after))
-        late = right_w * highs[b - 1] + behind[b]
-        beta.append(lows[b] + scale * (decay * right_w * before + right_u * late))
-    beta.append(jnp.zeros_like(decay))
+        fall[b] = downward[b] + joint_ref[b, 1, rows] * fall[b + 1]
+    none = jnp.zeros_like(upward[0])
+    alpha = [none] + [rise[b] + joint_ref[b, 2, rows] * fall[b] for b in range(1, 8)]
+    beta = [fall[b] + joint_ref[b, 3, rows] * rise[b] for b in range(1, 8)] + [none]
     return alpha, beta
 
 
 def stream_back_kernel(
-    in_ref, waves_ref, pressure_ref, table_ref, wall_ref, marks_ref, stream_ref, inverse_ref, gain_ref, share_ref, coef_ref, slope_ref, joint_ref,
+    in_ref, local_ref, waves_ref, pressure_ref, table_ref, wall_ref, marks_ref, stream_ref, inverse_ref, gain_ref, share_ref, coef_ref, slope_ref, joint_ref,
     out_ref, alpha_ref, beta_ref,
 ):
     head, tail = marks_ref[1], marks_ref[2]
     span = slope_ref[0:1, :]
     alpha, beta = joints(
-        joint_ref, pl.ds(0, 8), [in_ref[b, :8] for b in range(8)], [in_ref[b, 40:48] for b in range(8)]
+        joint_ref, pl.ds(0, 8), [in_ref[b, 0] for b in range(8)], [in_ref[b, 1] for b in range(8)]
     )
+    own = lax.axis_index("wall_0")
     coef = [coef_ref[at] for at in range(11)]
     slope = stream_ref[1]
-    highs, lows = [], []
+    upward, downward = [[], [], [], []], [[], [], [], []]
     for b in range(8):
         one, two = alpha[b], beta[b]
         one_x, two_x = slope * pltpu.roll(one, 64, 1), slope * pltpu.roll(two, 64, 1)
@@ -397,23 +412,34 @@
             -(one_x * coef[1] + two_x * coef[0]),
             coef[10] * (one * coef[9] + two * coef[8]) - (one * coef[6] + two * coef[7]),
             one_z * coef[3] + two_z * coef[2],
-            jnp.zeros_like(one),
         ]
         low = [
             -(one_x * coef[0] + two_x * coef[1]),
             -coef[10] * (one * coef[8] + two * coef[9]) - (one * coef[4] + two * coef[5]),
             one_z * coef[2] + two_z * coef[3],
-            jnp.zeros_like(one),
         ]
-        highs.append(in_ref[b, 8:40] + jnp.concatenate(high, axis=0))
-        lows.append(in_ref[b, 48:80] + jnp.concatenate(low, axis=0))
-    alphas, betas = joints(joint_ref, pl.ds(8, 32), highs, lows)
+        for field in range(4):
+            up, down = local_ref[0, field], local_ref[1, field]
+            up = jnp.where(own == b, up, in_ref[b, field + 2])
+            down = jnp.where(own == b, down, in_ref[b, field + 2])
+            if field < 3:
+                coefs = [joint_ref[b, at, pl.ds(8 + 2 * field, 1)] for at in range(4, 8)]
+                up += coefs[0] * high[field] + coefs[1] * low[field]
+                down += coefs[2] * low[field] + coefs[3] * high[field]
+            upward[field].append(up)
+            downward[field].append(down)
+    pairs = [
+        joints(joint_ref, pl.ds(8 + 2 * field, 1), upward[field], downward[field])
+        for field in range(4)
+    ]
+    for b in range(8):
+        for field in range(4):
+            rows = slice(LINES * (field + 1), LINES * (field + 2))
+            alpha_ref[b, rows] = pairs[field][0][b]
+            beta_ref[b, rows] = pairs[field][1][b]
     for b in range(8):
         alpha_ref[b, :8] = alpha[b]
         beta_ref[b, :8] = beta[b]
-        alpha_ref[b, 8:] = alphas[b]
-        beta_ref[b, 8:] = betas[b]
-    own = lax.axis_index("wall_0")
 
     def outside(field, tile):
         at = LINES * field + tile
@@ -575,7 +601,7 @@
         out_specs=[VMEM] * 8,
         out_shape=[
             f32(NZ, LANES), f32(NZ, LANES), f32(ROWS, NX), f32(4, ROWS, LANES),
-            f32(4, ROWS, LANES), f32(11, LINES, LANES), f32(LINES, LANES), f32(32, 40, LANES),
+            f32(4, ROWS, LANES), f32(11, LINES, LANES), f32(LINES, LANES), f32(8, 8, ROWS, LANES),
         ],
         compiler_params=SMALL,
         name="edges",
@@ -595,27 +621,31 @@
         name="advect",
     )(first, second, left, right, inner, outer, span)
     lines = lax.all_to_all(modes.reshape(NZ, LINES, LANES), plane, 0, 0, tiled=True)
-    waves, pressure, ends = pl.pallas_call(
+    waves, pressure, ends, local = pl.pallas_call(
         stream_kernel,
-        in_specs=[VMEM] * 9,
-        out_specs=[VMEM] * 3,
-        out_shape=[f32(ROWS, 4 * NX), f32(ROWS, NX), f32(8, 80, LANES)],
+        in_specs=[VMEM] * 10,
+        out_specs=[VMEM] * 4,
+        out_shape=[
+            f32(ROWS, 4 * NX), f32(ROWS, NX), f32(8, 6, LINES, LANES), f32(2, 4, LINES, LANES)
+        ],
+        scratch_shapes=[pltpu.VMEM((2, 40, LANES), jnp.float32)],
         compiler_params=SMALL,
         name="stream",
     )(
-        lines.reshape(-1, LANES), stream, wall, marks, stream_columns, inverse, gain, coef, slope
+        lines.reshape(-1, LANES), stream, wall, marks, stream_columns, inverse, gain, coef, slope,
+        joint,
     )
     ends = lax.all_to_all(ends, "wall_0", 0, 0, tiled=True)
     lines = pl.pallas_call(
         stream_back_kernel,
-        in_specs=[VMEM] * 13,
+        in_specs=[VMEM] * 14,
         out_specs=VMEM,
         out_shape=f32(NZ * LINES, LANES),
         scratch_shapes=[pltpu.VMEM((8, 40, LANES), jnp.float32)] * 2,
         compiler_params=SMALL,
         name="stream_back",
     )(
-        ends, waves, pressure, stream.transpose(0, 1, 3, 2), wall, marks, stream_columns,
+        ends, local, waves, pressure, stream.transpose(0, 1, 3, 2), wall, marks, stream_columns,
         inverse, gain, share, coef, slope, joint,
     )
     modes = lax.all_to_all(lines.reshape(NZ, LINES, LANES), plane, 0, 0, tiled=True)

time: 106 us -> 103 us (0.972)
  blocking collectives: 85.1 us -> 82.3 us
    all_to_all x1, blocking collectives: 22.6 us -> 19.4 us  [shards(): ends = lax.all_to_all(ends, 'wall_0', 0, 0, tiled=True)]
where the time goes in v5:
time: 103 us
  blocking collectives  82.3 us (80%)
  starting transfers between devices  12.9 us (13%)
  Pallas kernels  6.08 us (6%)
    all_to_all x1, blocking collectives, shards(): lax.all_to_all(modes.reshape(NZ, LINES, LANES), plane, 0, 0, tiled=True)  21.7 us
    all_to_all x1, blocking collectives, shards(): ends = lax.all_to_all(ends, 'wall_0', 0, 0, tiled=True)  19.4 us
    all_to_all x1, blocking collectives, shards(): lax.all_to_all(lines.reshape(NZ, LINES, LANES), plane, 0, 0, tiled=True)  19 us
    all_to_all x1, blocking collectives, shards(): sums = lax.all_to_all(sums, ('wall_1', 'xs_0'), 0, 0, tiled=True)  12.5 us
    all_to_all x1, blocking collectives, shards(): lax.all_to_all(sums, ('wall_0', 'xs_1'), 0, 0, tiled=True).sum(axis=0)  9.74 us
    ppermute x1, starting transfers between devices, shards(): right = lax.ppermute(low_x, XS, [((i + 1) % size, i) for i in range(size)])  4.27 us
    ppermute x1, starting transfers between devices, shards(): lax.ppermute(first, WALL + XS, sum([(down, up)[s % 2][s] for s in range(s...  4.03 us
    ppermute x1, starting transfers between devices, shards(): left = lax.ppermute(high_x, XS, [(i, (i + 1) % size) for i in range(size)])  3.13 us
  transfers between devices with their start and end apart: 4, of which 2 were waited for; matrix products, arithmetic and copies ran while one was open for 0% of the time, Pallas kernels for 1%

profile of v5, /device:TPU:1, one launch (start us, length us, event | category | flops | bytes accessed | tf_op | source)
XLA Modules:
  0.0 103.0 jit_solution(5845817144658111989)
XLA Ops:
  0.6 0.0 copy-start.3
  0.6 0.0 copy-start.4
  0.7 0.0 copy-start.8
  0.7 0.0 copy-start.5
  0.7 1.2 %copy.15 = (f32[8,64,128]{2,1,0:T(8,128)S(1)}, f32[8,64,128]{2,1,0:T(8,128)S(1)}) custom-call(f32[3,4,2,64,128]{4,3,2,1,0:T(8,128)} %vec_ref.5, f32[4,2,64,128]{3,2,1,0:T(8,128)} %base_ref.1), custom_call_target="tpu_custom_call" | custom-call | tf_op jit(solution)/shard_map/copy/pallas_call | solution.py:584
  1.9 0.0 copy-start.9
  1.9 4.0 %collective-permute-start.2 = (f32[8,64,128]{2,1,0:T(8,128)S(1)}, f32[8,64,128]{2,1,0:T(8,128)S(1)}, u32[]{:S(2)}, u32[]{:S(2)}) collective-permute-start(f32[8,64,128]{2,1,0:T(8,128)S(1)} %get-tuple-element.18.first_ref), channel_id=1, source_target_pairs={{8,0},{16,8},{24,16},{32,24},{40,32},{48,40},{56,48},{64,56},{72,6... | collective-permute-start | bytes 786440 | tf_op jit(solution)/shard_map/ppermute | solution.py:596
  5.9 0.0 copy-start.7
  5.9 1.4 %collective-permute-start.3 = (f32[8,64,128]{2,1,0:T(8,128)S(1)}, f32[8,64,128]{2,1,0:T(8,128)S(1)}, u32[]{:S(2)}, u32[]{:S(2)}) collective-permute-start(f32[8,64,128]{2,1,0:T(8,128)S(1)} %get-tuple-element.19.second_ref), channel_id=1, source_target_pairs={{0,8},{8,16},{16,24},{24,32},{32,40},{40,48},{48,56},{56,64},{64,7... | collective-permute-start | bytes 786440 | tf_op jit(solution)/shard_map/ppermute | solution.py:597
  7.4 0.0 copy-done.3
  7.4 0.0 copy-done.4
  7.4 0.0 copy-done.8
  7.4 0.0 copy-done.5
  7.4 0.0 copy-done.9
  7.4 0.9 edges.1
  8.3 0.0 copy-start.2
  8.4 3.1 %collective-permute-start = (f32[64,128]{1,0:T(8,128)S(1)}, f32[64,128]{1,0:T(8,128)S(1)}, u32[]{:S(2)}, u32[]{:S(2)}) collective-permute-start(f32[64,128]{1,0:T(8,128)S(1)} %get-tuple-element.20), channel_id=1, source_target_pairs={{0,1},{1,2},{2,3},{3,4},{4,5},{5,6},{6,7},{7,0},{8,9},{9,10},{10,1... | collective-permute-start | bytes 98312 | tf_op jit(solution)/shard_map/ppermute | solution.py:612
  11.5 4.3 %collective-permute-start.1 = (f32[64,128]{1,0:T(8,128)S(1)}, f32[64,128]{1,0:T(8,128)S(1)}, u32[]{:S(2)}, u32[]{:S(2)}) collective-permute-start(f32[64,128]{1,0:T(8,128)S(1)} %get-tuple-element.21), channel_id=1, source_target_pairs={{1,0},{2,1},{3,2},{4,3},{5,4},{6,5},{7,6},{0,7},{9,8},{10,9},{11,1... | collective-permute-start | bytes 98312 | tf_op jit(solution)/shard_map/ppermute | solution.py:611
  15.8 0.7 collective-permute-done.left_ref
  16.4 0.2 collective-permute-done.1.right_ref
  16.6 0.0 collective-permute-done.2.inner_ref
  16.6 0.0 collective-permute-done.3.outer_ref
  16.6 0.0 copy-done.7
  16.6 0.7 advect.1
  17.4 21.7 %all_to_all.32 = f32[64,8,128]{2,1,0:T(8,128)S(1)} all-to-all(f32[64,8,128]{2,1,0:T(8,128)S(1)} %bitcast.10), channel_id=1, replica_groups=mesh['wall_0'=8,'wall_1'=8,'xs_0'=4,'xs_1'=2] {'wall_1','xs_0','xs_1'}, dimensions={0} | all-to-all | bytes 524288 | tf_op jit(solution)/shard_map/all_to_all | solution.py:623
  39.1 0.0 copy-done.2
  39.1 0.0 copy-start.1
  39.1 0.9 stream.1
  40.0 19.4 %all_to_all.33.in_ref = f32[8,6,8,128]{3,2,1,0:T(8,128)S(1)} all-to-all(f32[8,6,8,128]{3,2,1,0:T(8,128)S(1)} %get-tuple-element.27), channel_id=1, replica_groups=mesh['wall_0'=8,'wall_1'=8,'xs_0'=4,'xs_1'=2] {'wall_0'}, dimensions={0} | all-to-all | bytes 393216 | tf_op jit(solution)/shard_map/all_to_all | solution.py:638
  59.4 0.0 copy-done.1
  59.4 0.0 copy-start
  59.4 1.0 stream_back.1
  60.5 0.0 copy-start.6
  60.5 19.0 %all_to_all.34 = f32[64,8,128]{2,1,0:T(8,128)S(1)} all-to-all(f32[64,8,128]{2,1,0:T(8,128)S(1)} %bitcast.8), channel_id=1, replica_groups=mesh['wall_0'=8,'wall_1'=8,'xs_0'=4,'xs_1'=2] {'wall_1','xs_0','xs_1'}, dimensions={0} | all-to-all | bytes 524288 | tf_op jit(solution)/shard_map/all_to_all | solution.py:651
  79.4 0.0 copy-done
  79.4 0.0 copy-done.6
  79.4 0.4 cells.1
  79.9 9.7 %all_to_all.35 = f32[16,1,128]{2,1,0:T(1,128)S(1)} all-to-all(f32[16,1,128]{2,1,0:T(1,128)S(1)} %bitcast.13), channel_id=1, replica_groups=mesh['wall_0'=8,'wall_1'=8,'xs_0'=4,'xs_1'=2] {'wall_0','xs_1'}, dimensions={0} | all-to-all | bytes 16384 | tf_op jit(solution)/shard_map/all_to_all | solution.py:660
  89.7 12.5 %all_to_all.36 = f32[32,1,128]{2,1,0:T(1,128)S(1)} all-to-all(f32[32,1,128]{2,1,0:T(1,128)S(1)} %broadcast_in_dim.3), channel_id=1, replica_groups=mesh['wall_0'=8,'wall_1'=8,'xs_0'=4,'xs_1'=2] {'wall_1','xs_0'}, dimensions={0} | all-to-all | bytes 32768 | tf_op jit(solution)/shard_map/all_to_all | solution.py:662
  102.1 0.9 residual.1
  (2 shorter events, 0.0 us)
Async XLA Ops:
  0.6 6.7 %copy-start.3 = (bf16[2,5,16,16]{3,2,1,0:T(8,128)(2,1)S(1)}, bf16[2,5,16,16]{3,2,1,0:T(8,128)(2,1)}, u32[]{:S(2)}) copy-start(bf16[2,5,16,16]{3,2,1,0:T(8,128)(2,1)} %constant.21.clone.wall_ref) | copy-start | bytes 15364
  0.6 6.7 %copy-start.4 = (f32[3,16,128]{2,1,0:T(8,128)S(1)}, f32[3,16,128]{2,1,0:T(8,128)}, u32[]{:S(2)}) copy-start(f32[3,16,128]{2,1,0:T(8,128)} %constant.18.clone.marks_ref) | copy-start | bytes 73732
  0.7 6.7 %copy-start.8 = (f32[64,2,128]{2,1,0:T(2,128)S(1)}, f32[64,2,128]{2,1,0:T(2,128)}, u32[]{:S(2)}) copy-start(f32[64,2,128]{2,1,0:T(2,128)} %constant.20.clone.span_ref) | copy-start | bytes 196612
  0.7 6.7 %copy-start.5 = (f32[2,8,128]{2,1,0:T(8,128)S(1)}, f32[2,8,128]{2,1,0:T(8,128)}, u32[]{:S(2)}) copy-start(f32[2,8,128]{2,1,0:T(8,128)} %constant.19.clone.stream_ref) | copy-start | bytes 24580
  1.9 5.5 %copy-start.9 = (f32[4]{0:T(128)S(1)}, f32[4]{0:T(128)}, u32[]{:S(2)}) copy-start(f32[4]{0:T(128)} %diff_ref.1) | copy-start | bytes 52
  1.9 14.7 %collective-permute-start.2 = (f32[8,64,128]{2,1,0:T(8,128)S(1)}, f32[8,64,128]{2,1,0:T(8,128)S(1)}, u32[]{:S(2)}, u32[]{:S(2)}) collective-permute-start(f32[8,64,128]{2,1,0:T(8,128)S(1)} %get-tuple-element.18.first_ref), channel_id=1, source_target_pairs={{8,0},{16,8},{24,16},{32,24},{40,32},{48,40},{56,48},{64,56},{72,6... | collective-permute-start | bytes 786440 | tf_op jit(solution)/shard_map/ppermute | solution.py:596
  5.9 10.7 %copy-start.7 = (bf16[2,2,64,64]{3,2,1,0:T(8,128)(2,1)S(1)}, bf16[2,2,64,64]{3,2,1,0:T(8,128)(2,1)}, u32[]{:S(2)}) copy-start(bf16[2,2,64,64]{3,2,1,0:T(8,128)(2,1)} %constant.22.clone.table_ref) | copy-start | bytes 98308
  5.9 10.7 %collective-permute-start.3 = (f32[8,64,128]{2,1,0:T(8,128)S(1)}, f32[8,64,128]{2,1,0:T(8,128)S(1)}, u32[]{:S(2)}, u32[]{:S(2)}) collective-permute-start(f32[8,64,128]{2,1,0:T(8,128)S(1)} %get-tuple-element.19.second_ref), channel_id=1, source_target_pairs={{0,8},{8,16},{16,24},{24,32},{32,40},{40,48},{48,56},{56,64},{64,7... | collective-permute-start | bytes 786440 | tf_op jit(solution)/shard_map/ppermute | solution.py:597
  8.3 30.8 %copy-start.2 = (bf16[2,4,256,256]{3,2,1,0:T(8,128)(2,1)S(1)}, bf16[2,4,256,256]{3,2,1,0:T(8,128)(2,1)}, u32[]{:S(2)}) copy-start(bf16[2,4,256,256]{3,2,1,0:T(8,128)(2,1)} %constant.23.clone.table_ref) | copy-start | bytes 3145732
  8.4 8.1 %collective-permute-start = (f32[64,128]{1,0:T(8,128)S(1)}, f32[64,128]{1,0:T(8,128)S(1)}, u32[]{:S(2)}, u32[]{:S(2)}) collective-permute-start(f32[64,128]{1,0:T(8,128)S(1)} %get-tuple-element.20), channel_id=1, source_target_pairs={{0,1},{1,2},{2,3},{3,4},{4,5},{5,6},{6,7},{7,0},{8,9},{9,10},{10,1... | collective-permute-start | bytes 98312 | tf_op jit(solution)/shard_map/ppermute | solution.py:612
  11.5 5.1 %collective-permute-start.1 = (f32[64,128]{1,0:T(8,128)S(1)}, f32[64,128]{1,0:T(8,128)S(1)}, u32[]{:S(2)}, u32[]{:S(2)}) collective-permute-start(f32[64,128]{1,0:T(8,128)S(1)} %get-tuple-element.21), channel_id=1, source_target_pairs={{1,0},{2,1},{3,2},{4,3},{5,4},{6,5},{7,6},{0,7},{9,8},{10,9},{11,1... | collective-permute-start | bytes 98312 | tf_op jit(solution)/shard_map/ppermute | solution.py:611
  39.1 20.3 %copy-start.1 = (bf16[2,4,256,256]{3,2,1,0:T(8,128)(2,1)S(1)}, bf16[2,4,256,256]{3,2,1,0:T(8,128)(2,1)}, u32[]{:S(2)}) copy-start(bf16[2,4,256,256]{3,2,1,0:T(8,128)(2,1)} %constant.24.clone.table_ref) | copy-start | bytes 3145732
  59.4 20.0 %copy-start = (f32[3,4,2,64,128]{4,3,2,1,0:T(8,128)S(1)}, f32[3,4,2,64,128]{4,3,2,1,0:T(8,128)}, u32[]{:S(2)}) copy-start(f32[3,4,2,64,128]{4,3,2,1,0:T(8,128)} %vec_ref.5) | copy-start | bytes 2359300
  60.5 19.0 %copy-start.6 = (bf16[2,2,64,64]{3,2,1,0:T(8,128)(2,1)S(1)}, bf16[2,2,64,64]{3,2,1,0:T(8,128)(2,1)}, u32[]{:S(2)}) copy-start(bf16[2,2,64,64]{3,2,1,0:T(8,128)(2,1)} %constant.25.clone.table_ref) | copy-start | bytes 98308

commit v6 on v5

--- a/solution.py
+++ b/solution.py
@@ -228,15 +228,11 @@
         joint_ref[b, 7] = scale * sixteen * right_u[b] * right_w[above]
 
 
-def advect_kernel(
-    first_ref, second_ref, left_ref, right_ref, inner_ref, outer_ref, table_ref,
-    out_ref,
-):
+def advect_kernel(first_ref, second_ref, left_ref, right_ref, out_ref):
     lanes = lane_ids(NZ)
     first, last = lanes == 0, lanes == LANES - 1
     left, right = left_ref[...], right_ref[...]
-    core = lax.axis_index("xs_1")
-    half = jnp.where(core == 0, 0.5, -0.5)
+    half = jnp.where(lax.axis_index("xs_1") == 0, 0.5, -0.5)
 
     def value(field, slot):
         return (first_ref, second_ref)[slot][field]
@@ -247,15 +243,11 @@
         up = jnp.where(last, pltpu.roll(right, (LANES - 1 - at) % LANES, 1), pltpu.roll(x, LANES - 1, 1))
         down = jnp.where(first, pltpu.roll(left, (LANES - at) % LANES, 1), pltpu.roll(x, 1, 1))
         along_x = (up - down) * 0.5
-        if slot == 0:
-            along_y = (value(field, 1) - outer_ref[field]) * half
-        else:
-            along_y = (inner_ref[field] - value(field, 0)) * half
+        along_y = value(field, 1) * half if slot == 0 else value(field, 0) * -half
         along_z = (pltpu.roll(x, NZ - 1, 0) - pltpu.roll(x, 1, 0)) * 0.5
         return along_x, along_y, along_z
 
     for field in range(4):
-        updated = []
         for slot in range(2):
             grad = slopes(field, slot)
             base_grad = slopes(field + 4, slot)
@@ -266,7 +258,18 @@
             result = value(field, slot) - ADV_STEP * advect
             if field == 1:
                 result += BUOYANCY * value(3, slot)
-            updated.append(result)
+            out_ref[field, slot] = result
+
+
+def update_kernel(part_ref, first_ref, second_ref, inner_ref, outer_ref, table_ref, out_ref):
+    core = lax.axis_index("xs_1")
+    step = ADV_STEP * jnp.where(core == 0, 0.5, -0.5)
+    sides = ((first_ref, outer_ref, step), (second_ref, inner_ref, -step))
+    for field in range(4):
+        updated = []
+        for slot, (own_ref, far_ref, weight) in enumerate(sides):
+            far = own_ref[5] * far_ref[field] + own_ref[1] * far_ref[field + 4]
+            updated.append(part_ref[field, slot] + weight * far)
         rows = (
             jnp.where(core == 0, updated[0], updated[1]),
             jnp.where(core == 0, updated[1], updated[0]),
@@ -612,14 +615,22 @@
     left = lax.ppermute(high_x, XS, [(i, (i + 1) % size) for i in range(size)])
 
     plane = ("wall_1",) + XS
+    part = pl.pallas_call(
+        advect_kernel,
+        in_specs=[VMEM] * 4,
+        out_specs=VMEM,
+        out_shape=f32(4, 2, NZ, LANES),
+        compiler_params=SMALL,
+        name="advect",
+    )(first, second, left, right)
     modes = pl.pallas_call(
-        advect_kernel,
-        in_specs=[VMEM] * 7,
+        update_kernel,
+        in_specs=[VMEM] * 6,
         out_specs=VMEM,
         out_shape=f32(NZ * LINES, LANES),
         compiler_params=SMALL,
-        name="advect",
-    )(first, second, left, right, inner, outer, span)
+        name="update",
+    )(part, first, second, inner, outer, span)
     lines = lax.all_to_all(modes.reshape(NZ, LINES, LANES), plane, 0, 0, tiled=True)
     waves, pressure, ends, local = pl.pallas_call(
         stream_kernel,

time: 103 us -> 103 us (level)
  transfers between devices with their start and end apart: 4 -> 4, of which waited for: 2 -> 2; matrix products, arithmetic and copies ran while one was open for 0% -> 0% of each run, Pallas kernels for 1% -> 2%
where the time goes in v6:
time: 103 us
  blocking collectives  81.9 us (80%)
  starting transfers between devices  12.7 us (12%)
  Pallas kernels  6.28 us (6%)
    all_to_all x1, blocking collectives, shards(): lax.all_to_all(modes.reshape(NZ, LINES, LANES), plane, 0, 0, tiled=True)  21.3 us
    all_to_all x1, blocking collectives, shards(): ends = lax.all_to_all(ends, 'wall_0', 0, 0, tiled=True)  19.4 us
    all_to_all x1, blocking collectives, shards(): lax.all_to_all(lines.reshape(NZ, LINES, LANES), plane, 0, 0, tiled=True)  19 us
    all_to_all x1, blocking collectives, shards(): sums = lax.all_to_all(sums, ('wall_1', 'xs_0'), 0, 0, tiled=True)  12.5 us
    all_to_all x1, blocking collectives, shards(): lax.all_to_all(sums, ('wall_0', 'xs_1'), 0, 0, tiled=True).sum(axis=0)  9.75 us
    ppermute x1, starting transfers between devices, shards(): right = lax.ppermute(low_x, XS, [((i + 1) % size, i) for i in range(size)])  4.28 us
    ppermute x1, starting transfers between devices, shards(): lax.ppermute(first, WALL + XS, sum([(down, up)[s % 2][s] for s in range(s...  4.03 us
    ppermute x1, starting transfers between devices, shards(): left = lax.ppermute(high_x, XS, [(i, (i + 1) % size) for i in range(size)])  3.13 us
  transfers between devices with their start and end apart: 4, of which 2 were waited for; matrix products, arithmetic and copies ran while one was open for 0% of the time, Pallas kernels for 2%

profile of v6, /device:TPU:1, one launch (start us, length us, event | category | flops | bytes accessed | tf_op | source)
XLA Modules:
  0.0 102.7 jit_solution(1429644844484219309)
XLA Ops:
  0.6 0.0 copy-start.3
  0.6 0.0 copy-start.4
  0.7 0.0 copy-start.8
  0.7 0.0 copy-start.5
  0.7 1.2 %copy.15 = (f32[8,64,128]{2,1,0:T(8,128)S(1)}, f32[8,64,128]{2,1,0:T(8,128)S(1)}) custom-call(f32[3,4,2,64,128]{4,3,2,1,0:T(8,128)} %vec_ref.5, f32[4,2,64,128]{3,2,1,0:T(8,128)} %base_ref.1), custom_call_target="tpu_custom_call" | custom-call | tf_op jit(solution)/shard_map/copy/pallas_call | solution.py:587
  1.9 0.0 copy-start.9
  1.9 4.0 %collective-permute-start.2 = (f32[8,64,128]{2,1,0:T(8,128)S(1)}, f32[8,64,128]{2,1,0:T(8,128)S(1)}, u32[]{:S(2)}, u32[]{:S(2)}) collective-permute-start(f32[8,64,128]{2,1,0:T(8,128)S(1)} %get-tuple-element.18.first_ref), channel_id=1, source_target_pairs={{8,0},{16,8},{24,16},{32,24},{40,32},{48,40},{56,48},{64,56},{72,6... | collective-permute-start | bytes 786440 | tf_op jit(solution)/shard_map/ppermute | solution.py:599
  5.9 1.3 %collective-permute-start.3 = (f32[8,64,128]{2,1,0:T(8,128)S(1)}, f32[8,64,128]{2,1,0:T(8,128)S(1)}, u32[]{:S(2)}, u32[]{:S(2)}) collective-permute-start(f32[8,64,128]{2,1,0:T(8,128)S(1)} %get-tuple-element.19.second_ref), channel_id=1, source_target_pairs={{0,8},{8,16},{16,24},{24,32},{32,40},{40,48},{48,56},{56,64},{64,7... | collective-permute-start | bytes 786440 | tf_op jit(solution)/shard_map/ppermute | solution.py:600
  7.2 0.0 copy-done.3
  7.2 0.0 copy-done.4
  7.2 0.0 copy-done.8
  7.2 0.0 copy-done.5
  7.3 0.0 copy-done.9
  7.3 0.9 edges.1
  8.2 3.1 %collective-permute-start = (f32[64,128]{1,0:T(8,128)S(1)}, f32[64,128]{1,0:T(8,128)S(1)}, u32[]{:S(2)}, u32[]{:S(2)}) collective-permute-start(f32[64,128]{1,0:T(8,128)S(1)} %get-tuple-element.20), channel_id=1, source_target_pairs={{0,1},{1,2},{2,3},{3,4},{4,5},{5,6},{6,7},{7,0},{8,9},{9,10},{10,1... | collective-permute-start | bytes 98312 | tf_op jit(solution)/shard_map/ppermute | solution.py:615
  11.3 0.0 copy-start.7
  11.3 4.3 %collective-permute-start.1 = (f32[64,128]{1,0:T(8,128)S(1)}, f32[64,128]{1,0:T(8,128)S(1)}, u32[]{:S(2)}, u32[]{:S(2)}) collective-permute-start(f32[64,128]{1,0:T(8,128)S(1)} %get-tuple-element.21), channel_id=1, source_target_pairs={{1,0},{2,1},{3,2},{4,3},{5,4},{6,5},{7,6},{0,7},{9,8},{10,9},{11,1... | collective-permute-start | bytes 98312 | tf_op jit(solution)/shard_map/ppermute | solution.py:614
  15.6 0.7 collective-permute-done.left_ref
  16.3 0.2 collective-permute-done.1.right_ref
  16.5 0.7 advect.1.part_ref
  17.1 0.0 copy-start.2
  17.1 0.0 collective-permute-done.2.inner_ref
  17.2 0.0 collective-permute-done.3.outer_ref
  17.2 0.0 copy-done.7
  17.2 0.3 update.1
  17.5 21.3 %all_to_all.32 = f32[64,8,128]{2,1,0:T(8,128)S(1)} all-to-all(f32[64,8,128]{2,1,0:T(8,128)S(1)} %bitcast.9), channel_id=1, replica_groups=mesh['wall_0'=8,'wall_1'=8,'xs_0'=4,'xs_1'=2] {'wall_1','xs_0','xs_1'}, dimensions={0} | all-to-all | bytes 524288 | tf_op jit(solution)/shard_map/all_to_all | solution.py:634
  38.8 0.0 copy-done.2
  38.8 0.0 copy-start.1
  38.8 0.9 stream.1
  39.7 19.4 %all_to_all.33.in_ref = f32[8,6,8,128]{3,2,1,0:T(8,128)S(1)} all-to-all(f32[8,6,8,128]{3,2,1,0:T(8,128)S(1)} %get-tuple-element.27), channel_id=1, replica_groups=mesh['wall_0'=8,'wall_1'=8,'xs_0'=4,'xs_1'=2] {'wall_0'}, dimensions={0} | all-to-all | bytes 393216 | tf_op jit(solution)/shard_map/all_to_all | solution.py:649
  59.1 0.0 copy-done.1
  59.1 0.0 copy-start
  59.1 1.0 stream_back.1
  60.1 0.0 copy-start.6
  60.1 19.0 %all_to_all.34 = f32[64,8,128]{2,1,0:T(8,128)S(1)} all-to-all(f32[64,8,128]{2,1,0:T(8,128)S(1)} %bitcast.8), channel_id=1, replica_groups=mesh['wall_0'=8,'wall_1'=8,'xs_0'=4,'xs_1'=2] {'wall_1','xs_0','xs_1'}, dimensions={0} | all-to-all | bytes 524288 | tf_op jit(solution)/shard_map/all_to_all | solution.py:662
  79.1 0.0 copy-done
  79.1 0.0 copy-done.6
  79.1 0.4 cells.1
  79.5 9.7 %all_to_all.35 = f32[16,1,128]{2,1,0:T(1,128)S(1)} all-to-all(f32[16,1,128]{2,1,0:T(1,128)S(1)} %bitcast.13), channel_id=1, replica_groups=mesh['wall_0'=8,'wall_1'=8,'xs_0'=4,'xs_1'=2] {'wall_0','xs_1'}, dimensions={0} | all-to-all | bytes 16384 | tf_op jit(solution)/shard_map/all_to_all | solution.py:671
  89.3 12.5 %all_to_all.36 = f32[32,1,128]{2,1,0:T(1,128)S(1)} all-to-all(f32[32,1,128]{2,1,0:T(1,128)S(1)} %broadcast_in_dim.3), channel_id=1, replica_groups=mesh['wall_0'=8,'wall_1'=8,'xs_0'=4,'xs_1'=2] {'wall_1','xs_0'}, dimensions={0} | all-to-all | bytes 32768 | tf_op jit(solution)/shard_map/all_to_all | solution.py:673
  101.8 0.9 residual.1
  (2 shorter events, 0.0 us)
Async XLA Ops:
  0.6 6.6 %copy-start.3 = (bf16[2,5,16,16]{3,2,1,0:T(8,128)(2,1)S(1)}, bf16[2,5,16,16]{3,2,1,0:T(8,128)(2,1)}, u32[]{:S(2)}) copy-start(bf16[2,5,16,16]{3,2,1,0:T(8,128)(2,1)} %constant.21.clone.wall_ref) | copy-start | bytes 15364
  0.6 6.6 %copy-start.4 = (f32[3,16,128]{2,1,0:T(8,128)S(1)}, f32[3,16,128]{2,1,0:T(8,128)}, u32[]{:S(2)}) copy-start(f32[3,16,128]{2,1,0:T(8,128)} %constant.18.clone.marks_ref) | copy-start | bytes 73732
  0.7 6.6 %copy-start.8 = (f32[64,2,128]{2,1,0:T(2,128)S(1)}, f32[64,2,128]{2,1,0:T(2,128)}, u32[]{:S(2)}) copy-start(f32[64,2,128]{2,1,0:T(2,128)} %constant.20.clone.span_ref) | copy-start | bytes 196612
  0.7 6.6 %copy-start.5 = (f32[2,8,128]{2,1,0:T(8,128)S(1)}, f32[2,8,128]{2,1,0:T(8,128)}, u32[]{:S(2)}) copy-start(f32[2,8,128]{2,1,0:T(8,128)} %constant.19.clone.stream_ref) | copy-start | bytes 24580
  1.9 5.4 %copy-start.9 = (f32[4]{0:T(128)S(1)}, f32[4]{0:T(128)}, u32[]{:S(2)}) copy-start(f32[4]{0:T(128)} %diff_ref.1) | copy-start | bytes 52
  1.9 15.3 %collective-permute-start.2 = (f32[8,64,128]{2,1,0:T(8,128)S(1)}, f32[8,64,128]{2,1,0:T(8,128)S(1)}, u32[]{:S(2)}, u32[]{:S(2)}) collective-permute-start(f32[8,64,128]{2,1,0:T(8,128)S(1)} %get-tuple-element.18.first_ref), channel_id=1, source_target_pairs={{8,0},{16,8},{24,16},{32,24},{40,32},{48,40},{56,48},{64,56},{72,6... | collective-permute-start | bytes 786440 | tf_op jit(solution)/shard_map/ppermute | solution.py:599
  5.9 11.2 %collective-permute-start.3 = (f32[8,64,128]{2,1,0:T(8,128)S(1)}, f32[8,64,128]{2,1,0:T(8,128)S(1)}, u32[]{:S(2)}, u32[]{:S(2)}) collective-permute-start(f32[8,64,128]{2,1,0:T(8,128)S(1)} %get-tuple-element.19.second_ref), channel_id=1, source_target_pairs={{0,8},{8,16},{16,24},{24,32},{32,40},{40,48},{48,56},{56,64},{64,7... | collective-permute-start | bytes 786440 | tf_op jit(solution)/shard_map/ppermute | solution.py:600
  8.2 8.1 %collective-permute-start = (f32[64,128]{1,0:T(8,128)S(1)}, f32[64,128]{1,0:T(8,128)S(1)}, u32[]{:S(2)}, u32[]{:S(2)}) collective-permute-start(f32[64,128]{1,0:T(8,128)S(1)} %get-tuple-element.20), channel_id=1, source_target_pairs={{0,1},{1,2},{2,3},{3,4},{4,5},{5,6},{6,7},{7,0},{8,9},{9,10},{10,1... | collective-permute-start | bytes 98312 | tf_op jit(solution)/shard_map/ppermute | solution.py:615
  11.3 5.9 %copy-start.7 = (bf16[2,2,64,64]{3,2,1,0:T(8,128)(2,1)S(1)}, bf16[2,2,64,64]{3,2,1,0:T(8,128)(2,1)}, u32[]{:S(2)}) copy-start(bf16[2,2,64,64]{3,2,1,0:T(8,128)(2,1)} %constant.22.clone.table_ref) | copy-start | bytes 98308
  11.3 5.1 %collective-permute-start.1 = (f32[64,128]{1,0:T(8,128)S(1)}, f32[64,128]{1,0:T(8,128)S(1)}, u32[]{:S(2)}, u32[]{:S(2)}) collective-permute-start(f32[64,128]{1,0:T(8,128)S(1)} %get-tuple-element.21), channel_id=1, source_target_pairs={{1,0},{2,1},{3,2},{4,3},{5,4},{6,5},{7,6},{0,7},{9,8},{10,9},{11,1... | collective-permute-start | bytes 98312 | tf_op jit(solution)/shard_map/ppermute | solution.py:614
  17.1 21.7 %copy-start.2 = (bf16[2,4,256,256]{3,2,1,0:T(8,128)(2,1)S(1)}, bf16[2,4,256,256]{3,2,1,0:T(8,128)(2,1)}, u32[]{:S(2)}) copy-start(bf16[2,4,256,256]{3,2,1,0:T(8,128)(2,1)} %constant.23.clone.table_ref) | copy-start | bytes 3145732
  38.8 20.3 %copy-start.1 = (bf16[2,4,256,256]{3,2,1,0:T(8,128)(2,1)S(1)}, bf16[2,4,256,256]{3,2,1,0:T(8,128)(2,1)}, u32[]{:S(2)}) copy-start(bf16[2,4,256,256]{3,2,1,0:T(8,128)(2,1)} %constant.24.clone.table_ref) | copy-start | bytes 3145732
  59.1 20.0 %copy-start = (f32[3,4,2,64,128]{4,3,2,1,0:T(8,128)S(1)}, f32[3,4,2,64,128]{4,3,2,1,0:T(8,128)}, u32[]{:S(2)}) copy-start(f32[3,4,2,64,128]{4,3,2,1,0:T(8,128)} %vec_ref.5) | copy-start | bytes 2359300
  60.1 19.0 %copy-start.6 = (bf16[2,2,64,64]{3,2,1,0:T(8,128)(2,1)S(1)}, bf16[2,2,64,64]{3,2,1,0:T(8,128)(2,1)}, u32[]{:S(2)}) copy-start(bf16[2,2,64,64]{3,2,1,0:T(8,128)(2,1)} %constant.25.clone.table_ref) | copy-start | bytes 98308

commit v7 on v6

--- a/solution.py
+++ b/solution.py
@@ -320,7 +320,7 @@
     waves = wall_times(wall_ref, SINE, side_by_side(fields))
     waves_ref[...] = waves
     rise = wall_times(wall_ref, SINE_SLOPE, fields[1])
-    head, tail = marks_ref[1], marks_ref[2]
+    head = marks_ref[1]
     span = slope_ref[0:1, :]
 
     def wave(field, tile):
@@ -337,9 +337,12 @@
     lift = wall_times(wall_ref, LIFT, joined)
 
     def ends(f):
-        return (
-            jnp.sum(f * tail, axis=0, keepdims=True), jnp.sum(f * head, axis=0, keepdims=True)
-        )
+        weighted = f * head
+        total = weighted[:LINES] + weighted[LINES:]
+        total = total + pltpu.roll(total, 4, 0)
+        total = total + pltpu.roll(total, 2, 0)
+        even, odd = total[:1], total[1:2]
+        return even - odd, even + odd
 
     for tile in range(BLOCKS):
         p = pressure[tile]
@@ -531,7 +534,8 @@
     lanes = lane_ids(16)
     packed = jnp.zeros((16, LANES), jnp.float32)
     for at in range(10):
-        packed = jnp.where(lanes == at, jnp.sum(sums[at]), packed)
+        total = jnp.sum(jnp.sum(sums[at], axis=0, keepdims=True), axis=1, keepdims=True)
+        packed = jnp.where(lanes == at, total, packed)
     sums_ref[...] = packed
 
 

time: 103 us -> 103 us (level)
  no operation moved by 1% of the time
where the time goes in v7:
time: 103 us
  blocking collectives  81.9 us (80%)
  starting transfers between devices  12.7 us (12%)
  Pallas kernels  6.18 us (6%)
    all_to_all x1, blocking collectives, shards(): lax.all_to_all(modes.reshape(NZ, LINES, LANES), plane, 0, 0, tiled=True)  21.3 us
    all_to_all x1, blocking collectives, shards(): ends = lax.all_to_all(ends, 'wall_0', 0, 0, tiled=True)  19.4 us
    all_to_all x1, blocking collectives, shards(): lax.all_to_all(lines.reshape(NZ, LINES, LANES), plane, 0, 0, tiled=True)  19 us
    all_to_all x1, blocking collectives, shards(): sums = lax.all_to_all(sums, ('wall_1', 'xs_0'), 0, 0, tiled=True)  12.5 us
    all_to_all x1, blocking collectives, shards(): lax.all_to_all(sums, ('wall_0', 'xs_1'), 0, 0, tiled=True).sum(axis=0)  9.76 us
    ppermute x1, starting transfers between devices, shards(): right = lax.ppermute(low_x, XS, [((i + 1) % size, i) for i in range(size)])  4.28 us
    ppermute x1, starting transfers between devices, shards(): lax.ppermute(first, WALL + XS, sum([(down, up)[s % 2][s] for s in range(s...  4.03 us
    ppermute x1, starting transfers between devices, shards(): left = lax.ppermute(high_x, XS, [(i, (i + 1) % size) for i in range(size)])  3.13 us
  transfers between devices with their start and end apart: 4, of which 2 were waited for; matrix products, arithmetic and copies ran while one was open for 0% of the time, Pallas kernels for 2%

profile of v7, /device:TPU:1, one launch (start us, length us, event | category | flops | bytes accessed | tf_op | source)
XLA Modules:
  0.0 102.6 jit_solution(9612509387283693870)
XLA Ops:
  0.6 0.0 copy-start.3
  0.6 0.0 copy-start.4
  0.7 0.0 copy-start.8
  0.7 0.0 copy-start.5
  0.7 1.2 %copy.15 = (f32[8,64,128]{2,1,0:T(8,128)S(1)}, f32[8,64,128]{2,1,0:T(8,128)S(1)}) custom-call(f32[3,4,2,64,128]{4,3,2,1,0:T(8,128)} %vec_ref.5, f32[4,2,64,128]{3,2,1,0:T(8,128)} %base_ref.1), custom_call_target="tpu_custom_call" | custom-call | tf_op jit(solution)/shard_map/copy/pallas_call | solution.py:591
  1.9 0.0 copy-start.9
  1.9 4.0 %collective-permute-start.2 = (f32[8,64,128]{2,1,0:T(8,128)S(1)}, f32[8,64,128]{2,1,0:T(8,128)S(1)}, u32[]{:S(2)}, u32[]{:S(2)}) collective-permute-start(f32[8,64,128]{2,1,0:T(8,128)S(1)} %get-tuple-element.18.first_ref), channel_id=1, source_target_pairs={{8,0},{16,8},{24,16},{32,24},{40,32},{48,40},{56,48},{64,56},{72,6... | collective-permute-start | bytes 786440 | tf_op jit(solution)/shard_map/ppermute | solution.py:603
  5.9 1.3 %collective-permute-start.3 = (f32[8,64,128]{2,1,0:T(8,128)S(1)}, f32[8,64,128]{2,1,0:T(8,128)S(1)}, u32[]{:S(2)}, u32[]{:S(2)}) collective-permute-start(f32[8,64,128]{2,1,0:T(8,128)S(1)} %get-tuple-element.19.second_ref), channel_id=1, source_target_pairs={{0,8},{8,16},{16,24},{24,32},{32,40},{40,48},{48,56},{56,64},{64,7... | collective-permute-start | bytes 786440 | tf_op jit(solution)/shard_map/ppermute | solution.py:604
  7.2 0.0 copy-done.3
  7.2 0.0 copy-done.4
  7.2 0.0 copy-done.8
  7.2 0.0 copy-done.5
  7.3 0.0 copy-done.9
  7.3 0.9 edges.1
  8.2 3.1 %collective-permute-start = (f32[64,128]{1,0:T(8,128)S(1)}, f32[64,128]{1,0:T(8,128)S(1)}, u32[]{:S(2)}, u32[]{:S(2)}) collective-permute-start(f32[64,128]{1,0:T(8,128)S(1)} %get-tuple-element.20), channel_id=1, source_target_pairs={{0,1},{1,2},{2,3},{3,4},{4,5},{5,6},{6,7},{7,0},{8,9},{9,10},{10,1... | collective-permute-start | bytes 98312 | tf_op jit(solution)/shard_map/ppermute | solution.py:619
  11.3 0.0 copy-start.7
  11.3 4.3 %collective-permute-start.1 = (f32[64,128]{1,0:T(8,128)S(1)}, f32[64,128]{1,0:T(8,128)S(1)}, u32[]{:S(2)}, u32[]{:S(2)}) collective-permute-start(f32[64,128]{1,0:T(8,128)S(1)} %get-tuple-element.21), channel_id=1, source_target_pairs={{1,0},{2,1},{3,2},{4,3},{5,4},{6,5},{7,6},{0,7},{9,8},{10,9},{11,1... | collective-permute-start | bytes 98312 | tf_op jit(solution)/shard_map/ppermute | solution.py:618
  15.6 0.7 collective-permute-done.left_ref
  16.3 0.2 collective-permute-done.1.right_ref
  16.5 0.7 advect.1.part_ref
  17.1 0.0 copy-start.2
  17.1 0.0 collective-permute-done.2.inner_ref
  17.2 0.0 collective-permute-done.3.outer_ref
  17.2 0.0 copy-done.7
  17.2 0.3 update.1
  17.5 21.3 %all_to_all.32 = f32[64,8,128]{2,1,0:T(8,128)S(1)} all-to-all(f32[64,8,128]{2,1,0:T(8,128)S(1)} %bitcast.9), channel_id=1, replica_groups=mesh['wall_0'=8,'wall_1'=8,'xs_0'=4,'xs_1'=2] {'wall_1','xs_0','xs_1'}, dimensions={0} | all-to-all | bytes 524288 | tf_op jit(solution)/shard_map/all_to_all | solution.py:638
  38.8 0.0 copy-done.2
  38.8 0.0 copy-start.1
  38.8 0.9 stream.1
  39.7 19.4 %all_to_all.33.in_ref = f32[8,6,8,128]{3,2,1,0:T(8,128)S(1)} all-to-all(f32[8,6,8,128]{3,2,1,0:T(8,128)S(1)} %get-tuple-element.27), channel_id=1, replica_groups=mesh['wall_0'=8,'wall_1'=8,'xs_0'=4,'xs_1'=2] {'wall_0'}, dimensions={0} | all-to-all | bytes 393216 | tf_op jit(solution)/shard_map/all_to_all | solution.py:653
  59.1 0.0 copy-done.1
  59.1 0.0 copy-start
  59.1 1.0 stream_back.1
  60.1 0.0 copy-start.6
  60.1 19.0 %all_to_all.34 = f32[64,8,128]{2,1,0:T(8,128)S(1)} all-to-all(f32[64,8,128]{2,1,0:T(8,128)S(1)} %bitcast.8), channel_id=1, replica_groups=mesh['wall_0'=8,'wall_1'=8,'xs_0'=4,'xs_1'=2] {'wall_1','xs_0','xs_1'}, dimensions={0} | all-to-all | bytes 524288 | tf_op jit(solution)/shard_map/all_to_all | solution.py:666
  79.1 0.0 copy-done
  79.1 0.0 copy-done.6
  79.1 0.3 cells.1
  79.4 9.8 %all_to_all.35 = f32[16,1,128]{2,1,0:T(1,128)S(1)} all-to-all(f32[16,1,128]{2,1,0:T(1,128)S(1)} %bitcast.13), channel_id=1, replica_groups=mesh['wall_0'=8,'wall_1'=8,'xs_0'=4,'xs_1'=2] {'wall_0','xs_1'}, dimensions={0} | all-to-all | bytes 16384 | tf_op jit(solution)/shard_map/all_to_all | solution.py:675
  89.2 12.5 %all_to_all.36 = f32[32,1,128]{2,1,0:T(1,128)S(1)} all-to-all(f32[32,1,128]{2,1,0:T(1,128)S(1)} %broadcast_in_dim.3), channel_id=1, replica_groups=mesh['wall_0'=8,'wall_1'=8,'xs_0'=4,'xs_1'=2] {'wall_1','xs_0'}, dimensions={0} | all-to-all | bytes 32768 | tf_op jit(solution)/shard_map/all_to_all | solution.py:677
  101.7 0.9 residual.1
  (2 shorter events, 0.0 us)
Async XLA Ops:
  0.6 6.6 %copy-start.3 = (bf16[2,5,16,16]{3,2,1,0:T(8,128)(2,1)S(1)}, bf16[2,5,16,16]{3,2,1,0:T(8,128)(2,1)}, u32[]{:S(2)}) copy-start(bf16[2,5,16,16]{3,2,1,0:T(8,128)(2,1)} %constant.21.clone.wall_ref) | copy-start | bytes 15364
  0.6 6.6 %copy-start.4 = (f32[3,16,128]{2,1,0:T(8,128)S(1)}, f32[3,16,128]{2,1,0:T(8,128)}, u32[]{:S(2)}) copy-start(f32[3,16,128]{2,1,0:T(8,128)} %constant.18.clone.marks_ref) | copy-start | bytes 73732
  0.7 6.6 %copy-start.8 = (f32[64,2,128]{2,1,0:T(2,128)S(1)}, f32[64,2,128]{2,1,0:T(2,128)}, u32[]{:S(2)}) copy-start(f32[64,2,128]{2,1,0:T(2,128)} %constant.20.clone.span_ref) | copy-start | bytes 196612
  0.7 6.6 %copy-start.5 = (f32[2,8,128]{2,1,0:T(8,128)S(1)}, f32[2,8,128]{2,1,0:T(8,128)}, u32[]{:S(2)}) copy-start(f32[2,8,128]{2,1,0:T(8,128)} %constant.19.clone.stream_ref) | copy-start | bytes 24580
  1.9 5.4 %copy-start.9 = (f32[4]{0:T(128)S(1)}, f32[4]{0:T(128)}, u32[]{:S(2)}) copy-start(f32[4]{0:T(128)} %diff_ref.1) | copy-start | bytes 52
  1.9 15.3 %collective-permute-start.2 = (f32[8,64,128]{2,1,0:T(8,128)S(1)}, f32[8,64,128]{2,1,0:T(8,128)S(1)}, u32[]{:S(2)}, u32[]{:S(2)}) collective-permute-start(f32[8,64,128]{2,1,0:T(8,128)S(1)} %get-tuple-element.18.first_ref), channel_id=1, source_target_pairs={{8,0},{16,8},{24,16},{32,24},{40,32},{48,40},{56,48},{64,56},{72,6... | collective-permute-start | bytes 786440 | tf_op jit(solution)/shard_map/ppermute | solution.py:603
  5.9 11.2 %collective-permute-start.3 = (f32[8,64,128]{2,1,0:T(8,128)S(1)}, f32[8,64,128]{2,1,0:T(8,128)S(1)}, u32[]{:S(2)}, u32[]{:S(2)}) collective-permute-start(f32[8,64,128]{2,1,0:T(8,128)S(1)} %get-tuple-element.19.second_ref), channel_id=1, source_target_pairs={{0,8},{8,16},{16,24},{24,32},{32,40},{40,48},{48,56},{56,64},{64,7... | collective-permute-start | bytes 786440 | tf_op jit(solution)/shard_map/ppermute | solution.py:604
  8.2 8.1 %collective-permute-start = (f32[64,128]{1,0:T(8,128)S(1)}, f32[64,128]{1,0:T(8,128)S(1)}, u32[]{:S(2)}, u32[]{:S(2)}) collective-permute-start(f32[64,128]{1,0:T(8,128)S(1)} %get-tuple-element.20), channel_id=1, source_target_pairs={{0,1},{1,2},{2,3},{3,4},{4,5},{5,6},{6,7},{7,0},{8,9},{9,10},{10,1... | collective-permute-start | bytes 98312 | tf_op jit(solution)/shard_map/ppermute | solution.py:619
  11.3 5.9 %copy-start.7 = (bf16[2,2,64,64]{3,2,1,0:T(8,128)(2,1)S(1)}, bf16[2,2,64,64]{3,2,1,0:T(8,128)(2,1)}, u32[]{:S(2)}) copy-start(bf16[2,2,64,64]{3,2,1,0:T(8,128)(2,1)} %constant.22.clone.table_ref) | copy-start | bytes 98308
  11.3 5.1 %collective-permute-start.1 = (f32[64,128]{1,0:T(8,128)S(1)}, f32[64,128]{1,0:T(8,128)S(1)}, u32[]{:S(2)}, u32[]{:S(2)}) collective-permute-start(f32[64,128]{1,0:T(8,128)S(1)} %get-tuple-element.21), channel_id=1, source_target_pairs={{1,0},{2,1},{3,2},{4,3},{5,4},{6,5},{7,6},{0,7},{9,8},{10,9},{11,1... | collective-permute-start | bytes 98312 | tf_op jit(solution)/shard_map/ppermute | solution.py:618
  17.1 21.7 %copy-start.2 = (bf16[2,4,256,256]{3,2,1,0:T(8,128)(2,1)S(1)}, bf16[2,4,256,256]{3,2,1,0:T(8,128)(2,1)}, u32[]{:S(2)}) copy-start(bf16[2,4,256,256]{3,2,1,0:T(8,128)(2,1)} %constant.23.clone.table_ref) | copy-start | bytes 3145732
  38.8 20.3 %copy-start.1 = (bf16[2,4,256,256]{3,2,1,0:T(8,128)(2,1)S(1)}, bf16[2,4,256,256]{3,2,1,0:T(8,128)(2,1)}, u32[]{:S(2)}) copy-start(bf16[2,4,256,256]{3,2,1,0:T(8,128)(2,1)} %constant.24.clone.table_ref) | copy-start | bytes 3145732
  59.1 20.0 %copy-start = (f32[3,4,2,64,128]{4,3,2,1,0:T(8,128)S(1)}, f32[3,4,2,64,128]{4,3,2,1,0:T(8,128)}, u32[]{:S(2)}) copy-start(f32[3,4,2,64,128]{4,3,2,1,0:T(8,128)} %vec_ref.5) | copy-start | bytes 2359300
  60.1 19.0 %copy-start.6 = (bf16[2,2,64,64]{3,2,1,0:T(8,128)(2,1)S(1)}, bf16[2,2,64,64]{3,2,1,0:T(8,128)(2,1)}, u32[]{:S(2)}) copy-start(bf16[2,2,64,64]{3,2,1,0:T(8,128)(2,1)} %constant.25.clone.table_ref) | copy-start | bytes 98308

commit v8 on v7

--- a/solution.py
+++ b/solution.py
@@ -28,6 +28,11 @@
     high = table.astype(ml_dtypes.bfloat16)
     low = (table - high.astype(np.float64)).astype(ml_dtypes.bfloat16)
     return high, low
+
+
+def joined(table):
+    high, low = split(table)
+    return np.concatenate([high, high, low], axis=-1)
 
 
 def spanwise_tables():
@@ -99,7 +104,7 @@
     marks = np.broadcast_to(marks[:, :, None], (3, ROWS, LANES)).astype(np.float32)
     lift = sine @ slope @ sine
     tables = np.stack([sine[:, rows], (sine @ slope)[:, rows], lift, sine[:, rows].T, lift.T])
-    return np.stack(split(tables)), marks
+    return joined(tables), marks
 
 
 def halves(x):
@@ -121,12 +126,12 @@
 
 
 def wall_times(ref, which, x):
-    return table_times(ref[0, which], ref[1, which], x)
-
-
-def table_times(high_table, low_table, x):
+    return table_times(ref[which], x)
+
+
+def table_times(table, x):
     high, low = halves(x)
-    return dot(high_table, high) + (dot(high_table, low) + dot(low_table, high))
+    return dot(table, jnp.concatenate([high, low, high], axis=0))
 
 
 def lane_ids(rows):
@@ -276,7 +281,7 @@
         )
         if field < 3:
             kind = field // 2
-            modes = table_times(table_ref[0, kind], table_ref[1, kind], jnp.concatenate(rows, axis=1))
+            modes = table_times(table_ref[kind], jnp.concatenate(rows, axis=1))
             rows = (modes[:, :LANES], modes[:, LANES:])
         for row in range(2):
             out_ref[pl.ds(2 * field + row, NZ, stride=LINES), :] = rows[row]
@@ -523,7 +528,7 @@
             part = 2 * field + row
             cells = in_ref[pl.ds(part, NZ, stride=LINES), :]
             if field < 3:
-                cells = table_times(table_ref[0, field // 2], table_ref[1, field // 2], cells)
+                cells = table_times(table_ref[field // 2], cells)
             cur_ref[field, row] = cells
             vectors = [vec_ref[q, field, row] for q in range(3)]
             for q in range(3):
@@ -585,7 +590,8 @@
     span_columns = np.broadcast_to(span_columns[:, :, None], (NZ, 2, LANES)).astype(np.float32)
     stream, stream_columns = stream_tables()
     wall, marks = block_tables()
-    span, stream = np.stack(split(span)), np.stack(split(stream))
+    stream = np.stack(split(stream))
+    span, span_back = joined(span), joined(span.transpose(0, 2, 1))
 
     rows = f32(8, NZ, LANES)
     first, second = pl.pallas_call(
@@ -671,7 +677,7 @@
         out_shape=[f32(4, 2, NZ, LANES), f32(16, LANES)],
         compiler_params=SMALL,
         name="cells",
-    )(modes.reshape(-1, LANES), krylov_basis, span.transpose(0, 1, 3, 2))
+    )(modes.reshape(-1, LANES), krylov_basis, span_back)
     sums = lax.all_to_all(sums, ("wall_0", "xs_1"), 0, 0, tiled=True).sum(axis=0)
     sums = jnp.broadcast_to(sums, (32, LANES))
     sums = lax.all_to_all(sums, ("wall_1", "xs_0"), 0, 0, tiled=True)

time: 103 us -> 103 us (level)
  no operation moved by 1% of the time
where the time goes in v8:
time: 103 us; the launch traced here: 102 us
  blocking collectives  82 us (80%)
  starting transfers between devices  12.7 us (12%)
  Pallas kernels  5.91 us (6%)
    all_to_all x1, blocking collectives, shards(): lax.all_to_all(modes.reshape(NZ, LINES, LANES), plane, 0, 0, tiled=True)  21.4 us
    all_to_all x1, blocking collectives, shards(): ends = lax.all_to_all(ends, 'wall_0', 0, 0, tiled=True)  19.4 us
    all_to_all x1, blocking collectives, shards(): lax.all_to_all(lines.reshape(NZ, LINES, LANES), plane, 0, 0, tiled=True)  19 us
    all_to_all x1, blocking collectives, shards(): sums = lax.all_to_all(sums, ('wall_1', 'xs_0'), 0, 0, tiled=True)  12.5 us
    all_to_all x1, blocking collectives, shards(): lax.all_to_all(sums, ('wall_0', 'xs_1'), 0, 0, tiled=True).sum(axis=0)  9.76 us
    ppermute x1, starting transfers between devices, shards(): right = lax.ppermute(low_x, XS, [((i + 1) % size, i) for i in range(size)])  4.28 us
    ppermute x1, starting transfers between devices, shards(): lax.ppermute(first, WALL + XS, sum([(down, up)[s % 2][s] for s in range(s...  4.03 us
    ppermute x1, starting transfers between devices, shards(): left = lax.ppermute(high_x, XS, [(i, (i + 1) % size) for i in range(size)])  3.13 us
  transfers between devices with their start and end apart: 4, of which 2 were waited for; matrix products, arithmetic and copies ran while one was open for 0% of the time, Pallas kernels for 2%

profile of v8, /device:TPU:1, one launch (start us, length us, event | category | flops | bytes accessed | tf_op | source)
XLA Modules:
  0.0 102.5 jit_solution(3174128947182648916)
XLA Ops:
  0.6 0.0 copy-start.3
  0.6 0.0 copy-start.4
  0.7 0.0 copy-start.8
  0.7 0.0 copy-start.5
  0.7 1.2 %copy.15 = (f32[8,64,128]{2,1,0:T(8,128)S(1)}, f32[8,64,128]{2,1,0:T(8,128)S(1)}) custom-call(f32[3,4,2,64,128]{4,3,2,1,0:T(8,128)} %vec_ref.5, f32[4,2,64,128]{3,2,1,0:T(8,128)} %base_ref.1), custom_call_target="tpu_custom_call" | custom-call | tf_op jit(solution)/shard_map/copy/pallas_call | solution.py:597
  1.9 0.0 copy-start.9
  1.9 4.0 %collective-permute-start.2 = (f32[8,64,128]{2,1,0:T(8,128)S(1)}, f32[8,64,128]{2,1,0:T(8,128)S(1)}, u32[]{:S(2)}, u32[]{:S(2)}) collective-permute-start(f32[8,64,128]{2,1,0:T(8,128)S(1)} %get-tuple-element.18.first_ref), channel_id=1, source_target_pairs={{8,0},{16,8},{24,16},{32,24},{40,32},{48,40},{56,48},{64,56},{72,6... | collective-permute-start | bytes 786440 | tf_op jit(solution)/shard_map/ppermute | solution.py:609
  5.9 1.3 %collective-permute-start.3 = (f32[8,64,128]{2,1,0:T(8,128)S(1)}, f32[8,64,128]{2,1,0:T(8,128)S(1)}, u32[]{:S(2)}, u32[]{:S(2)}) collective-permute-start(f32[8,64,128]{2,1,0:T(8,128)S(1)} %get-tuple-element.19.second_ref), channel_id=1, source_target_pairs={{0,8},{8,16},{16,24},{24,32},{32,40},{40,48},{48,56},{56,64},{64,7... | collective-permute-start | bytes 786440 | tf_op jit(solution)/shard_map/ppermute | solution.py:610
  7.2 0.0 copy-done.3
  7.2 0.0 copy-done.4
  7.2 0.0 copy-done.8
  7.2 0.0 copy-done.5
  7.3 0.0 copy-done.9
  7.3 0.9 edges.1
  8.2 3.1 %collective-permute-start = (f32[64,128]{1,0:T(8,128)S(1)}, f32[64,128]{1,0:T(8,128)S(1)}, u32[]{:S(2)}, u32[]{:S(2)}) collective-permute-start(f32[64,128]{1,0:T(8,128)S(1)} %get-tuple-element.20), channel_id=1, source_target_pairs={{0,1},{1,2},{2,3},{3,4},{4,5},{5,6},{6,7},{7,0},{8,9},{9,10},{10,1... | collective-permute-start | bytes 98312 | tf_op jit(solution)/shard_map/ppermute | solution.py:625
  11.3 0.0 copy-start.7
  11.3 4.3 %collective-permute-start.1 = (f32[64,128]{1,0:T(8,128)S(1)}, f32[64,128]{1,0:T(8,128)S(1)}, u32[]{:S(2)}, u32[]{:S(2)}) collective-permute-start(f32[64,128]{1,0:T(8,128)S(1)} %get-tuple-element.21), channel_id=1, source_target_pairs={{1,0},{2,1},{3,2},{4,3},{5,4},{6,5},{7,6},{0,7},{9,8},{10,9},{11,1... | collective-permute-start | bytes 98312 | tf_op jit(solution)/shard_map/ppermute | solution.py:624
  15.6 0.7 collective-permute-done.left_ref
  16.3 0.2 collective-permute-done.1.right_ref
  16.5 0.7 advect.1.part_ref
  17.1 0.0 copy-start.2
  17.1 0.0 collective-permute-done.2.inner_ref
  17.2 0.0 collective-permute-done.3.outer_ref
  17.2 0.0 copy-done.7
  17.2 0.2 update.1
  17.4 21.4 %all_to_all.32 = f32[64,8,128]{2,1,0:T(8,128)S(1)} all-to-all(f32[64,8,128]{2,1,0:T(8,128)S(1)} %bitcast.9), channel_id=1, replica_groups=mesh['wall_0'=8,'wall_1'=8,'xs_0'=4,'xs_1'=2] {'wall_1','xs_0','xs_1'}, dimensions={0} | all-to-all | bytes 524288 | tf_op jit(solution)/shard_map/all_to_all | solution.py:644
  38.9 0.0 copy-done.2
  38.9 0.0 copy-start.1
  38.9 0.8 stream.1
  39.7 19.4 %all_to_all.33.in_ref = f32[8,6,8,128]{3,2,1,0:T(8,128)S(1)} all-to-all(f32[8,6,8,128]{3,2,1,0:T(8,128)S(1)} %get-tuple-element.27), channel_id=1, replica_groups=mesh['wall_0'=8,'wall_1'=8,'xs_0'=4,'xs_1'=2] {'wall_0'}, dimensions={0} | all-to-all | bytes 393216 | tf_op jit(solution)/shard_map/all_to_all | solution.py:659
  59.1 0.0 copy-done.1
  59.1 0.0 copy-start
  59.1 0.9 stream_back.1
  60.0 0.0 copy-start.6
  60.0 19.0 %all_to_all.34 = f32[64,8,128]{2,1,0:T(8,128)S(1)} all-to-all(f32[64,8,128]{2,1,0:T(8,128)S(1)} %bitcast.8), channel_id=1, replica_groups=mesh['wall_0'=8,'wall_1'=8,'xs_0'=4,'xs_1'=2] {'wall_1','xs_0','xs_1'}, dimensions={0} | all-to-all | bytes 524288 | tf_op jit(solution)/shard_map/all_to_all | solution.py:672
  78.9 0.0 copy-done
  79.0 0.0 copy-done.6
  79.0 0.3 cells.1
  79.3 9.8 %all_to_all.35 = f32[16,1,128]{2,1,0:T(1,128)S(1)} all-to-all(f32[16,1,128]{2,1,0:T(1,128)S(1)} %bitcast.13), channel_id=1, replica_groups=mesh['wall_0'=8,'wall_1'=8,'xs_0'=4,'xs_1'=2] {'wall_0','xs_1'}, dimensions={0} | all-to-all | bytes 16384 | tf_op jit(solution)/shard_map/all_to_all | solution.py:681
  89.1 12.5 %all_to_all.36 = f32[32,1,128]{2,1,0:T(1,128)S(1)} all-to-all(f32[32,1,128]{2,1,0:T(1,128)S(1)} %broadcast_in_dim.3), channel_id=1, replica_groups=mesh['wall_0'=8,'wall_1'=8,'xs_0'=4,'xs_1'=2] {'wall_1','xs_0'}, dimensions={0} | all-to-all | bytes 32768 | tf_op jit(solution)/shard_map/all_to_all | solution.py:683
  101.6 0.9 residual.1
  (2 shorter events, 0.0 us)
Async XLA Ops:
  0.6 6.6 %copy-start.3 = (f32[3,16,128]{2,1,0:T(8,128)S(1)}, f32[3,16,128]{2,1,0:T(8,128)}, u32[]{:S(2)}) copy-start(f32[3,16,128]{2,1,0:T(8,128)} %constant.18.clone.marks_ref) | copy-start | bytes 73732
  0.6 6.6 %copy-start.4 = (bf16[5,16,48]{2,1,0:T(8,128)(2,1)S(1)}, bf16[5,16,48]{2,1,0:T(8,128)(2,1)}, u32[]{:S(2)}) copy-start(bf16[5,16,48]{2,1,0:T(8,128)(2,1)} %constant.21.clone.wall_ref) | copy-start | bytes 23044
  0.7 6.6 %copy-start.8 = (f32[64,2,128]{2,1,0:T(2,128)S(1)}, f32[64,2,128]{2,1,0:T(2,128)}, u32[]{:S(2)}) copy-start(f32[64,2,128]{2,1,0:T(2,128)} %constant.20.clone.span_ref) | copy-start | bytes 196612
  0.7 6.6 %copy-start.5 = (f32[2,8,128]{2,1,0:T(8,128)S(1)}, f32[2,8,128]{2,1,0:T(8,128)}, u32[]{:S(2)}) copy-start(f32[2,8,128]{2,1,0:T(8,128)} %constant.19.clone.stream_ref) | copy-start | bytes 24580
  1.9 5.4 %copy-start.9 = (f32[4]{0:T(128)S(1)}, f32[4]{0:T(128)}, u32[]{:S(2)}) copy-start(f32[4]{0:T(128)} %diff_ref.1) | copy-start | bytes 52
  1.9 15.3 %collective-permute-start.2 = (f32[8,64,128]{2,1,0:T(8,128)S(1)}, f32[8,64,128]{2,1,0:T(8,128)S(1)}, u32[]{:S(2)}, u32[]{:S(2)}) collective-permute-start(f32[8,64,128]{2,1,0:T(8,128)S(1)} %get-tuple-element.18.first_ref), channel_id=1, source_target_pairs={{8,0},{16,8},{24,16},{32,24},{40,32},{48,40},{56,48},{64,56},{72,6... | collective-permute-start | bytes 786440 | tf_op jit(solution)/shard_map/ppermute | solution.py:609
  5.9 11.2 %collective-permute-start.3 = (f32[8,64,128]{2,1,0:T(8,128)S(1)}, f32[8,64,128]{2,1,0:T(8,128)S(1)}, u32[]{:S(2)}, u32[]{:S(2)}) collective-permute-start(f32[8,64,128]{2,1,0:T(8,128)S(1)} %get-tuple-element.19.second_ref), channel_id=1, source_target_pairs={{0,8},{8,16},{16,24},{24,32},{32,40},{40,48},{48,56},{56,64},{64,7... | collective-permute-start | bytes 786440 | tf_op jit(solution)/shard_map/ppermute | solution.py:610
  8.2 8.1 %collective-permute-start = (f32[64,128]{1,0:T(8,128)S(1)}, f32[64,128]{1,0:T(8,128)S(1)}, u32[]{:S(2)}, u32[]{:S(2)}) collective-permute-start(f32[64,128]{1,0:T(8,128)S(1)} %get-tuple-element.20), channel_id=1, source_target_pairs={{0,1},{1,2},{2,3},{3,4},{4,5},{5,6},{6,7},{7,0},{8,9},{9,10},{10,1... | collective-permute-start | bytes 98312 | tf_op jit(solution)/shard_map/ppermute | solution.py:625
  11.3 5.9 %copy-start.7 = (bf16[2,64,192]{2,1,0:T(8,128)(2,1)S(1)}, bf16[2,64,192]{2,1,0:T(8,128)(2,1)}, u32[]{:S(2)}) copy-start(bf16[2,64,192]{2,1,0:T(8,128)(2,1)} %constant.22.clone.table_ref) | copy-start | bytes 147460
  11.3 5.1 %collective-permute-start.1 = (f32[64,128]{1,0:T(8,128)S(1)}, f32[64,128]{1,0:T(8,128)S(1)}, u32[]{:S(2)}, u32[]{:S(2)}) collective-permute-start(f32[64,128]{1,0:T(8,128)S(1)} %get-tuple-element.21), channel_id=1, source_target_pairs={{1,0},{2,1},{3,2},{4,3},{5,4},{6,5},{7,6},{0,7},{9,8},{10,9},{11,1... | collective-permute-start | bytes 98312 | tf_op jit(solution)/shard_map/ppermute | solution.py:624
  17.1 21.8 %copy-start.2 = (bf16[2,4,256,256]{3,2,1,0:T(8,128)(2,1)S(1)}, bf16[2,4,256,256]{3,2,1,0:T(8,128)(2,1)}, u32[]{:S(2)}) copy-start(bf16[2,4,256,256]{3,2,1,0:T(8,128)(2,1)} %constant.23.clone.table_ref) | copy-start | bytes 3145732
  38.9 20.2 %copy-start.1 = (bf16[2,4,256,256]{3,2,1,0:T(8,128)(2,1)S(1)}, bf16[2,4,256,256]{3,2,1,0:T(8,128)(2,1)}, u32[]{:S(2)}) copy-start(bf16[2,4,256,256]{3,2,1,0:T(8,128)(2,1)} %constant.24.clone.table_ref) | copy-start | bytes 3145732
  59.1 19.8 %copy-start = (f32[3,4,2,64,128]{4,3,2,1,0:T(8,128)S(1)}, f32[3,4,2,64,128]{4,3,2,1,0:T(8,128)}, u32[]{:S(2)}) copy-start(f32[3,4,2,64,128]{4,3,2,1,0:T(8,128)} %vec_ref.5) | copy-start | bytes 2359300
  60.0 19.0 %copy-start.6 = (bf16[2,64,192]{2,1,0:T(8,128)(2,1)S(1)}, bf16[2,64,192]{2,1,0:T(8,128)(2,1)}, u32[]{:S(2)}) copy-start(bf16[2,64,192]{2,1,0:T(8,128)(2,1)} %constant.25.clone.table_ref) | copy-start | bytes 147460

commit v9 on v8

--- a/solution.py
+++ b/solution.py
@@ -119,7 +119,9 @@
 
 def times_table(x, high_table, low_table):
     high, low = halves(x)
-    return dot(high, high_table) + (dot(low, high_table) + dot(high, low_table))
+    both = dot(jnp.concatenate([high, low], axis=0), high_table)
+    rows = x.shape[0]
+    return both[:rows] + (both[rows:] + dot(high, low_table))
 
 
 SINE, SINE_SLOPE, LIFT, SINE_BACK, LIFT_BACK = range(5)

time: 103 us -> 103 us (level)
  no operation moved by 1% of the time
where the time goes in v9:
time: 103 us; the launch traced here: 102 us
  blocking collectives  82 us (80%)
  starting transfers between devices  12.7 us (12%)
  Pallas kernels  5.76 us (6%)
    all_to_all x1, blocking collectives, shards(): lax.all_to_all(modes.reshape(NZ, LINES, LANES), plane, 0, 0, tiled=True)  21.4 us
    all_to_all x1, blocking collectives, shards(): ends = lax.all_to_all(ends, 'wall_0', 0, 0, tiled=True)  19.4 us
    all_to_all x1, blocking collectives, shards(): lax.all_to_all(lines.reshape(NZ, LINES, LANES), plane, 0, 0, tiled=True)  19 us
    all_to_all x1, blocking collectives, shards(): sums = lax.all_to_all(sums, ('wall_1', 'xs_0'), 0, 0, tiled=True)  12.5 us
    all_to_all x1, blocking collectives, shards(): lax.all_to_all(sums, ('wall_0', 'xs_1'), 0, 0, tiled=True).sum(axis=0)  9.76 us
    ppermute x1, starting transfers between devices, shards(): right = lax.ppermute(low_x, XS, [((i + 1) % size, i) for i in range(size)])  4.28 us
    ppermute x1, starting transfers between devices, shards(): lax.ppermute(first, WALL + XS, sum([(down, up)[s % 2][s] for s in range(s...  4.03 us
    ppermute x1, starting transfers between devices, shards(): left = lax.ppermute(high_x, XS, [(i, (i + 1) % size) for i in range(size)])  3.13 us
  transfers between devices with their start and end apart: 4, of which 2 were waited for; matrix products, arithmetic and copies ran while one was open for 0% of the time, Pallas kernels for 2%

profile of v9, /device:TPU:1, one launch (start us, length us, event | category | flops | bytes accessed | tf_op | source)
XLA Modules:
  0.0 102.3 jit_solution(261289275793009483)
XLA Ops:
  0.6 0.0 copy-start.3
  0.6 0.0 copy-start.4
  0.7 0.0 copy-start.8
  0.7 0.0 copy-start.5
  0.7 1.2 %copy.15 = (f32[8,64,128]{2,1,0:T(8,128)S(1)}, f32[8,64,128]{2,1,0:T(8,128)S(1)}) custom-call(f32[3,4,2,64,128]{4,3,2,1,0:T(8,128)} %vec_ref.5, f32[4,2,64,128]{3,2,1,0:T(8,128)} %base_ref.1), custom_call_target="tpu_custom_call" | custom-call | tf_op jit(solution)/shard_map/copy/pallas_call | solution.py:599
  1.9 0.0 copy-start.9
  1.9 4.0 %collective-permute-start.2 = (f32[8,64,128]{2,1,0:T(8,128)S(1)}, f32[8,64,128]{2,1,0:T(8,128)S(1)}, u32[]{:S(2)}, u32[]{:S(2)}) collective-permute-start(f32[8,64,128]{2,1,0:T(8,128)S(1)} %get-tuple-element.18.first_ref), channel_id=1, source_target_pairs={{8,0},{16,8},{24,16},{32,24},{40,32},{48,40},{56,48},{64,56},{72,6... | collective-permute-start | bytes 786440 | tf_op jit(solution)/shard_map/ppermute | solution.py:611
  5.9 1.3 %collective-permute-start.3 = (f32[8,64,128]{2,1,0:T(8,128)S(1)}, f32[8,64,128]{2,1,0:T(8,128)S(1)}, u32[]{:S(2)}, u32[]{:S(2)}) collective-permute-start(f32[8,64,128]{2,1,0:T(8,128)S(1)} %get-tuple-element.19.second_ref), channel_id=1, source_target_pairs={{0,8},{8,16},{16,24},{24,32},{32,40},{40,48},{48,56},{56,64},{64,7... | collective-permute-start | bytes 786440 | tf_op jit(solution)/shard_map/ppermute | solution.py:612
  7.2 0.0 copy-done.3
  7.2 0.0 copy-done.4
  7.2 0.0 copy-done.8
  7.2 0.0 copy-done.5
  7.3 0.0 copy-done.9
  7.3 0.9 edges.1
  8.2 3.1 %collective-permute-start = (f32[64,128]{1,0:T(8,128)S(1)}, f32[64,128]{1,0:T(8,128)S(1)}, u32[]{:S(2)}, u32[]{:S(2)}) collective-permute-start(f32[64,128]{1,0:T(8,128)S(1)} %get-tuple-element.20), channel_id=1, source_target_pairs={{0,1},{1,2},{2,3},{3,4},{4,5},{5,6},{6,7},{7,0},{8,9},{9,10},{10,1... | collective-permute-start | bytes 98312 | tf_op jit(solution)/shard_map/ppermute | solution.py:627
  11.3 0.0 copy-start.7
  11.3 4.3 %collective-permute-start.1 = (f32[64,128]{1,0:T(8,128)S(1)}, f32[64,128]{1,0:T(8,128)S(1)}, u32[]{:S(2)}, u32[]{:S(2)}) collective-permute-start(f32[64,128]{1,0:T(8,128)S(1)} %get-tuple-element.21), channel_id=1, source_target_pairs={{1,0},{2,1},{3,2},{4,3},{5,4},{6,5},{7,6},{0,7},{9,8},{10,9},{11,1... | collective-permute-start | bytes 98312 | tf_op jit(solution)/shard_map/ppermute | solution.py:626
  15.6 0.7 collective-permute-done.left_ref
  16.3 0.2 collective-permute-done.1.right_ref
  16.5 0.7 advect.1.part_ref
  17.1 0.0 copy-start.2
  17.1 0.0 collective-permute-done.2.inner_ref
  17.2 0.0 collective-permute-done.3.outer_ref
  17.2 0.0 copy-done.7
  17.2 0.2 update.1
  17.4 21.4 %all_to_all.32 = f32[64,8,128]{2,1,0:T(8,128)S(1)} all-to-all(f32[64,8,128]{2,1,0:T(8,128)S(1)} %bitcast.9), channel_id=1, replica_groups=mesh['wall_0'=8,'wall_1'=8,'xs_0'=4,'xs_1'=2] {'wall_1','xs_0','xs_1'}, dimensions={0} | all-to-all | bytes 524288 | tf_op jit(solution)/shard_map/all_to_all | solution.py:646
  38.9 0.0 copy-done.2
  38.9 0.0 copy-start.1
  38.9 0.7 stream.1
  39.6 19.4 %all_to_all.33.in_ref = f32[8,6,8,128]{3,2,1,0:T(8,128)S(1)} all-to-all(f32[8,6,8,128]{3,2,1,0:T(8,128)S(1)} %get-tuple-element.27), channel_id=1, replica_groups=mesh['wall_0'=8,'wall_1'=8,'xs_0'=4,'xs_1'=2] {'wall_0'}, dimensions={0} | all-to-all | bytes 393216 | tf_op jit(solution)/shard_map/all_to_all | solution.py:661
  59.0 0.0 copy-done.1
  59.0 0.0 copy-start
  59.0 0.8 stream_back.1
  59.8 0.0 copy-start.6
  59.8 19.0 %all_to_all.34 = f32[64,8,128]{2,1,0:T(8,128)S(1)} all-to-all(f32[64,8,128]{2,1,0:T(8,128)S(1)} %bitcast.8), channel_id=1, replica_groups=mesh['wall_0'=8,'wall_1'=8,'xs_0'=4,'xs_1'=2] {'wall_1','xs_0','xs_1'}, dimensions={0} | all-to-all | bytes 524288 | tf_op jit(solution)/shard_map/all_to_all | solution.py:674
  78.8 0.0 copy-done
  78.8 0.0 copy-done.6
  78.8 0.3 cells.1
  79.1 9.8 %all_to_all.35 = f32[16,1,128]{2,1,0:T(1,128)S(1)} all-to-all(f32[16,1,128]{2,1,0:T(1,128)S(1)} %bitcast.13), channel_id=1, replica_groups=mesh['wall_0'=8,'wall_1'=8,'xs_0'=4,'xs_1'=2] {'wall_0','xs_1'}, dimensions={0} | all-to-all | bytes 16384 | tf_op jit(solution)/shard_map/all_to_all | solution.py:683
  89.0 12.5 %all_to_all.36 = f32[32,1,128]{2,1,0:T(1,128)S(1)} all-to-all(f32[32,1,128]{2,1,0:T(1,128)S(1)} %broadcast_in_dim.3), channel_id=1, replica_groups=mesh['wall_0'=8,'wall_1'=8,'xs_0'=4,'xs_1'=2] {'wall_1','xs_0'}, dimensions={0} | all-to-all | bytes 32768 | tf_op jit(solution)/shard_map/all_to_all | solution.py:685
  101.4 0.9 residual.1
  (2 shorter events, 0.0 us)
Async XLA Ops:
  0.6 6.6 %copy-start.3 = (f32[3,16,128]{2,1,0:T(8,128)S(1)}, f32[3,16,128]{2,1,0:T(8,128)}, u32[]{:S(2)}) copy-start(f32[3,16,128]{2,1,0:T(8,128)} %constant.18.clone.marks_ref) | copy-start | bytes 73732
  0.6 6.6 %copy-start.4 = (bf16[5,16,48]{2,1,0:T(8,128)(2,1)S(1)}, bf16[5,16,48]{2,1,0:T(8,128)(2,1)}, u32[]{:S(2)}) copy-start(bf16[5,16,48]{2,1,0:T(8,128)(2,1)} %constant.21.clone.wall_ref) | copy-start | bytes 23044
  0.7 6.6 %copy-start.8 = (f32[64,2,128]{2,1,0:T(2,128)S(1)}, f32[64,2,128]{2,1,0:T(2,128)}, u32[]{:S(2)}) copy-start(f32[64,2,128]{2,1,0:T(2,128)} %constant.20.clone.span_ref) | copy-start | bytes 196612
  0.7 6.6 %copy-start.5 = (f32[2,8,128]{2,1,0:T(8,128)S(1)}, f32[2,8,128]{2,1,0:T(8,128)}, u32[]{:S(2)}) copy-start(f32[2,8,128]{2,1,0:T(8,128)} %constant.19.clone.stream_ref) | copy-start | bytes 24580
  1.9 5.4 %copy-start.9 = (f32[4]{0:T(128)S(1)}, f32[4]{0:T(128)}, u32[]{:S(2)}) copy-start(f32[4]{0:T(128)} %diff_ref.1) | copy-start | bytes 52
  1.9 15.3 %collective-permute-start.2 = (f32[8,64,128]{2,1,0:T(8,128)S(1)}, f32[8,64,128]{2,1,0:T(8,128)S(1)}, u32[]{:S(2)}, u32[]{:S(2)}) collective-permute-start(f32[8,64,128]{2,1,0:T(8,128)S(1)} %get-tuple-element.18.first_ref), channel_id=1, source_target_pairs={{8,0},{16,8},{24,16},{32,24},{40,32},{48,40},{56,48},{64,56},{72,6... | collective-permute-start | bytes 786440 | tf_op jit(solution)/shard_map/ppermute | solution.py:611
  5.9 11.2 %collective-permute-start.3 = (f32[8,64,128]{2,1,0:T(8,128)S(1)}, f32[8,64,128]{2,1,0:T(8,128)S(1)}, u32[]{:S(2)}, u32[]{:S(2)}) collective-permute-start(f32[8,64,128]{2,1,0:T(8,128)S(1)} %get-tuple-element.19.second_ref), channel_id=1, source_target_pairs={{0,8},{8,16},{16,24},{24,32},{32,40},{40,48},{48,56},{56,64},{64,7... | collective-permute-start | bytes 786440 | tf_op jit(solution)/shard_map/ppermute | solution.py:612
  8.2 8.1 %collective-permute-start = (f32[64,128]{1,0:T(8,128)S(1)}, f32[64,128]{1,0:T(8,128)S(1)}, u32[]{:S(2)}, u32[]{:S(2)}) collective-permute-start(f32[64,128]{1,0:T(8,128)S(1)} %get-tuple-element.20), channel_id=1, source_target_pairs={{0,1},{1,2},{2,3},{3,4},{4,5},{5,6},{6,7},{7,0},{8,9},{9,10},{10,1... | collective-permute-start | bytes 98312 | tf_op jit(solution)/shard_map/ppermute | solution.py:627
  11.3 5.9 %copy-start.7 = (bf16[2,64,192]{2,1,0:T(8,128)(2,1)S(1)}, bf16[2,64,192]{2,1,0:T(8,128)(2,1)}, u32[]{:S(2)}) copy-start(bf16[2,64,192]{2,1,0:T(8,128)(2,1)} %constant.22.clone.table_ref) | copy-start | bytes 147460
  11.3 5.1 %collective-permute-start.1 = (f32[64,128]{1,0:T(8,128)S(1)}, f32[64,128]{1,0:T(8,128)S(1)}, u32[]{:S(2)}, u32[]{:S(2)}) collective-permute-start(f32[64,128]{1,0:T(8,128)S(1)} %get-tuple-element.21), channel_id=1, source_target_pairs={{1,0},{2,1},{3,2},{4,3},{5,4},{6,5},{7,6},{0,7},{9,8},{10,9},{11,1... | collective-permute-start | bytes 98312 | tf_op jit(solution)/shard_map/ppermute | solution.py:626
  17.1 21.8 %copy-start.2 = (bf16[2,4,256,256]{3,2,1,0:T(8,128)(2,1)S(1)}, bf16[2,4,256,256]{3,2,1,0:T(8,128)(2,1)}, u32[]{:S(2)}) copy-start(bf16[2,4,256,256]{3,2,1,0:T(8,128)(2,1)} %constant.23.clone.table_ref) | copy-start | bytes 3145732
  38.9 20.1 %copy-start.1 = (bf16[2,4,256,256]{3,2,1,0:T(8,128)(2,1)S(1)}, bf16[2,4,256,256]{3,2,1,0:T(8,128)(2,1)}, u32[]{:S(2)}) copy-start(bf16[2,4,256,256]{3,2,1,0:T(8,128)(2,1)} %constant.24.clone.table_ref) | copy-start | bytes 3145732
  59.0 19.8 %copy-start = (f32[3,4,2,64,128]{4,3,2,1,0:T(8,128)S(1)}, f32[3,4,2,64,128]{4,3,2,1,0:T(8,128)}, u32[]{:S(2)}) copy-start(f32[3,4,2,64,128]{4,3,2,1,0:T(8,128)} %vec_ref.5) | copy-start | bytes 2359300
  59.8 19.0 %copy-start.6 = (bf16[2,64,192]{2,1,0:T(8,128)(2,1)S(1)}, bf16[2,64,192]{2,1,0:T(8,128)(2,1)}, u32[]{:S(2)}) copy-start(bf16[2,64,192]{2,1,0:T(8,128)(2,1)} %constant.25.clone.table_ref) | copy-start | bytes 147460
